TPU v7x, 128 devices: a whole 4x4x4 slice. The times are simulated.
128 devices in a mesh: dom: 128 (over x, y, z, core).
Axes of the slice: x: 4, y: 4, z: 4, core: 2. Of those that a mesh axis runs over, the one named last changes fastest.
Arguments:
- traction: float32 [65536, 3, 128], P('dom'), may hold values from -6 to 6
- fluid_coords: float32 [65536, 3, 128], P('dom'), may hold values from 0 to 1
- struct_coords: float32 [3, 32, 16384], P(None, None, 'dom'), may hold values from 0 to 1
- dest: int32 [65536, 1], P('dom'), may hold values from 0 to 127; in each aligned block of 512 rows (0 to 511, 512 to 1023, ...) at most 8 rows name the same one
- target: int32 [65536], P('dom'), may hold values from 0 to 127
- blocks: float32 [3, 96, 96, 16384], P(None, None, None, 'dom'), may hold values from -1 to 7, as said below
- columns: int32 [2, 16384], P(None, 'dom'), may hold values from 0 to 159
- halo_list: int32 [2048], P('dom'), may hold values from 0 to 127
- precond: float32 [96, 96, 16384], P(None, None, 'dom'), may hold values from -1 to 1
Outputs:
- load_field: float32 [96, 16384], P(None, 'dom')
- solution: float32 [96, 16384], P(None, 'dom')
- residual: float32 [96, 16384], P(None, 'dom')
Inputs may be any that keep to these rules, and one draw needn't show every extreme that they name: `dest`: among the fluid blocks of one partition no partition is named more than 8 times, a bound that some block reaches. Each diagonal block is its positive diagonal plus small full entries; coupling blocks are small full blocks.
All inputs are finite; a program needn't handle non-finite values.
Results may differ from a plain program's by a relative error of at most 0.0003.
Values sent between devices are 32-bit elements; how exact they have to be, the bound alone decides.
No kernel may reach another device: no remote copies, remote signals or barrier semaphores. Data moves between devices by JAX's collectives and lax.ppermute only.
A program may use at most 128 MiB of HBM per device.

v0:
```python
import jax
import jax.numpy as jnp
from jax import lax
from jax.sharding import Mesh
from jax.sharding import PartitionSpec as P

ITERS = 2
DOM = ("dom_0", "dom_1", "dom_2", "dom_3")


support = 0.9


def from_behind(block, axis, distance):
    devices = range(lax.axis_size(axis))
    route = [(i - distance, i) for i in devices if i - distance in devices]
    return lax.ppermute(block, axis, route)


def over_axes(shard, axes):
    for axis in axes:
        shard = lax.psum(shard, axis)
    return shard


def wendland_map(fluid_pos, force, struct_pos):
    dist_sq = jnp.zeros((fluid_pos.shape[0], struct_pos.shape[2], fluid_pos.shape[2]), jnp.float32)
    for component in range(3):
        dist_sq = (
            dist_sq + (struct_pos[:, component, :, None] - fluid_pos[:, component, None, :]) ** 2
        )
    radius = jnp.sqrt(dist_sq) / support
    weight = jnp.maximum(1.0 - radius, 0.0) ** 4 * (4.0 * radius + 1.0)
    mapped = jnp.einsum("bjn,bcn->bcj", weight, force, precision=lax.Precision.HIGHEST)
    return mapped.reshape(mapped.shape[0], -1)


def precondition(precond, vector):
    return jnp.einsum("abi,bi->ai", precond, vector, precision=lax.Precision.HIGHEST)


def apply_operator(vector, blocks, columns, halo_list):
    outgoing = jnp.take(vector, halo_list, axis=1)
    from_left = from_behind(outgoing, DOM, 1)
    from_right = from_behind(outgoing, DOM, -1)
    extended = jnp.concatenate([vector, from_left, from_right], axis=1)
    result = jnp.einsum("abi,bi->ai", blocks[0], vector, precision=lax.Precision.HIGHEST)
    for neighbor in range(columns.shape[0]):
        taken = jnp.take(extended, columns[neighbor], axis=1)
        result = result + jnp.einsum(
            "abi,bi->ai", blocks[neighbor + 1], taken, precision=lax.Precision.HIGHEST
        )
    return result


def on_device(
    traction, fluid_coords, struct_coords, dest, target, blocks, columns, halo_list, precond
):
    partitions = lax.axis_size(DOM)
    fluid_count = dest.shape[0]
    node_count = traction.shape[2]
    cluster = blocks.shape[1]
    local_blocks = blocks.shape[3]
    capacity = max(2, 2 * fluid_count // partitions)
    owner_part = dest[:, 0]
    owner_hits = (owner_part[:, None] == jnp.arange(partitions, dtype=jnp.int32)[None, :]).astype(
        jnp.int32
    )
    before = jnp.sum((jnp.cumsum(owner_hits, axis=0) - owner_hits) * owner_hits, axis=1)
    slot_index = owner_part * capacity + before
    slot_target = jnp.zeros((partitions * capacity,), jnp.int32).at[slot_index].set(target)
    slot_target = slot_target.reshape(partitions, capacity)
    packed = jnp.concatenate([traction, fluid_coords], axis=1)
    outgoing = (
        jnp.zeros((partitions * capacity, 6, node_count), jnp.float32).at[slot_index].set(packed)
    )
    outgoing = outgoing.reshape(partitions, capacity, 6, node_count)
    floats = lax.all_to_all(outgoing, DOM, split_axis=0, concat_axis=0, tiled=True)
    labels = lax.all_to_all(slot_target, DOM, split_axis=0, concat_axis=0, tiled=True)
    item_count = floats.shape[1]
    flattened = floats.reshape(partitions * item_count, 6, node_count)
    struct_pos = jnp.transpose(jnp.take(struct_coords, labels.reshape(-1), axis=2), (2, 0, 1))
    mapped = wendland_map(flattened[:, 3:], flattened[:, :3], struct_pos)
    arrived, labels = (mapped.reshape(partitions, item_count, cluster), labels)
    onehot = (
        labels.reshape(-1)[:, None] == jnp.arange(local_blocks, dtype=jnp.int32)[None, :]
    ).astype(jnp.float32)
    load_field = jnp.dot(
        arrived.reshape(-1, cluster).T,
        onehot,
        precision=lax.Precision.HIGHEST,
        preferred_element_type=jnp.float32,
    )
    solution = jnp.zeros_like(load_field)
    residual = load_field
    search = load_field
    alignment = over_axes(jnp.sum(load_field * residual), DOM)
    for step in range(ITERS):
        search_pre = precondition(precond, search)
        image = apply_operator(search_pre, blocks, columns, halo_list)
        step_size = alignment / over_axes(jnp.sum(load_field * image), DOM)
        middle = residual - step_size * image
        middle_pre = precondition(precond, middle)
        middle_image = apply_operator(middle_pre, blocks, columns, halo_list)
        crossed, squared, with_middle, with_image = (
            over_axes(jnp.sum(middle_image * middle), DOM),
            over_axes(jnp.sum(middle_image * middle_image), DOM),
            over_axes(jnp.sum(load_field * middle), DOM),
            over_axes(jnp.sum(load_field * middle_image), DOM),
        )
        smoothing = crossed / squared
        solution = solution + step_size * search_pre + smoothing * middle_pre
        residual = middle - smoothing * middle_image
        new_alignment = with_middle - smoothing * with_image
        momentum = new_alignment / alignment * (step_size / smoothing)
        search = residual + momentum * (search - smoothing * image)
        alignment = new_alignment
    return (load_field, solution, residual)


def solution(mesh):
    finer = Mesh(mesh.devices.reshape(4, 4, 4, 2), ("dom_0", "dom_1", "dom_2", "dom_3"))
    in_specs = (
        P(DOM, None, None),
        P(DOM, None, None),
        P(None, None, DOM),
        P(DOM, None),
        P(DOM),
        P(None, None, None, DOM),
        P(None, DOM),
        P(DOM),
        P(None, None, DOM),
    )
    out_specs = (P(None, DOM), P(None, DOM), P(None, DOM))
    return jax.shard_map(
        on_device, mesh=finer, in_specs=in_specs, out_specs=out_specs, check_vma=False
    )
```

profile of v0, /device:TPU:1, one launch (start us, length us, event | category | flops | bytes accessed | tf_op | source)
XLA Modules:
  0.0 407.9 jit_solution(7936706679427344915)
XLA Ops:
  0.6 0.8 copy.101
  1.7 0.9 fusion.43
  2.6 0.7 compare_select_fusion.1
  3.3 2.6 scatter_custom_fusion.1
  5.9 0.7 all_to_all.10
  6.7 11.5 %all-to-all-start.1 = ((s32[128,1,8]{2,1,0:T(1,128)}), s32[128,1,8]{2,1,0:T(1,128)S(1)}, u32[]{:S(2)}, u32[]{:S(2)}) async-start(s32[128,1,8]{2,1,0:T(1,128)} %bitcast.41), calls=%async_computation.1 | async-start | bytes 131072 | tf_op jit(solution)/shard_map/all_to_all | solution.py:79
  18.1 1.5 pad_maximum_fusion
  19.6 0.9 copy.103
  20.6 2.2 broadcast_in_dim.40
  22.8 47.3 %scatter_fusion = f32[1024,6,128]{2,1,0:T(8,128)} fusion(f32[1024,6,128]{2,1,0:T(8,128)} %broadcast_in_dim.40, s32[512]{0:T(512)S(1)} %bitcast.249, f32[512,6,128]{2,1,0:T(8,128)S(1)} %copy.103), kind=kCustom, calls=%fused_computation.13 | custom fusion | bytes 4720640 | tf_op jit(solution)/shard_map/scatter | solution.py:75
  70.1 4.6 %copy.104 = f32[128,8,6,128]{3,1,2,0:T(8,128)} copy(f32[128,8,6,128]{3,2,1,0:T(8,128)} %bitcast.221) | data formatting | bytes 6291456 | tf_op jit(solution)/shard_map/reshape | solution.py:77
  74.8 9.9 %all-to-all-start = ((f32[128,8,6,128]{3,1,2,0:T(8,128)}), f32[128,8,6,128]{3,1,2,0:T(8,128)S(1)}, u32[]{:S(2)}, u32[]{:S(2)}) async-start(f32[128,8,6,128]{3,1,2,0:T(8,128)} %copy.104), calls=%async_computation | async-start | bytes 6291456 | tf_op jit(solution)/shard_map/all_to_all | solution.py:78
  85.5 1.4 reduce.37
  86.9 0.9 reshape.92
  87.9 7.9 %gather_fusion = f32[1024,3,32]{2,1,0:T(4,128)} fusion(f32[3,32,128]{1,0,2:T(4,128)S(1)} %copy.107, s32[1024]{0:T(1024)S(1)} %broadcast_clamp_fusion), kind=kCustom, calls=%fused_computation.12 | custom fusion | bytes 790528 | tf_op jit(solution)/shard_map/jit(_take)/gather | solution.py:82
  95.8 5.5 %broadcast_select_fusion = f32[1024,3,32]{2,1,0:T(4,128)S(1)} fusion(f32[1024,3,32]{2,1,0:T(4,128)} %gather_fusion, pred[1024]{0:T(1024)(128)(4,1)S(1)} %compare_and_fusion), kind=kLoop, calls=%fused_computation.73 | loop fusion | flops 98304 | bytes 787456 | tf_op jit(solution)/shard_map/jit(_take)/select_n | solution.py:82
  101.3 2.3 fusion.71
  103.6 22.7 %all-to-all-done = f32[128,8,6,128]{3,1,2,0:T(8,128)S(1)} async-done(((f32[128,8,6,128]{3,1,2,0:T(8,128)}), f32[128,8,6,128]{3,1,2,0:T(8,128)S(1)}, u32[]{:S(2)}, u32[]{:S(2)}) %all-to-all-start) | async-done | bytes 3145760 | tf_op jit(solution)/shard_map/all_to_all | solution.py:78
  126.4 0.9 copy.105
  127.3 1.3 fusion.70
  128.6 42.6 %fusion = f32[1024,3,32]{2,1,0:T(4,128)S(1)} fusion(f32[1024,128]{1,0:T(8,128)S(1)} %bitcast.242, f32[1024,32]{1,0:T(8,128)S(1)} %bitcast.240, f32[1024,128]{1,0:T(8,128)S(1)} %bitcast.243, f32[1024,32]{1,0:T(8,128)S(1)} %bitcast.239, f32[1024,128]{1,0:T(8,128)S(1)} %bitcast.241, f32[1024,32]{1,0:T(8,128)S(1)} %bitcast.238, f32[1024,6,128]{2,1,0:T(8,128)S(1)} %bitcast.223), kind=kOutput, calls=%fused_computation.15 | convolution fusion | flops 218103808 | bytes 5636096 | tf_op jit(solution)/shard_map/bjn,bcn->bcj/dot_general | solution.py:34
  172.3 3.1 multiply_reduce_fusion.3
  176.2 3.1 collective-permute-start.1
  179.3 2.5 collective-permute-start
  181.9 0.7 collective-permute-done
  182.8 0.7 gather_fusion.2
  183.6 0.7 gather_fusion.3
  184.5 6.2 %fusion.32 = (f32[128,96]{0,1:T(8,128)S(1)}, f32[128,96]{0,1:T(8,128)S(1)}, f32[128,96]{0,1:T(8,128)S(1)}) fusion(f32[3,96,96,128]{3,2,1,0:T(8,128)} %param.18, f32[128,96]{0,1:T(8,128)S(1)} %copy.236, f32[128,96]{0,1:T(8,128)S(1)} %multiply_reduce_fusion.3, f32[128,96]{0,1:T(8,128)S(1)} %copy.237), kind=kLoop, calls=%fused_computation.55 | loop fusion | flops 7041024 | bytes 14450688 | tf_op jit(solution)/shard_map/abi,bi->ai/dot_general | solution.py:50
  191.3 8.0 %all-reduce.8 = (f32[]{:T(128)}, f32[]{:T(128)}) all-reduce(f32[]{:T(128)} %get-tuple-element.24, f32[]{:T(128)} %get-tuple-element.23), channel_id=1, replica_groups=mesh['dom_0'=4,'dom_1'=4,'dom_2'=4,'dom_3'=2] {'dom_0'}, use_global_device_ids=true, to_apply=%region_6.7 | all-reduce | flops 2 | bytes 16 | tf_op jit(solution)/shard_map/psum | solution.py:22
  199.3 6.7 %all-reduce.5 = (f32[]{:T(128)}, f32[]{:T(128)}) all-reduce(f32[]{:T(128)} %get-tuple-element.47, f32[]{:T(128)} %get-tuple-element.48), channel_id=1, replica_groups=mesh['dom_0'=4,'dom_1'=4,'dom_2'=4,'dom_3'=2] {'dom_1'}, use_global_device_ids=true, to_apply=%region_7.8 | all-reduce | flops 2 | bytes 16 | tf_op jit(solution)/shard_map/psum | solution.py:22
  206.1 11.0 %all-reduce.2 = (f32[]{:T(128)}, f32[]{:T(128)}) all-reduce(f32[]{:T(128)} %get-tuple-element.39, f32[]{:T(128)} %get-tuple-element.40), channel_id=1, replica_groups=mesh['dom_0'=4,'dom_1'=4,'dom_2'=4,'dom_3'=2] {'dom_2'}, use_global_device_ids=true, to_apply=%region_8.9 | all-reduce | flops 2 | bytes 16 | tf_op jit(solution)/shard_map/psum | solution.py:22
  217.0 10.4 %all-reduce.11 = (f32[]{:T(128)}, f32[]{:T(128)}) all-reduce(f32[]{:T(128)} %get-tuple-element.31, f32[]{:T(128)} %get-tuple-element.32), channel_id=1, replica_groups=mesh['dom_0'=4,'dom_1'=4,'dom_2'=4,'dom_3'=2] {'dom_3'}, use_global_device_ids=true, to_apply=%region_9.10 | all-reduce | flops 2 | bytes 16 | tf_op jit(solution)/shard_map/psum | solution.py:22
  228.8 3.1 multiply_reduce_fusion.2
  232.6 2.2 collective-permute-start.3
  234.9 3.8 collective-permute-start.2
  239.5 0.7 gather_fusion.5
  240.1 0.6 gather_fusion.6
  241.1 6.2 %fusion.33 = (f32[128,96]{0,1:T(8,128)S(1)}, f32[128,96]{0,1:T(8,128)S(1)}, f32[128,96]{0,1:T(8,128)S(1)}) fusion(f32[3,96,96,128]{3,2,1,0:T(8,128)} %param.18, f32[128,96]{0,1:T(8,128)S(1)} %copy.241, f32[128,96]{0,1:T(8,128)S(1)} %multiply_reduce_fusion.2, f32[128,96]{0,1:T(8,128)S(1)} %copy.242), kind=kLoop, calls=%fused_computation.56 | loop fusion | flops 7041024 | bytes 14450688 | tf_op jit(solution)/shard_map/abi,bi->ai/dot_general | solution.py:50
  247.4 0.7 fusion.55
  248.1 9.3 %all-reduce.7 = (f32[]{:T(128)}, f32[]{:T(128)}, f32[]{:T(128)}, f32[]{:T(128)}) all-reduce(f32[]{:T(128)} %get-tuple-element.19, f32[]{:T(128)} %get-tuple-element.18, f32[]{:T(128)} %get-tuple-element.22, f32[]{:T(128)} %get-tuple-element.17), channel_id=1, replica_groups=mesh['dom_0'=4,'dom_1'=4,'dom_2'=4,'dom_3'=2] {'dom_0'}, use_global_device_ids=true, to_apply=%region_26.29 | all-reduce | flops 4 | bytes 32 | tf_op jit(solution)/shard_map/psum | solution.py:22
  257.4 6.7 %all-reduce.4 = (f32[]{:T(128)}, f32[]{:T(128)}, f32[]{:T(128)}, f32[]{:T(128)}) all-reduce(f32[]{:T(128)} %get-tuple-element.43, f32[]{:T(128)} %get-tuple-element.44, f32[]{:T(128)} %get-tuple-element.45, f32[]{:T(128)} %get-tuple-element.46), channel_id=1, replica_groups=mesh['dom_0'=4,'dom_1'=4,'dom_2'=4,'dom_3'=2] {'dom_1'}, use_global_device_ids=true, to_apply=%region_27.30 | all-reduce | flops 4 | bytes 32 | tf_op jit(solution)/shard_map/psum | solution.py:22
  264.1 11.5 %all-reduce.1 = (f32[]{:T(128)}, f32[]{:T(128)}, f32[]{:T(128)}, f32[]{:T(128)}) all-reduce(f32[]{:T(128)} %get-tuple-element.35, f32[]{:T(128)} %get-tuple-element.36, f32[]{:T(128)} %get-tuple-element.37, f32[]{:T(128)} %get-tuple-element.38), channel_id=1, replica_groups=mesh['dom_0'=4,'dom_1'=4,'dom_2'=4,'dom_3'=2] {'dom_2'}, use_global_device_ids=true, to_apply=%region_28.31 | all-reduce | flops 4 | bytes 32 | tf_op jit(solution)/shard_map/psum | solution.py:22
  275.6 10.1 %all-reduce.10 = (f32[]{:T(128)}, f32[]{:T(128)}, f32[]{:T(128)}, f32[]{:T(128)}) all-reduce(f32[]{:T(128)} %get-tuple-element.27, f32[]{:T(128)} %get-tuple-element.28, f32[]{:T(128)} %get-tuple-element.29, f32[]{:T(128)} %get-tuple-element.30), channel_id=1, replica_groups=mesh['dom_0'=4,'dom_1'=4,'dom_2'=4,'dom_3'=2] {'dom_3'}, use_global_device_ids=true, to_apply=%region_29.32 | all-reduce | flops 4 | bytes 32 | tf_op jit(solution)/shard_map/psum | solution.py:22
  291.5 3.1 multiply_reduce_fusion.1
  295.4 2.2 collective-permute-start.5
  297.6 3.5 collective-permute-start.4
  301.2 0.7 collective-permute-done.4
  302.2 0.7 gather_fusion.8
  303.8 6.2 %fusion.34 = (f32[128,96]{0,1:T(8,128)S(1)}, f32[128,96]{0,1:T(8,128)S(1)}, f32[128,96]{0,1:T(8,128)S(1)}) fusion(f32[3,96,96,128]{3,2,1,0:T(8,128)} %param.18, f32[128,96]{0,1:T(8,128)S(1)} %copy.246, f32[128,96]{0,1:T(8,128)S(1)} %multiply_reduce_fusion.1, f32[128,96]{0,1:T(8,128)S(1)} %copy.247), kind=kLoop, calls=%fused_computation.57 | loop fusion | flops 7041024 | bytes 14450688 | tf_op jit(solution)/shard_map/abi,bi->ai/dot_general | solution.py:50
  310.7 9.3 %psum.276 = f32[]{:T(128)} all-reduce(f32[]{:T(128)} %fusion.51), channel_id=1, replica_groups=mesh['dom_0'=4,'dom_1'=4,'dom_2'=4,'dom_3'=2] {'dom_0'}, use_global_device_ids=true, to_apply=%region_36.39 | all-reduce | flops 1 | bytes 8 | tf_op jit(solution)/shard_map/psum | solution.py:22
  320.0 6.6 %psum.277 = f32[]{:T(128)} all-reduce(f32[]{:T(128)} %psum.276), channel_id=1, replica_groups=mesh['dom_0'=4,'dom_1'=4,'dom_2'=4,'dom_3'=2] {'dom_1'}, use_global_device_ids=true, to_apply=%region_37.40 | all-reduce | flops 1 | bytes 8 | tf_op jit(solution)/shard_map/psum | solution.py:22
  326.6 11.4 %psum.278 = f32[]{:T(128)} all-reduce(f32[]{:T(128)} %psum.277), channel_id=1, replica_groups=mesh['dom_0'=4,'dom_1'=4,'dom_2'=4,'dom_3'=2] {'dom_2'}, use_global_device_ids=true, to_apply=%region_38.41 | all-reduce | flops 1 | bytes 8 | tf_op jit(solution)/shard_map/psum | solution.py:22
  338.0 10.0 %psum.279 = f32[]{:T(128)} all-reduce(f32[]{:T(128)} %psum.278), channel_id=1, replica_groups=mesh['dom_0'=4,'dom_1'=4,'dom_2'=4,'dom_3'=2] {'dom_3'}, use_global_device_ids=true, to_apply=%region_39.42 | all-reduce | flops 1 | bytes 8 | tf_op jit(solution)/shard_map/psum | solution.py:22
  348.8 3.1 multiply_reduce_fusion
  352.6 2.2 collective-permute-start.7
  354.9 3.5 collective-permute-start.6
  358.5 0.7 collective-permute-done.6
  359.5 0.7 gather_fusion.12
  360.1 0.6 gather_fusion.11
  361.0 6.2 %fusion.35 = (f32[128,96]{0,1:T(8,128)S(1)}, f32[128,96]{0,1:T(8,128)S(1)}, f32[128,96]{0,1:T(8,128)S(1)}) fusion(f32[3,96,96,128]{3,2,1,0:T(8,128)} %param.18, f32[128,96]{0,1:T(8,128)S(1)} %copy.251, f32[128,96]{0,1:T(8,128)S(1)} %multiply_reduce_fusion, f32[128,96]{0,1:T(8,128)S(1)} %copy.252), kind=kLoop, calls=%fused_computation.58 | loop fusion | flops 7041024 | bytes 14450688 | tf_op jit(solution)/shard_map/abi,bi->ai/dot_general | solution.py:50
  367.9 9.3 %all-reduce.6 = (f32[]{:T(128)}, f32[]{:T(128)}) all-reduce(f32[]{:T(128)} %get-tuple-element.21, f32[]{:T(128)} %get-tuple-element.20), channel_id=1, replica_groups=mesh['dom_0'=4,'dom_1'=4,'dom_2'=4,'dom_3'=2] {'dom_0'}, use_global_device_ids=true, to_apply=%region_41.44 | all-reduce | flops 2 | bytes 16 | tf_op jit(solution)/shard_map/psum | solution.py:22
  377.2 6.6 %all-reduce.3 = (f32[]{:T(128)}, f32[]{:T(128)}) all-reduce(f32[]{:T(128)} %get-tuple-element.41, f32[]{:T(128)} %get-tuple-element.42), channel_id=1, replica_groups=mesh['dom_0'=4,'dom_1'=4,'dom_2'=4,'dom_3'=2] {'dom_1'}, use_global_device_ids=true, to_apply=%region_42.45 | all-reduce | flops 2 | bytes 16 | tf_op jit(solution)/shard_map/psum | solution.py:22
  383.8 11.4 %all-reduce = (f32[]{:T(128)}, f32[]{:T(128)}) all-reduce(f32[]{:T(128)} %get-tuple-element.33, f32[]{:T(128)} %get-tuple-element.34), channel_id=1, replica_groups=mesh['dom_0'=4,'dom_1'=4,'dom_2'=4,'dom_3'=2] {'dom_2'}, use_global_device_ids=true, to_apply=%region_43.46 | all-reduce | flops 2 | bytes 16 | tf_op jit(solution)/shard_map/psum | solution.py:22
  395.2 10.0 %all-reduce.9 = (f32[]{:T(128)}, f32[]{:T(128)}) all-reduce(f32[]{:T(128)} %get-tuple-element.25, f32[]{:T(128)} %get-tuple-element.26), channel_id=1, replica_groups=mesh['dom_0'=4,'dom_1'=4,'dom_2'=4,'dom_3'=2] {'dom_3'}, use_global_device_ids=true, to_apply=%region_44.47 | all-reduce | flops 2 | bytes 16 | tf_op jit(solution)/shard_map/psum | solution.py:22
  (93 shorter events, 12.1 us)
Async XLA Ops:
  6.7 68.1 %all-to-all-start.1 = ((s32[128,1,8]{2,1,0:T(1,128)}), s32[128,1,8]{2,1,0:T(1,128)S(1)}, u32[]{:S(2)}, u32[]{:S(2)}) async-start(s32[128,1,8]{2,1,0:T(1,128)} %bitcast.41), calls=%async_computation.1 | async-start | bytes 131072 | tf_op jit(solution)/shard_map/all_to_all | solution.py:79
  74.7 9.9 %copy-start.4 = (f32[3,32,128]{2,1,0:T(8,128)S(1)}, f32[3,32,128]{2,1,0:T(8,128)}, u32[]{:S(2)}) copy-start(f32[3,32,128]{2,1,0:T(8,128)} %param.15) | copy-start | bytes 147460
  74.7 10.1 %copy-start.6 = (s32[16]{0:T(128)S(1)}, s32[16]{0:T(128)}, u32[]{:S(2)}) copy-start(s32[16]{0:T(128)} %param.20) | copy-start | bytes 196
  74.7 10.1 %copy-start.5 = (s32[2,128]{1,0:T(2,128)S(1)}, s32[2,128]{1,0:T(2,128)}, u32[]{:S(2)}) copy-start(s32[2,128]{1,0:T(2,128)} %param.19) | copy-start | bytes 3076
  74.8 51.6 %all-to-all-start = ((f32[128,8,6,128]{3,1,2,0:T(8,128)}), f32[128,8,6,128]{3,1,2,0:T(8,128)S(1)}, u32[]{:S(2)}, u32[]{:S(2)}) async-start(f32[128,8,6,128]{3,1,2,0:T(8,128)} %copy.104), calls=%async_computation | async-start | bytes 6291456 | tf_op jit(solution)/shard_map/all_to_all | solution.py:78
  126.4 2.2 copy-start.1
  126.4 2.2 copy-start.2
  126.4 2.2 copy-start.3
  172.3 176.4 %copy-start = (f32[96,128]{1,0:T(8,128)}, f32[96,128]{1,0:T(8,128)S(1)}, u32[]{:S(2)}) copy-start(f32[96,128]{1,0:T(8,128)S(1)} %fusion.41) | copy-start | bytes 147460
  176.2 5.6 %collective-permute-start.1 = (f32[96,16]{0,1:T(8,128)S(1)}, f32[96,16]{0,1:T(8,128)S(1)}, u32[]{:S(2)}, u32[]{:S(2)}) collective-permute-start(f32[96,16]{0,1:T(8,128)S(1)} %select_bitcast_fusion.3), channel_id=1, source_target_pairs={{1,0},{2,1},{3,2},{4,3},{5,4},{6,5},{7,6},{8,7},{9,8},{10,9},{11,1... | collective-permute-start | bytes 18440 | tf_op jit(solution)/shard_map/ppermute | solution.py:17
  179.3 3.3 collective-permute-start
  232.6 6.0 %collective-permute-start.3 = (f32[96,16]{0,1:T(8,128)S(1)}, f32[96,16]{0,1:T(8,128)S(1)}, u32[]{:S(2)}, u32[]{:S(2)}) collective-permute-start(f32[96,16]{0,1:T(8,128)S(1)} %select_bitcast_fusion.2), channel_id=1, source_target_pairs={{1,0},{2,1},{3,2},{4,3},{5,4},{6,5},{7,6},{8,7},{9,8},{10,9},{11,1... | collective-permute-start | bytes 18440 | tf_op jit(solution)/shard_map/ppermute | solution.py:17
  234.9 4.3 %collective-permute-start.2 = (f32[96,16]{0,1:T(8,128)S(1)}, f32[96,16]{0,1:T(8,128)S(1)}, u32[]{:S(2)}, u32[]{:S(2)}) collective-permute-start(f32[96,16]{0,1:T(8,128)S(1)} %select_bitcast_fusion.2), channel_id=1, source_target_pairs={{0,1},{1,2},{2,3},{3,4},{4,5},{5,6},{6,7},{7,8},{8,9},{9,10},{10,1... | collective-permute-start | bytes 18440 | tf_op jit(solution)/shard_map/ppermute | solution.py:17
  295.4 5.8 %collective-permute-start.5 = (f32[96,16]{0,1:T(8,128)S(1)}, f32[96,16]{0,1:T(8,128)S(1)}, u32[]{:S(2)}, u32[]{:S(2)}) collective-permute-start(f32[96,16]{0,1:T(8,128)S(1)} %select_bitcast_fusion.1), channel_id=1, source_target_pairs={{1,0},{2,1},{3,2},{4,3},{5,4},{6,5},{7,6},{8,7},{9,8},{10,9},{11,1... | collective-permute-start | bytes 18440 | tf_op jit(solution)/shard_map/ppermute | solution.py:17
  297.6 4.3 %collective-permute-start.4 = (f32[96,16]{0,1:T(8,128)S(1)}, f32[96,16]{0,1:T(8,128)S(1)}, u32[]{:S(2)}, u32[]{:S(2)}) collective-permute-start(f32[96,16]{0,1:T(8,128)S(1)} %select_bitcast_fusion.1), channel_id=1, source_target_pairs={{0,1},{1,2},{2,3},{3,4},{4,5},{5,6},{6,7},{7,8},{8,9},{9,10},{10,1... | collective-permute-start | bytes 18440 | tf_op jit(solution)/shard_map/ppermute | solution.py:17
  352.6 5.8 %collective-permute-start.7 = (f32[96,16]{0,1:T(8,128)S(1)}, f32[96,16]{0,1:T(8,128)S(1)}, u32[]{:S(2)}, u32[]{:S(2)}) collective-permute-start(f32[96,16]{0,1:T(8,128)S(1)} %select_bitcast_fusion), channel_id=1, source_target_pairs={{1,0},{2,1},{3,2},{4,3},{5,4},{6,5},{7,6},{8,7},{9,8},{10,9},{11,1... | collective-permute-start | bytes 18440 | tf_op jit(solution)/shard_map/ppermute | solution.py:17
  354.9 4.3 %collective-permute-start.6 = (f32[96,16]{0,1:T(8,128)S(1)}, f32[96,16]{0,1:T(8,128)S(1)}, u32[]{:S(2)}, u32[]{:S(2)}) collective-permute-start(f32[96,16]{0,1:T(8,128)S(1)} %select_bitcast_fusion), channel_id=1, source_target_pairs={{0,1},{1,2},{2,3},{3,4},{4,5},{5,6},{6,7},{7,8},{8,9},{9,10},{10,1... | collective-permute-start | bytes 18440 | tf_op jit(solution)/shard_map/ppermute | solution.py:17
where the time goes:
time: 410 us; the launch traced here: 408 us
  blocking collectives  148 us (36%)
  local copies, waits for them, and re-layouts  83.5 us (20%)
  other arithmetic  52.8 us (13%)
  starting transfers between devices  44.5 us (11%)
  matrix products  43.1 us (11%)
  waiting for transfers between devices  25.2 us (6%)
  between operations  10.3 us (3%)
    psum x16, blocking collectives, over_axes(): shard = lax.psum(shard, axis)  148 us
    scatter x1, local copies, waits for them, and re-layouts, on_device(): jnp.zeros((partitions * capacity, 6, node_count), jnp.float32)  47.3 us
    dot_general x1, matrix products, wendland_map(): jnp.einsum('bjn,bcn->bcj', weight, force, precision=lax.Precision.HIGHEST)  42.6 us
    dot_general x4, other arithmetic, apply_operator(): jnp.einsum('abi,bi->ai', blocks[neighbor + 1], taken, precision=lax.Preci...  24.9 us
    ppermute x8, starting transfers between devices, from_behind(): return lax.ppermute(block, axis, route)  23.1 us
    all_to_all x1, waiting for transfers between devices, on_device(): lax.all_to_all(outgoing, DOM, split_axis=0, concat_axis=0, tiled=True)  22.7 us
    dot_general x4, other arithmetic, precondition(): jnp.einsum('abi,bi->ai', precond, vector, precision=lax.Precision.HIGHEST)  12.5 us
    all_to_all x1, starting transfers between devices, on_device(): lax.all_to_all(slot_target, DOM, split_axis=0, concat_axis=0, tiled=True)  11.5 us
  transfers between devices with their start and end apart: 10, of which 5 were waited for; matrix products, arithmetic and copies ran while one was open for 19% of the time, Pallas kernels for 0%

commit v1 on v0

v1 whole, which is shorter than its diff:
```python
import jax
import jax.numpy as jnp
from jax import lax
from jax.experimental import pallas as pl
from jax.experimental.pallas import tpu as pltpu
from jax.sharding import Mesh
from jax.sharding import PartitionSpec as P

DOM = ("dom_0", "dom_1", "dom_2", "dom_3")
SUPPORT = 0.9
CAP = 8
LANES = 128
STEPS = 4
F32 = jnp.float32
BF16 = jnp.bfloat16
NN = (((1,), (0,)), ((), ()))
NT = (((1,), (1,)), ((), ()))
TN = (((0,), (0,)), ((), ()))


def iota(shape, dim):
    return lax.broadcasted_iota(jnp.int32, shape, dim)


def flag(mask):
    return jnp.where(mask, 1.0, 0.0).astype(BF16)


def split3(x):
    high = x.astype(BF16)
    rest = x - high.astype(F32)
    mid = rest.astype(BF16)
    low = (rest - mid.astype(F32)).astype(BF16)
    return high, mid, low


def dot(a, b, dims):
    return lax.dot_general(a, b, dims, preferred_element_type=F32)


def pick(x, onehot, dims):
    return sum(dot(part, onehot, dims) for part in reversed(split3(x)))


def pick_from(onehot, x, dims):
    return sum(dot(onehot, part, dims) for part in reversed(split3(x)))


def pad_rows(x, rows):
    if x.shape[0] == rows:
        return x
    return jnp.concatenate([x, jnp.zeros((rows - x.shape[0], x.shape[1]), x.dtype)], axis=0)


def slots_kernel(dest_ref, target_ref, labels_ref, slot_ref):
    dest = dest_ref[...]
    count = dest.shape[1]
    parts = labels_ref.shape[0]
    hits = flag(iota((parts, count), 0) == dest)
    earlier = flag(iota((count, count), 0) < iota((count, count), 1))
    running = dot(hits, earlier, NN)
    before = jnp.sum(running * hits.astype(F32), axis=0, keepdims=True)
    slot_ref[...] = dest * CAP + before.astype(jnp.int32)
    place = iota((LANES, count), 0).astype(F32)
    wanted = jnp.where(place == before, (target_ref[...] + 1).astype(F32), 0.0)
    labels_ref[...] = dot(hits, wanted.astype(BF16), NT)


def slots(dest, target, parts):
    count = dest.shape[1]
    return pl.pallas_call(
        slots_kernel,
        out_shape=(
            jax.ShapeDtypeStruct((parts, LANES), F32),
            jax.ShapeDtypeStruct((1, count), jnp.int32),
        ),
        name="slots",
    )(dest, target)


def answer_kernel(labels_ref, coords_ref, onehot_ref, out_ref):
    rows = out_ref.shape[0]
    parts = labels_ref.shape[0]
    repeat = flag(iota((rows, parts), 0) // CAP == iota((rows, parts), 1))
    spread = dot(repeat, labels_ref[...].astype(BF16), NN)
    own = iota((rows, LANES), 0) % CAP == iota((rows, LANES), 1)
    own_label = jnp.where(own, spread, 0.0).astype(BF16)
    label = dot(own_label, jnp.ones((LANES, LANES), BF16), NN)
    onehot = flag(label == (iota((rows, LANES), 1) + 1).astype(F32))
    onehot_ref[...] = onehot
    out_ref[...] = pick_from(onehot, pad_rows(coords_ref[...], LANES), NT)


def answer(labels, coords):
    rows = labels.shape[0] * CAP
    return pl.pallas_call(
        answer_kernel,
        out_shape=(
            jax.ShapeDtypeStruct((rows, LANES), BF16),
            jax.ShapeDtypeStruct((rows, LANES), F32),
        ),
        name="answer",
    )(labels, coords)


def transfer_kernel(slot_ref, coords_ref, fluid_ref, force_ref, out_ref, turned, struct, mapped):
    rows = coords_ref.shape[0]
    count = slot_ref.shape[1]
    chosen = flag(iota((rows, count), 0) == slot_ref[...])
    struct[...] = pick(coords_ref[...], chosen, TN) * (1.0 / SUPPORT)
    nodes = fluid_ref.shape[2]
    for group in range(count // LANES):
        lanes = pl.ds(group * LANES, LANES)
        for c in range(3):
            turned[c] = fluid_ref[c, lanes, :].T * (1.0 / SUPPORT)
            turned[3 + c] = force_ref[c, lanes, :].T * 4.0
        where = [struct[pl.ds(c * 32, 32), lanes] for c in range(3)]

        def body(step, sums):
            sums = list(sums)
            for k in range(8):
                n = pl.ds(step * 8 + k, 1)
                apart = [where[c] - turned[c, n, :] for c in range(3)]
                square = apart[0] * apart[0] + apart[1] * apart[1] + apart[2] * apart[2]
                square = jnp.maximum(square, 1e-30)
                left = jnp.maximum(1.0 - square * lax.rsqrt(square), 0.0)
                twice = left * left
                quarter = twice * twice * (1.25 - left)
                for c in range(3):
                    sums[c] = sums[c] + quarter * turned[3 + c, n, :]
            return tuple(sums)

        zero = jnp.zeros((32, LANES), F32)
        sums = lax.fori_loop(0, nodes // 8, body, (zero, zero, zero))
        for c in range(3):
            mapped[pl.ds(c * 32, 32), lanes] = sums[c]
    mapped[pl.ds(96, 32), :] = jnp.zeros((32, count), F32)
    out_ref[...] = pick_from(chosen, mapped[...], NT)


def transfer(slot, coords, fluid, force):
    count = slot.shape[1]
    return pl.pallas_call(
        transfer_kernel,
        out_shape=jax.ShapeDtypeStruct(coords.shape, F32),
        scratch_shapes=[
            pltpu.VMEM((6, fluid.shape[2], LANES), F32),
            pltpu.VMEM((LANES, count), F32),
            pltpu.VMEM((LANES, count), F32),
        ],
        name="transfer",
    )(slot, coords, fluid, force)


def times(matrix, vectors, put):
    rows = vectors[0].shape[0]

    def body(step, carry):
        for k in range(8):
            row = step * 8 + k
            total = None
            for index, vector in enumerate(vectors):
                term = matrix(index, row) * vector
                total = term if total is None else total + term
            put(row, jnp.sum(total, axis=0, keepdims=True))
        return carry

    lax.fori_loop(0, rows // 8, body, 0)


def precondition(precond_ref, vector, out_ref):
    def put(row, value):
        out_ref[pl.ds(row, 1), :] = value

    times(lambda _, row: precond_ref[row], [vector], put)


def listed(halo_ref, vector):
    count = halo_ref.shape[0]
    rows = iota((count, LANES), 0)
    column = jnp.zeros((count, LANES), jnp.int32)
    for h in range(count):
        column = jnp.where(rows == h, halo_ref[h], column)
    onehot = flag(column == iota((count, LANES), 1))
    return pick_from(onehot, pad_rows(vector, LANES), NT)


def start_kernel(halo_ref, mapped_ref, onehot_ref, precond_ref, load_ref, pre_ref, send_ref):
    load = pick(mapped_ref[...], onehot_ref[...], TN)[: load_ref.shape[0]]
    load_ref[...] = load
    precondition(precond_ref, load, pre_ref)
    send_ref[...] = listed(halo_ref, pre_ref[...])


SMEM = pl.BlockSpec(memory_space=pltpu.SMEM)
VMEM = pl.BlockSpec(memory_space=pltpu.VMEM)


def start(halo_list, mapped, onehot, precond):
    shape = jax.ShapeDtypeStruct((precond.shape[0], LANES), F32)
    send = jax.ShapeDtypeStruct((halo_list.shape[0], LANES), F32)
    return pl.pallas_call(
        start_kernel,
        out_shape=(shape, shape, send),
        in_specs=[SMEM, VMEM, VMEM, VMEM],
        name="start",
    )(halo_list, mapped, onehot, precond)


def apply(parity_ref, columns_ref, blocks_ref, old, pre, near_ref, far_ref, out_ref):
    size = pre.shape[0]
    count = near_ref.shape[0]
    halo = jnp.concatenate([near_ref[...], far_ref[...]], axis=0)
    flip = (1 - parity_ref[0]) * count
    vectors = [pre]
    for neighbor in range(2):
        column = columns_ref[pl.ds(neighbor, 1), :]
        local = flag(iota((LANES, LANES), 0) == column)
        outside = flag(iota((2 * count, LANES), 0) == ((column - LANES) ^ flip))
        taken = pick(pre, local, NN) + pick(halo, outside, TN)[:size]
        vectors.append(taken)

    def put(row, value):
        out_ref[pl.ds(row, 1), :] = value

    times(lambda index, row: blocks_ref[index, row], vectors, put)
    out_ref[...] = out_ref[...] - old


def step_kernel(
    parity_ref, halo_ref, columns_ref, blocks_ref, precond_ref, old_ref, pre_ref, near_ref, far_ref,
    new_ref, new_pre_ref, send_ref,
):
    apply(parity_ref, columns_ref, blocks_ref, old_ref[...], pre_ref[...], near_ref, far_ref, new_ref)
    precondition(precond_ref, new_ref[...], new_pre_ref)
    send_ref[...] = listed(halo_ref, new_pre_ref[...])


def step(parity, halo_list, columns, blocks, precond, old, pre, near, far):
    shape = jax.ShapeDtypeStruct(old.shape, F32)
    return pl.pallas_call(
        step_kernel,
        out_shape=(shape, shape, jax.ShapeDtypeStruct(near.shape, F32)),
        in_specs=[SMEM, SMEM] + [VMEM] * 7,
        name="step",
    )(parity, halo_list, columns, blocks, precond, old, pre, near, far)


PAIRS = [(i, j) for i in range(STEPS + 1) for j in range(i, STEPS + 1)]


def last_kernel(
    parity_ref, columns_ref, blocks_ref, basis_ref, pre_ref, near_ref, far_ref, new_ref, sums_ref
):
    apply(
        parity_ref, columns_ref, blocks_ref, basis_ref[STEPS - 1], pre_ref[...], near_ref, far_ref, new_ref
    )
    vectors = [basis_ref[j] for j in range(STEPS)] + [new_ref[...]]
    sums = [jnp.sum(vectors[i] * vectors[j], axis=0, keepdims=True) for i, j in PAIRS]
    sums.append(jnp.zeros((LANES - len(sums), LANES), F32))
    ones = jnp.ones((sums_ref.shape[0], LANES), BF16)
    sums_ref[...] = pick_from(ones, jnp.concatenate(sums, axis=0), NT)


def last(parity, columns, blocks, basis, pre, near, far, parts):
    shape = jax.ShapeDtypeStruct(pre.shape, F32)
    return pl.pallas_call(
        last_kernel,
        out_shape=(shape, jax.ShapeDtypeStruct((parts, LANES), F32)),
        in_specs=[SMEM] + [VMEM] * 6,
        name="last",
    )(parity, columns, blocks, basis, pre, near, far)


def plus(x, y):
    return [a + b for a, b in zip(x, y)]


def scaled(scale, x):
    return [scale * a for a in x]


def recurrences(product):
    def inner(x, y):
        return sum(
            a * b * product[min(i, j), max(i, j)]
            for i, a in enumerate(x)
            for j, b in enumerate(y)
        )

    def image_of(x):
        return plus([x[0] * 0.0] + x, x + [x[0] * 0.0])

    one = product[0, 0] * 0.0 + 1.0
    residual = search = shadow = [one]
    answer = []
    alignment = product[0, 0]

    def add(x, y):
        size = max(len(x), len(y))
        zero = one * 0.0
        return plus(x + [zero] * (size - len(x)), y + [zero] * (size - len(y)))

    for iteration in range(2):
        image = image_of(search)
        step_size = alignment / inner(shadow, image)
        middle = add(residual, scaled(-step_size, image))
        middle_image = image_of(middle)
        smoothing = inner(middle_image, middle) / inner(middle_image, middle_image)
        answer = add(answer, add(scaled(step_size, search), scaled(smoothing, middle)))
        residual = add(middle, scaled(-smoothing, middle_image))
        if iteration == 0:
            new_alignment = inner(shadow, residual)
            momentum = new_alignment / alignment * (step_size / smoothing)
            search = add(residual, scaled(momentum, add(search, scaled(-smoothing, image))))
            alignment = new_alignment
    return answer, residual


def finish_kernel(sums_ref, basis_ref, new_ref, pre_ref, solution_ref, residual_ref):
    totals = jnp.sum(sums_ref[...], axis=0, keepdims=True)
    product = {pair: totals[:, k : k + 1] for k, pair in enumerate(PAIRS)}
    answer, residual = recurrences(product)
    vectors = [basis_ref[j] for j in range(STEPS)] + [new_ref[...]]
    solution_ref[...] = sum(a * pre_ref[j] for j, a in enumerate(answer))
    residual_ref[...] = sum(a * v for a, v in zip(residual, vectors))


def finish(sums, basis, new, pre):
    shape = jax.ShapeDtypeStruct(new.shape, F32)
    return pl.pallas_call(finish_kernel, out_shape=(shape, shape), name="finish")(sums, basis, new, pre)


def exchange(send):
    devices = lax.axis_size(DOM)
    near = lax.ppermute(send, DOM, [(i, i ^ 1) for i in range(devices)])
    send, near = lax.optimization_barrier((send, near))
    odd = range(1, devices - 1, 2)
    far = lax.ppermute(send, DOM, [(i, i + 1) for i in odd] + [(i + 1, i) for i in odd])
    return near, far


def to_all(x):
    return lax.all_to_all(x, DOM, split_axis=0, concat_axis=0, tiled=True)


def on_device(
    traction, fluid_coords, struct_coords, dest, target, blocks, columns, halo_list, precond
):
    parts = lax.axis_size(DOM)
    force = jnp.transpose(traction, (1, 0, 2))
    fluid = jnp.transpose(fluid_coords, (1, 0, 2))
    coords = struct_coords.reshape(-1, struct_coords.shape[2])
    labels, slot = slots(dest.reshape(1, -1), target.reshape(1, -1), parts)
    labels = to_all(labels)
    onehot, answered = answer(labels, coords)
    answered = to_all(answered.reshape(parts, CAP, LANES)).reshape(parts * CAP, LANES)
    mapped = transfer(slot, answered, fluid, force)
    mapped = to_all(mapped.reshape(parts, CAP, LANES)).reshape(parts * CAP, LANES)
    load, pre, send = start(halo_list, mapped, onehot, precond)
    parity = lax.axis_index("dom_3").astype(jnp.int32).reshape(1)
    basis, pres = [load], [pre]
    for _ in range(STEPS - 1):
        near, far = exchange(send)
        new, pre, send = step(
            parity, halo_list, columns, blocks, precond, basis[-1], pres[-1], near, far
        )
        basis.append(new)
        pres.append(pre)
    near, far = exchange(send)
    basis = jnp.stack(basis)
    new, sums = last(parity, columns, blocks, basis, pre, near, far, parts)
    solution, residual = finish(to_all(sums), basis, new, jnp.stack(pres))
    return load, solution, residual


def solution(mesh):
    finer = Mesh(mesh.devices.reshape(4, 4, 4, 2), DOM)
    in_specs = (
        P(DOM, None, None),
        P(DOM, None, None),
        P(None, None, DOM),
        P(DOM, None),
        P(DOM),
        P(None, None, None, DOM),
        P(None, DOM),
        P(DOM),
        P(None, None, DOM),
    )
    out_specs = (P(None, DOM), P(None, DOM), P(None, DOM))
    return jax.shard_map(
        on_device, mesh=finer, in_specs=in_specs, out_specs=out_specs, check_vma=False
    )
```

time: 410 us -> 177 us (0.43)
  blocking collectives: 148 us -> 59.8 us
  local copies, waits for them, and re-layouts: 83.5 us -> 3.04 us
  Pallas kernels: 0 us -> 56.7 us
  other arithmetic: 52.8 us -> 2.18 us
  matrix products: 43.1 us -> 0 us
  starting transfers between devices: 44.5 us -> 28.9 us
  between operations: 10.3 us -> 0.77 us
    psum x16 -> x0, blocking collectives: 148 us -> none  [over_axes(): shard = lax.psum(shard, axis)]
    all_to_all x0 -> x3, blocking collectives: none -> 59.8 us  [to_all(): return lax.all_to_all(x, DOM, split_axis=0, concat_axis=0, tiled=True)]
    pallas_call x0 -> x9, Pallas kernels: none -> 56.7 us  [the longest x3 27.6 us: step(): pl.pallas_call(step_kernel, out_shape=(shape, shape, jax.ShapeDtypeStruct...]
    scatter x2 -> x0, local copies, waits for them, and re-layouts: 49.9 us -> none  [the longest x1 47.3 us: on_device(): jnp.zeros((partitions * capacity, 6, node_count), jnp.float32)]
    dot_general x2 -> x0, matrix products: 43.1 us -> none  [the longest x1 42.6 us: wendland_map(): jnp.einsum('bjn,bcn->bcj', weight, force, precision=lax.Precision.HIGHEST)]
    dot_general x8 -> x0, other arithmetic: 37.4 us -> none  [the longest x4 24.9 us: apply_operator(): jnp.einsum('abi,bi->ai', blocks[neighbor + 1], taken, precision=lax.Preci...]
    gather x13 -> x0, local copies, waits for them, and re-layouts: 15.4 us -> none  [the longest x1 7.93 us: on_device(): jnp.take(struct_coords, labels.reshape(-1), axis=2)]
    all_to_all x2 -> x1, waiting for transfers between devices: 22.7 us -> 8.65 us  [to_all(): return lax.all_to_all(x, DOM, split_axis=0, concat_axis=0, tiled=True)]
  transfers between devices with their start and end apart: 10 -> 9, of which waited for: 5 -> 9; matrix products, arithmetic and copies ran while one was open for 19% -> 1% of each run, Pallas kernels for 0% -> 0%
where the time goes in v1:
time: 177 us; the launch traced here: 176 us
  blocking collectives  59.8 us (34%)
  Pallas kernels  56.7 us (32%)
  starting transfers between devices  28.9 us (16%)
  waiting for transfers between devices  24.8 us (14%)
  local copies, waits for them, and re-layouts  3.04 us (2%)
  other arithmetic  2.18 us (1%)
    all_to_all x3, blocking collectives, to_all(): return lax.all_to_all(x, DOM, split_axis=0, concat_axis=0, tiled=True)  59.8 us
    pallas_call x3, Pallas kernels, step(): pl.pallas_call(step_kernel, out_shape=(shape, shape, jax.ShapeDtypeStruct...  27.6 us
    all_to_all x1, starting transfers between devices, to_all(): return lax.all_to_all(x, DOM, split_axis=0, concat_axis=0, tiled=True)  19.5 us
    pallas_call x1, Pallas kernels, transfer(): pl.pallas_call(transfer_kernel, out_shape=jax.ShapeDtypeStruct(coords.sha...  11.4 us
    ppermute x4, waiting for transfers between devices, exchange(): lax.ppermute(send, DOM, [(i, i + 1) for i in odd] + [(i + 1, i) for i in...  11 us
    all_to_all x1, waiting for transfers between devices, to_all(): return lax.all_to_all(x, DOM, split_axis=0, concat_axis=0, tiled=True)  8.65 us
    ppermute x4, starting transfers between devices, exchange(): lax.ppermute(send, DOM, [(i, i + 1) for i in odd] + [(i + 1, i) for i in...  8.1 us
    pallas_call x1, Pallas kernels, last(): pl.pallas_call(last_kernel, out_shape=(shape, jax.ShapeDtypeStruct((parts...  7.4 us
  transfers between devices with their start and end apart: 9, of which 9 were waited for; matrix products, arithmetic and copies ran while one was open for 1% of the time, Pallas kernels for 0%

profile of v1, /device:TPU:1, one launch (start us, length us, event | category | flops | bytes accessed | tf_op | source)
XLA Modules:
  0.0 176.2 jit_solution(2531630050949662472)
XLA Ops:
  0.6 1.8 %slots.1 = (f32[128,128]{1,0:T(8,128)}, s32[1,512]{1,0:T(1,128)}) custom-call(s32[1,512]{1,0:T(1,128)} %bitcast.45, s32[1,512]{1,0:T(1,128)} %bitcast.46), custom_call_target="tpu_custom_call" | custom-call | tf_op jit(solution)/shard_map/slots/pallas_call | solution.py:71
  2.4 21.3 %all_to_all.32 = f32[128,1,128]{2,1,0:T(1,128)} all-to-all(f32[128,1,128]{2,1,0:T(1,128)} %bitcast.42), channel_id=1, replica_groups=mesh['dom_0'=4,'dom_1'=4,'dom_2'=4,'dom_3'=2] {'dom_0','dom_1','dom_2','..., dimensions={0} | all-to-all | bytes 131072 | tf_op jit(solution)/shard_map/all_to_all | solution.py:344
  23.7 2.3 %answer.1 = (bf16[1024,128]{1,0:T(8,128)(2,1)}, f32[1024,128]{1,0:T(8,128)}) custom-call(f32[128,128]{1,0:T(8,128)} %bitcast.32, f32[96,128]{1,0:T(8,128)} %bitcast.43), custom_call_target="tpu_custom_call" | custom-call | tf_op jit(solution)/shard_map/answer/pallas_call | solution.py:96
  26.0 19.2 %all_to_all.33 = f32[128,8,128]{2,1,0:T(8,128)} all-to-all(f32[128,8,128]{2,1,0:T(8,128)} %bitcast.31), channel_id=1, replica_groups=mesh['dom_0'=4,'dom_1'=4,'dom_2'=4,'dom_3'=2] {'dom_0','dom_1','dom_2','..., dimensions={0} | all-to-all | bytes 1048576 | tf_op jit(solution)/shard_map/all_to_all | solution.py:344
  45.2 11.4 %transfer.1 = f32[1024,128]{1,0:T(8,128)} custom-call(s32[1,512]{1,0:T(1,128)} %get-tuple-element.31.slot_ref, f32[1024,128]{1,0:T(8,128)} %bitcast.26, f32[3,512,128]{2,1,0:T(8,128)} %bitcast.29, f32[3,512,128]{2,1,0:T(8,128)} %bitcast.30), custom_call_target="tpu_custom_call" | custom-call | tf_op jit(solution)/shard_map/transfer/pallas_call | solution.py:143
  56.6 19.3 %all_to_all.34 = f32[128,8,128]{2,1,0:T(8,128)} all-to-all(f32[128,8,128]{2,1,0:T(8,128)} %bitcast.27), channel_id=1, replica_groups=mesh['dom_0'=4,'dom_1'=4,'dom_2'=4,'dom_3'=2] {'dom_0','dom_1','dom_2','..., dimensions={0} | all-to-all | bytes 1048576 | tf_op jit(solution)/shard_map/all_to_all | solution.py:344
  75.9 4.3 %start.1 = (f32[96,128]{1,0:T(8,128)}, f32[96,128]{1,0:T(8,128)}, f32[16,128]{1,0:T(8,128)}) custom-call(s32[16]{0:T(128)} %halo_ref.7, f32[1024,128]{1,0:T(8,128)} %bitcast.28, bf16[1024,128]{1,0:T(8,128)(2,1)} %get-tuple-element.34.onehot_ref, f32[96,96,128]{2,1,0:T(8,128)} %precond_ref.7), custom_call_target="tpu_custom_call" | custom-call | tf_op jit(solution)/shard_map/start/pallas_call | solution.py:202
  80.2 1.3 collective-permute-start
  81.5 1.0 collective-permute-done.near_ref
  82.5 0.0 copy-start.8
  82.5 2.0 %collective-permute-start.1 = (f32[16,128]{1,0:T(8,128)}, f32[16,128]{1,0:T(8,128)S(1)}, u32[]{:S(2)}, u32[]{:S(2)}) collective-permute-start(f32[16,128]{1,0:T(8,128)} %get-tuple-element.39), channel_id=1, source_target_pairs={{1,2},{3,4},{5,6},{7,8},{9,10},{11,12},{13,14},{15,16},{17,18},{19... | collective-permute-start | bytes 24584 | tf_op jit(solution)/shard_map/ppermute | solution.py:339
  84.5 3.1 %collective-permute-done.1.far_ref = f32[16,128]{1,0:T(8,128)S(1)} collective-permute-done((f32[16,128]{1,0:T(8,128)}, f32[16,128]{1,0:T(8,128)S(1)}, u32[]{:S(2)}, u32[]{:S(2)}) %collective-permute-start.1) | collective-permute-done | bytes 8224 | tf_op jit(solution)/shard_map/ppermute | solution.py:339
  87.7 0.0 copy-start.10
  87.7 0.0 copy-done.8
  87.7 0.6 copy-done.10
  88.3 9.2 %step.3 = (f32[96,128]{1,0:T(8,128)}, f32[96,128]{1,0:T(8,128)}, f32[16,128]{1,0:T(8,128)}) custom-call(s32[1]{0:T(128)} %bitcast.12.parity_ref, s32[16]{0:T(128)} %halo_ref.7, s32[2,128]{1,0:T(2,128)} %columns_ref.7, f32[3,96,96,128]{3,2,1,0:T(8,128)} %blocks_ref.7, f32[96,96,128]{2,1,0:T(8,128)} %precond_ref.7, f32[96,128]{1,0:T(8,128)} %get-tuple-element.28.old_ref, ...), custom_call_target="tpu_custom_call" | custom-call | tf_op jit(solution)/shard_map/step/pallas_call | solution.py:241
  97.5 0.0 collective-permute-start.2
  97.5 1.4 collective-permute-done.2.near_ref
  98.8 0.0 copy-start.11
  98.8 2.0 %collective-permute-start.3 = (f32[16,128]{1,0:T(8,128)}, f32[16,128]{1,0:T(8,128)S(1)}, u32[]{:S(2)}, u32[]{:S(2)}) collective-permute-start(f32[16,128]{1,0:T(8,128)} %get-tuple-element.44), channel_id=1, source_target_pairs={{1,2},{3,4},{5,6},{7,8},{9,10},{11,12},{13,14},{15,16},{17,18},{19... | collective-permute-start | bytes 24584 | tf_op jit(solution)/shard_map/ppermute | solution.py:339
  100.9 3.1 %collective-permute-done.3.far_ref = f32[16,128]{1,0:T(8,128)S(1)} collective-permute-done((f32[16,128]{1,0:T(8,128)}, f32[16,128]{1,0:T(8,128)S(1)}, u32[]{:S(2)}, u32[]{:S(2)}) %collective-permute-start.3) | collective-permute-done | bytes 8224 | tf_op jit(solution)/shard_map/ppermute | solution.py:339
  104.0 0.0 copy-start.14
  104.0 0.0 copy-done.11
  104.0 0.6 copy-done.14
  104.6 9.2 %step.4 = (f32[96,128]{1,0:T(8,128)}, f32[96,128]{1,0:T(8,128)}, f32[16,128]{1,0:T(8,128)}) custom-call(s32[1]{0:T(128)} %bitcast.12.parity_ref, s32[16]{0:T(128)} %halo_ref.7, s32[2,128]{1,0:T(2,128)} %columns_ref.7, f32[3,96,96,128]{3,2,1,0:T(8,128)} %blocks_ref.7, f32[96,96,128]{2,1,0:T(8,128)} %precond_ref.7, f32[96,128]{1,0:T(8,128)} %get-tuple-element.40.old_ref, ...), custom_call_target="tpu_custom_call" | custom-call | tf_op jit(solution)/shard_map/step/pallas_call | solution.py:241
  113.8 0.0 copy-start.2
  113.8 0.0 copy-start.5
  113.8 0.0 copy-start.7
  113.8 0.1 collective-permute-start.4
  113.9 1.4 collective-permute-done.4.near_ref
  115.3 0.0 copy-start.12
  115.3 2.0 %collective-permute-start.5 = (f32[16,128]{1,0:T(8,128)}, f32[16,128]{1,0:T(8,128)S(1)}, u32[]{:S(2)}, u32[]{:S(2)}) collective-permute-start(f32[16,128]{1,0:T(8,128)} %get-tuple-element.49), channel_id=1, source_target_pairs={{1,2},{3,4},{5,6},{7,8},{9,10},{11,12},{13,14},{15,16},{17,18},{19... | collective-permute-start | bytes 24584 | tf_op jit(solution)/shard_map/ppermute | solution.py:339
  117.3 3.1 %collective-permute-done.5.far_ref = f32[16,128]{1,0:T(8,128)S(1)} collective-permute-done((f32[16,128]{1,0:T(8,128)}, f32[16,128]{1,0:T(8,128)S(1)}, u32[]{:S(2)}, u32[]{:S(2)}) %collective-permute-start.5) | collective-permute-done | bytes 8224 | tf_op jit(solution)/shard_map/ppermute | solution.py:339
  120.4 0.0 copy-start.15
  120.4 0.0 copy-done.12
  120.4 0.6 copy-done.15
  121.0 0.0 copy-start.3
  121.0 0.0 copy-start.4
  121.0 0.0 copy-start.6
  121.0 9.2 %step.5 = (f32[96,128]{1,0:T(8,128)}, f32[96,128]{1,0:T(8,128)}, f32[16,128]{1,0:T(8,128)}) custom-call(s32[1]{0:T(128)} %bitcast.12.parity_ref, s32[16]{0:T(128)} %halo_ref.7, s32[2,128]{1,0:T(2,128)} %columns_ref.7, f32[3,96,96,128]{3,2,1,0:T(8,128)} %blocks_ref.7, f32[96,96,128]{2,1,0:T(8,128)} %precond_ref.7, f32[96,128]{1,0:T(8,128)} %get-tuple-element.45.old_ref, ...), custom_call_target="tpu_custom_call" | custom-call | tf_op jit(solution)/shard_map/step/pallas_call | solution.py:241
  130.2 0.0 copy-start.1
  130.2 0.0 collective-permute-start.6
  130.2 1.4 collective-permute-done.6.near_ref
  131.6 0.0 copy-start.9
  131.6 2.0 %collective-permute-start.7 = (f32[16,128]{1,0:T(8,128)}, f32[16,128]{1,0:T(8,128)S(1)}, u32[]{:S(2)}, u32[]{:S(2)}) collective-permute-start(f32[16,128]{1,0:T(8,128)} %get-tuple-element.54), channel_id=1, source_target_pairs={{1,2},{3,4},{5,6},{7,8},{9,10},{11,12},{13,14},{15,16},{17,18},{19... | collective-permute-start | bytes 24584 | tf_op jit(solution)/shard_map/ppermute | solution.py:339
  133.7 0.0 copy-done.2
  133.7 0.0 copy-done.5
  133.7 0.0 copy-done.7
  133.7 1.5 pad_maximum_fusion.basis_ref
  135.2 1.6 collective-permute-done.7.far_ref
  136.8 0.0 copy-start.13
  136.8 0.0 copy-done.9
  136.8 0.6 copy-done.13
  137.4 7.4 %last.1 = (f32[96,128]{1,0:T(8,128)}, f32[128,128]{1,0:T(8,128)}) custom-call(s32[1]{0:T(128)} %bitcast.12.parity_ref, s32[2,128]{1,0:T(2,128)} %columns_ref.7, f32[3,96,96,128]{3,2,1,0:T(8,128)} %blocks_ref.7, f32[4,96,128]{2,1,0:T(8,128)} %pad_maximum_fusion.basis_ref, f32[96,128]{1,0:T(8,128)} %get-tuple-element.51.pre_ref, f32[16,128]{1,0:T(8,128)} %copy-done.9, ...), custom_call_target="tpu_custom_call" | custom-call | tf_op jit(solution)/shard_map/last/pallas_call | solution.py:267
  144.8 19.5 %all-to-all-start.3 = ((f32[128,1,128]{2,1,0:T(1,128)}), f32[128,1,128]{2,1,0:T(1,128)S(1)}, u32[]{:S(2)}, u32[]{:S(2)}) async-start(f32[128,1,128]{2,1,0:T(1,128)} %bitcast.41), calls=%async_computation.3 | async-start | bytes 131072 | tf_op jit(solution)/shard_map/all_to_all | solution.py:344
  164.3 0.0 copy-done.3
  164.3 0.0 copy-done.4
  164.3 0.0 copy-done.6
  164.3 0.0 copy-done.1
  164.3 0.7 pad_maximum_fusion.1.pre_ref
  165.0 8.6 %all-to-all-done.3 = f32[128,1,128]{2,1,0:T(1,128)S(1)} async-done(((f32[128,1,128]{2,1,0:T(1,128)}), f32[128,1,128]{2,1,0:T(1,128)S(1)}, u32[]{:S(2)}, u32[]{:S(2)}) %all-to-all-start.3) | async-done | bytes 65568 | tf_op jit(solution)/shard_map/all_to_all | solution.py:344
  173.6 0.0 copy-start
  173.6 0.6 copy-done
  174.3 2.0 %finish.1 = (f32[96,128]{1,0:T(8,128)}, f32[96,128]{1,0:T(8,128)}) custom-call(f32[128,128]{1,0:T(8,128)} %bitcast.33, f32[4,96,128]{2,1,0:T(8,128)} %pad_maximum_fusion.basis_ref, f32[96,128]{1,0:T(8,128)} %get-tuple-element.56.new_ref, f32[4,96,128]{2,1,0:T(8,128)} %pad_maximum_fusion.1.pre_ref), custom_call_target="tpu_custom_call" | custom-call | tf_op jit(solution)/shard_map/finish/pallas_call | solution.py:331
Async XLA Ops:
  80.2 2.3 %collective-permute-start = (f32[16,128]{1,0:T(8,128)}, f32[16,128]{1,0:T(8,128)S(1)}, u32[]{:S(2)}, u32[]{:S(2)}) collective-permute-start(f32[16,128]{1,0:T(8,128)} %get-tuple-element.39), channel_id=1, source_target_pairs={{0,1},{1,0},{2,3},{3,2},{4,5},{5,4},{6,7},{7,6},{8,9},{9,8},{10,11... | collective-permute-start | bytes 24584 | tf_op jit(solution)/shard_map/ppermute | solution.py:336
  82.5 5.2 %copy-start.8 = (f32[16,128]{1,0:T(8,128)}, f32[16,128]{1,0:T(8,128)S(1)}, u32[]{:S(2)}) copy-start(f32[16,128]{1,0:T(8,128)S(1)} %collective-permute-done.near_ref) | copy-start | bytes 24580
  82.5 5.2 %collective-permute-start.1 = (f32[16,128]{1,0:T(8,128)}, f32[16,128]{1,0:T(8,128)S(1)}, u32[]{:S(2)}, u32[]{:S(2)}) collective-permute-start(f32[16,128]{1,0:T(8,128)} %get-tuple-element.39), channel_id=1, source_target_pairs={{1,2},{3,4},{5,6},{7,8},{9,10},{11,12},{13,14},{15,16},{17,18},{19... | collective-permute-start | bytes 24584 | tf_op jit(solution)/shard_map/ppermute | solution.py:339
  87.7 0.6 copy-start.10
  97.5 1.4 collective-permute-start.2
  98.8 5.2 %copy-start.11 = (f32[16,128]{1,0:T(8,128)}, f32[16,128]{1,0:T(8,128)S(1)}, u32[]{:S(2)}) copy-start(f32[16,128]{1,0:T(8,128)S(1)} %collective-permute-done.2.near_ref) | copy-start | bytes 24580
  98.8 5.2 %collective-permute-start.3 = (f32[16,128]{1,0:T(8,128)}, f32[16,128]{1,0:T(8,128)S(1)}, u32[]{:S(2)}, u32[]{:S(2)}) collective-permute-start(f32[16,128]{1,0:T(8,128)} %get-tuple-element.44), channel_id=1, source_target_pairs={{1,2},{3,4},{5,6},{7,8},{9,10},{11,12},{13,14},{15,16},{17,18},{19... | collective-permute-start | bytes 24584 | tf_op jit(solution)/shard_map/ppermute | solution.py:339
  104.0 0.6 copy-start.14
  113.8 19.9 %copy-start.2 = (f32[96,128]{1,0:T(8,128)S(1)}, f32[96,128]{1,0:T(8,128)}, u32[]{:S(2)}) copy-start(f32[96,128]{1,0:T(8,128)} %get-tuple-element.28.old_ref) | copy-start | bytes 147460
  113.8 19.9 %copy-start.5 = (f32[96,128]{1,0:T(8,128)S(1)}, f32[96,128]{1,0:T(8,128)}, u32[]{:S(2)}) copy-start(f32[96,128]{1,0:T(8,128)} %get-tuple-element.40.old_ref) | copy-start | bytes 147460
  113.8 19.9 %copy-start.7 = (f32[96,128]{1,0:T(8,128)S(1)}, f32[96,128]{1,0:T(8,128)}, u32[]{:S(2)}) copy-start(f32[96,128]{1,0:T(8,128)} %get-tuple-element.45.old_ref) | copy-start | bytes 147460
  113.8 1.5 collective-permute-start.4
  115.3 5.2 %copy-start.12 = (f32[16,128]{1,0:T(8,128)}, f32[16,128]{1,0:T(8,128)S(1)}, u32[]{:S(2)}) copy-start(f32[16,128]{1,0:T(8,128)S(1)} %collective-permute-done.4.near_ref) | copy-start | bytes 24580
  115.3 5.2 %collective-permute-start.5 = (f32[16,128]{1,0:T(8,128)}, f32[16,128]{1,0:T(8,128)S(1)}, u32[]{:S(2)}, u32[]{:S(2)}) collective-permute-start(f32[16,128]{1,0:T(8,128)} %get-tuple-element.49), channel_id=1, source_target_pairs={{1,2},{3,4},{5,6},{7,8},{9,10},{11,12},{13,14},{15,16},{17,18},{19... | collective-permute-start | bytes 24584 | tf_op jit(solution)/shard_map/ppermute | solution.py:339
  120.4 0.6 copy-start.15
  121.0 43.2 %copy-start.3 = (f32[96,128]{1,0:T(8,128)S(1)}, f32[96,128]{1,0:T(8,128)}, u32[]{:S(2)}) copy-start(f32[96,128]{1,0:T(8,128)} %get-tuple-element.36.pre_ref) | copy-start | bytes 147460
  121.0 43.2 %copy-start.4 = (f32[96,128]{1,0:T(8,128)S(1)}, f32[96,128]{1,0:T(8,128)}, u32[]{:S(2)}) copy-start(f32[96,128]{1,0:T(8,128)} %get-tuple-element.41.pre_ref) | copy-start | bytes 147460
  121.0 43.2 %copy-start.6 = (f32[96,128]{1,0:T(8,128)S(1)}, f32[96,128]{1,0:T(8,128)}, u32[]{:S(2)}) copy-start(f32[96,128]{1,0:T(8,128)} %get-tuple-element.46.pre_ref) | copy-start | bytes 147460
  130.2 34.1 %copy-start.1 = (f32[96,128]{1,0:T(8,128)S(1)}, f32[96,128]{1,0:T(8,128)}, u32[]{:S(2)}) copy-start(f32[96,128]{1,0:T(8,128)} %get-tuple-element.51.pre_ref) | copy-start | bytes 147460
  130.2 1.4 collective-permute-start.6
  131.6 5.2 %copy-start.9 = (f32[16,128]{1,0:T(8,128)}, f32[16,128]{1,0:T(8,128)S(1)}, u32[]{:S(2)}) copy-start(f32[16,128]{1,0:T(8,128)S(1)} %collective-permute-done.6.near_ref) | copy-start | bytes 24580
  131.6 5.2 %collective-permute-start.7 = (f32[16,128]{1,0:T(8,128)}, f32[16,128]{1,0:T(8,128)S(1)}, u32[]{:S(2)}, u32[]{:S(2)}) collective-permute-start(f32[16,128]{1,0:T(8,128)} %get-tuple-element.54), channel_id=1, source_target_pairs={{1,2},{3,4},{5,6},{7,8},{9,10},{11,12},{13,14},{15,16},{17,18},{19... | collective-permute-start | bytes 24584 | tf_op jit(solution)/shard_map/ppermute | solution.py:339
  136.8 0.6 copy-start.13
  144.8 28.8 %all-to-all-start.3 = ((f32[128,1,128]{2,1,0:T(1,128)}), f32[128,1,128]{2,1,0:T(1,128)S(1)}, u32[]{:S(2)}, u32[]{:S(2)}) async-start(f32[128,1,128]{2,1,0:T(1,128)} %bitcast.41), calls=%async_computation.3 | async-start | bytes 131072 | tf_op jit(solution)/shard_map/all_to_all | solution.py:344
  173.6 0.6 copy-start

commit v2 on v1

v2 whole, which is shorter than its diff:
```python
import jax
import jax.numpy as jnp
from jax import lax
from jax.experimental import pallas as pl
from jax.experimental.pallas import tpu as pltpu
from jax.sharding import Mesh
from jax.sharding import PartitionSpec as P

DOM = ("dom_0", "dom_1", "dom_2", "dom_3")
SUPPORT = 0.9
CAP = 8
LANES = 128
STEPS = 4
F32 = jnp.float32
BF16 = jnp.bfloat16
NN = (((1,), (0,)), ((), ()))
NT = (((1,), (1,)), ((), ()))
TN = (((0,), (0,)), ((), ()))


SMEM = pl.BlockSpec(memory_space=pltpu.SMEM)
VMEM = pl.BlockSpec(memory_space=pltpu.VMEM)
ANY = pl.BlockSpec(memory_space=pl.ANY)
MIB = 1 << 20


def limit(mib):
    return pltpu.CompilerParams(vmem_limit_bytes=mib * MIB)


def near_core(*arrays):
    return [pltpu.with_memory_space_constraint(x, pltpu.VMEM) for x in arrays]


def in_hbm(*arrays):
    return [pltpu.with_memory_space_constraint(x, pltpu.HBM) for x in arrays]


def iota(shape, dim):
    return lax.broadcasted_iota(jnp.int32, shape, dim)


def flag(mask):
    return jnp.where(mask, 1.0, 0.0).astype(BF16)


def split3(x):
    high = x.astype(BF16)
    rest = x - high.astype(F32)
    mid = rest.astype(BF16)
    low = (rest - mid.astype(F32)).astype(BF16)
    return high, mid, low


def dot(a, b, dims):
    return lax.dot_general(a, b, dims, preferred_element_type=F32)


def pick(x, onehot, dims):
    return sum(dot(part, onehot, dims) for part in reversed(split3(x)))


def pick_from(onehot, x, dims):
    return sum(dot(onehot, part, dims) for part in reversed(split3(x)))


def pad_rows(x, rows):
    if x.shape[0] == rows:
        return x
    return jnp.concatenate([x, jnp.zeros((rows - x.shape[0], x.shape[1]), x.dtype)], axis=0)


def slots_kernel(dest_ref, target_ref, labels_ref, slot_ref):
    dest = dest_ref[...]
    count = dest.shape[1]
    parts = labels_ref.shape[0]
    hits = flag(iota((parts, count), 0) == dest)
    earlier = flag(iota((count, count), 0) < iota((count, count), 1))
    running = dot(hits, earlier, NN)
    before = jnp.sum(running * hits.astype(F32), axis=0, keepdims=True)
    slot_ref[...] = dest * CAP + before.astype(jnp.int32)
    place = iota((LANES, count), 0).astype(F32)
    wanted = jnp.where(place == before, (target_ref[...] + 1).astype(F32), 0.0)
    labels_ref[...] = dot(hits, wanted.astype(BF16), NT)


def slots(dest, target, parts):
    count = dest.shape[1]
    return pl.pallas_call(
        slots_kernel,
        out_shape=(
            jax.ShapeDtypeStruct((parts, LANES), F32),
            jax.ShapeDtypeStruct((1, count), jnp.int32),
        ),
        compiler_params=limit(2),
        name="slots",
    )(dest, target)


def prepare_kernel(
    halo_ref, parity_ref, columns_ref, after_ref, fluid_ref, force_ref,
    turned_ref, local_ref, outer_ref, listed_ref,
    points, sems,
):
    copies = [
        pltpu.make_async_copy(ref, points.at[k], sems.at[k])
        for k, ref in enumerate((fluid_ref, force_ref))
    ]
    for copy in copies:
        copy.start()
    flip = (1 - parity_ref[0]) * listed_ref.shape[0]
    for neighbor in range(2):
        column = columns_ref[pl.ds(neighbor, 1), :]
        local_ref[neighbor] = flag(iota((LANES, LANES), 0) == column)
        outer_ref[neighbor] = flag(iota(outer_ref.shape[1:], 0) == ((column - LANES) ^ flip))
    rows = iota(listed_ref.shape, 0)
    column = jnp.zeros(listed_ref.shape, jnp.int32)
    for h in range(listed_ref.shape[0]):
        column = jnp.where(rows == h, halo_ref[h], column)
    listed_ref[...] = flag(column == iota(listed_ref.shape, 1))
    for copy in copies:
        copy.wait()
    for group in range(points.shape[2] // LANES):
        lanes = pl.ds(group * LANES, LANES)
        for kind, factor in enumerate((1.0 / SUPPORT, 4.0)):
            for c in range(3):
                turned_ref[group, 3 * kind + c] = points[kind, c, lanes, :].T * factor


def prepare(halo_list, parity, columns, after, fluid, force):
    count, nodes = fluid.shape[1:]
    halo = halo_list.shape[0]
    return pl.pallas_call(
        prepare_kernel,
        out_shape=(
            pltpu.VMEM((count // LANES, 6, nodes, LANES), F32),
            pltpu.VMEM((2, LANES, LANES), BF16),
            pltpu.VMEM((2, 2 * halo, LANES), BF16),
            pltpu.VMEM((halo, LANES), BF16),
        ),
        in_specs=[SMEM, SMEM, VMEM] + [ANY] * 3,
        out_specs=[VMEM] * 4,
        scratch_shapes=[pltpu.VMEM((2, 3, count, nodes), F32), pltpu.SemaphoreType.DMA((2,))],
        compiler_params=limit(4),
        cost_estimate=pl.CostEstimate(flops=0, bytes_accessed=3 * MIB, transcendentals=0),
        name="prepare",
    )(halo_list, parity, columns, *in_hbm(after, fluid, force))


def answer_kernel(labels_ref, coords_ref, after_ref, onehot_ref, out_ref):
    rows = out_ref.shape[0]
    parts = labels_ref.shape[0]
    repeat = flag(iota((rows, parts), 0) // CAP == iota((rows, parts), 1))
    spread = dot(repeat, labels_ref[...].astype(BF16), NN)
    own = iota((rows, LANES), 0) % CAP == iota((rows, LANES), 1)
    own_label = jnp.where(own, spread, 0.0).astype(BF16)
    label = dot(own_label, jnp.ones((LANES, LANES), BF16), NN)
    onehot = flag(label == (iota((rows, LANES), 1) + 1).astype(F32))
    onehot_ref[...] = onehot
    out_ref[...] = pick_from(onehot, pad_rows(coords_ref[...], LANES), NT)


def answer(labels, coords, after):
    rows = labels.shape[0] * CAP
    return pl.pallas_call(
        answer_kernel,
        out_shape=(
            jax.ShapeDtypeStruct((rows, LANES), BF16),
            jax.ShapeDtypeStruct((rows, LANES), F32),
        ),
        in_specs=[VMEM, VMEM, ANY],
        compiler_params=limit(6),
        name="answer",
    )(labels, coords, after)


def transfer_kernel(
    slot_ref, coords_ref, turned_ref, blocks_ref, precond_ref, out_ref, blocks_out, precond_out,
    struct, mapped, sems,
):
    tables = [
        pltpu.make_async_copy(precond_ref, precond_out, sems.at[0]),
        pltpu.make_async_copy(blocks_ref, blocks_out, sems.at[1]),
    ]
    for copy in tables:
        copy.start()
    rows = coords_ref.shape[0]
    count = slot_ref.shape[1]
    chosen = flag(iota((rows, count), 0) == slot_ref[...])
    struct[...] = pick(coords_ref[...], chosen, TN) * (1.0 / SUPPORT)
    nodes = turned_ref.shape[2]
    for group in range(count // LANES):
        lanes = pl.ds(group * LANES, LANES)
        where = [struct[pl.ds(c * 32, 32), lanes] for c in range(3)]

        def body(step, sums):
            sums = list(sums)
            for k in range(8):
                n = pl.ds(step * 8 + k, 1)
                apart = [where[c] - turned_ref[group, c, n, :] for c in range(3)]
                square = apart[0] * apart[0] + apart[1] * apart[1] + apart[2] * apart[2]
                square = jnp.maximum(square, 1e-30)
                left = jnp.maximum(1.0 - square * lax.rsqrt(square), 0.0)
                twice = left * left
                quarter = twice * twice * (1.25 - left)
                for c in range(3):
                    sums[c] = sums[c] + quarter * turned_ref[group, 3 + c, n, :]
            return tuple(sums)

        zero = jnp.zeros((32, LANES), F32)
        sums = lax.fori_loop(0, nodes // 8, body, (zero, zero, zero))
        for c in range(3):
            mapped[pl.ds(c * 32, 32), lanes] = sums[c]
    mapped[pl.ds(96, 32), :] = jnp.zeros((32, count), F32)
    out_ref[...] = pick_from(chosen, mapped[...], NT)
    for copy in tables:
        copy.wait()


def transfer(slot, coords, turned, blocks, precond):
    count = slot.shape[1]
    return pl.pallas_call(
        transfer_kernel,
        out_shape=(
            jax.ShapeDtypeStruct(coords.shape, F32),
            pltpu.VMEM(blocks.shape, F32),
            pltpu.VMEM(precond.shape, F32),
        ),
        in_specs=[VMEM] * 3 + [ANY] * 2,
        out_specs=[VMEM] * 3,
        scratch_shapes=[
            pltpu.VMEM((LANES, count), F32),
            pltpu.VMEM((LANES, count), F32),
            pltpu.SemaphoreType.DMA((2,)),
        ],
        compiler_params=limit(10),
        name="transfer",
    )(slot, coords, *near_core(turned), *in_hbm(blocks, precond))


def times(matrices, vectors, put):
    rows = vectors[0].shape[0]

    def body(step, carry):
        for k in range(8):
            row = step * 8 + k
            total = None
            for matrix, vector in zip(matrices, vectors):
                term = matrix[row] * vector
                total = term if total is None else total + term
            put(row, jnp.sum(total, axis=0, keepdims=True))
        return carry

    lax.fori_loop(0, rows // 8, body, 0)


def precondition(precond_ref, listed_ref, vector, out_ref, send_ref):
    def put(row, value):
        out_ref[pl.ds(row, 1), :] = value

    times([precond_ref], [vector], put)
    send_ref[...] = pick_from(listed_ref[...], pad_rows(out_ref[...], LANES), NT)


def start_kernel(mapped_ref, onehot_ref, precond_ref, listed_ref, load_ref, pre_ref, send_ref):
    load = pick(mapped_ref[...], onehot_ref[...], TN)[: load_ref.shape[0]]
    load_ref[...] = load
    precondition(precond_ref, listed_ref, load, pre_ref, send_ref)


def start(mapped, onehot, precond, listed):
    shape = pltpu.VMEM((precond.shape[0], LANES), F32)
    return pl.pallas_call(
        start_kernel,
        out_shape=(shape, shape, pltpu.VMEM(listed.shape, F32)),
        in_specs=[VMEM] * 4,
        out_specs=[VMEM] * 3,
        compiler_params=limit(6),
        name="start",
    )(mapped, onehot, *near_core(precond, listed))


def inside_kernel(blocks_ref, local_ref, outer_ref, old_ref, pre_ref, near_ref, part_ref, taken_ref):
    pre = pre_ref[...]
    size = pre.shape[0]
    count = near_ref.shape[0]

    def put(row, value):
        part_ref[pl.ds(row, 1), :] = value - old_ref[pl.ds(row, 1), :]

    times([blocks_ref.at[0]], [pre], put)
    for neighbor in range(2):
        taken = pick(pre, local_ref[neighbor], NN)
        taken_ref[neighbor] = taken + pick(near_ref[...], outer_ref[neighbor, :count, :], TN)[:size]


def inside(blocks, local, outer, old, pre, near):
    size = old.shape[0]
    return pl.pallas_call(
        inside_kernel,
        out_shape=(pltpu.VMEM(old.shape, F32), pltpu.VMEM((2, size, LANES), F32)),
        in_specs=[VMEM] * 6,
        out_specs=[VMEM] * 2,
        compiler_params=limit(6),
        cost_estimate=pl.CostEstimate(flops=0, bytes_accessed=2 * MIB, transcendentals=0),
        name="inside",
    )(*near_core(blocks, local, outer, old, pre, near))


def outside(blocks_ref, outer_ref, part_ref, taken_ref, far_ref, new_ref):
    size = part_ref.shape[0]
    count = far_ref.shape[0]
    vectors = [
        taken_ref[neighbor] + pick(far_ref[...], outer_ref[neighbor, count:, :], TN)[:size]
        for neighbor in range(2)
    ]

    def put(row, value):
        new_ref[pl.ds(row, 1), :] = value + part_ref[pl.ds(row, 1), :]

    times([blocks_ref.at[1], blocks_ref.at[2]], vectors, put)


def step_kernel(
    blocks_ref, precond_ref, outer_ref, listed_ref, part_ref, taken_ref, far_ref,
    new_ref, new_pre_ref, send_ref,
):
    outside(blocks_ref, outer_ref, part_ref, taken_ref, far_ref, new_ref)
    precondition(precond_ref, listed_ref, new_ref[...], new_pre_ref, send_ref)


def step(blocks, precond, outer, listed, part, taken, far):
    shape = pltpu.VMEM(part.shape, F32)
    return pl.pallas_call(
        step_kernel,
        out_shape=(shape, shape, pltpu.VMEM(far.shape, F32)),
        in_specs=[VMEM] * 7,
        out_specs=[VMEM] * 3,
        compiler_params=limit(6),
        name="step",
    )(*near_core(blocks, precond, outer, listed, part, taken, far))


PAIRS = [(i, j) for i in range(STEPS + 1) for j in range(i, STEPS + 1)]


def last_kernel(
    blocks_ref, outer_ref, part_ref, taken_ref, far_ref, b0_ref, b1_ref, b2_ref, b3_ref,
    new_ref, sums_ref,
):
    outside(blocks_ref, outer_ref, part_ref, taken_ref, far_ref, new_ref)
    vectors = [ref[...] for ref in (b0_ref, b1_ref, b2_ref, b3_ref, new_ref)]
    sums = [jnp.sum(vectors[i] * vectors[j], axis=0, keepdims=True) for i, j in PAIRS]
    sums.append(jnp.zeros((LANES - len(sums), LANES), F32))
    ones = jnp.ones((sums_ref.shape[0], LANES), BF16)
    sums_ref[...] = pick_from(ones, jnp.concatenate(sums, axis=0), NT)


def last(blocks, outer, part, taken, far, basis, parts):
    return pl.pallas_call(
        last_kernel,
        out_shape=(pltpu.VMEM(part.shape, F32), pltpu.VMEM((parts, LANES), F32)),
        in_specs=[VMEM] * 9,
        out_specs=[VMEM] * 2,
        compiler_params=limit(6),
        name="last",
    )(*near_core(blocks, outer, part, taken, far, *basis))


def plus(x, y):
    return [a + b for a, b in zip(x, y)]


def scaled(scale, x):
    return [scale * a for a in x]


def recurrences(product):
    def inner(x, y):
        return sum(
            a * b * product[min(i, j), max(i, j)]
            for i, a in enumerate(x)
            for j, b in enumerate(y)
        )

    def image_of(x):
        return plus([x[0] * 0.0] + x, x + [x[0] * 0.0])

    one = product[0, 0] * 0.0 + 1.0
    residual = search = shadow = [one]
    answer = []
    alignment = product[0, 0]

    def add(x, y):
        size = max(len(x), len(y))
        zero = one * 0.0
        return plus(x + [zero] * (size - len(x)), y + [zero] * (size - len(y)))

    for iteration in range(2):
        image = image_of(search)
        step_size = alignment / inner(shadow, image)
        middle = add(residual, scaled(-step_size, image))
        middle_image = image_of(middle)
        smoothing = inner(middle_image, middle) / inner(middle_image, middle_image)
        answer = add(answer, add(scaled(step_size, search), scaled(smoothing, middle)))
        residual = add(middle, scaled(-smoothing, middle_image))
        if iteration == 0:
            new_alignment = inner(shadow, residual)
            momentum = new_alignment / alignment * (step_size / smoothing)
            search = add(residual, scaled(momentum, add(search, scaled(-smoothing, image))))
            alignment = new_alignment
    return answer, residual


def finish_kernel(sums_ref, *refs):
    basis, pres, (solution_ref, residual_ref) = refs[:5], refs[5:9], refs[9:]
    totals = jnp.sum(sums_ref[...], axis=0, keepdims=True)
    product = {pair: totals[:, k : k + 1] for k, pair in enumerate(PAIRS)}
    answer, residual = recurrences(product)
    solution_ref[...] = sum(a * ref[...] for a, ref in zip(answer, pres))
    residual_ref[...] = sum(a * ref[...] for a, ref in zip(residual, basis))


def finish(sums, basis, pres):
    shape = jax.ShapeDtypeStruct(pres[0].shape, F32)
    return pl.pallas_call(
        finish_kernel,
        out_shape=(shape, shape),
        in_specs=[VMEM] * 10,
        compiler_params=limit(4),
        name="finish",
    )(*near_core(sums, *basis, *pres))


def to_near(send):
    devices = lax.axis_size(DOM)
    return lax.ppermute(send, DOM, [(i, i ^ 1) for i in range(devices)])


def to_far(send):
    odd = range(1, lax.axis_size(DOM) - 1, 2)
    return lax.ppermute(send, DOM, [(i, i + 1) for i in odd] + [(i + 1, i) for i in odd])


def to_all(x):
    return lax.all_to_all(x, DOM, split_axis=0, concat_axis=0, tiled=True)


def on_device(
    traction, fluid_coords, struct_coords, dest, target, blocks, columns, halo_list, precond
):
    parts = lax.axis_size(DOM)
    parity = lax.axis_index("dom_3").astype(jnp.int32).reshape(1)
    force = jnp.transpose(traction, (1, 0, 2))
    fluid = jnp.transpose(fluid_coords, (1, 0, 2))
    coords = struct_coords.reshape(-1, struct_coords.shape[2])
    wanted, slot = slots(dest.reshape(1, -1), target.reshape(1, -1), parts)
    turned, local, outer, listed = prepare(halo_list, parity, columns, wanted, fluid, force)
    onehot, answered = answer(to_all(wanted), coords, listed)
    answered = to_all(answered.reshape(parts, CAP, LANES)).reshape(parts * CAP, LANES)
    mapped, blocks, precond = transfer(slot, answered, turned, blocks, precond)
    mapped = to_all(mapped.reshape(parts, CAP, LANES)).reshape(parts * CAP, LANES)
    load, pre, send = start(mapped, onehot, precond, listed)
    basis, pres = [load], [pre]
    for j in range(STEPS):
        near = to_near(send)
        send, near = lax.optimization_barrier((send, near))
        far = to_far(send)
        part, taken = inside(blocks, local, outer, basis[-1], pres[-1], near)
        if j < STEPS - 1:
            new, pre, send = step(blocks, precond, outer, listed, part, taken, far)
            pres.append(pre)
        else:
            new, sums = last(blocks, outer, part, taken, far, basis, parts)
        basis.append(new)
    solution, residual = finish(to_all(sums), basis, pres)
    return load, solution, residual


def solution(mesh):
    finer = Mesh(mesh.devices.reshape(4, 4, 4, 2), DOM)
    in_specs = (
        P(DOM, None, None),
        P(DOM, None, None),
        P(None, None, DOM),
        P(DOM, None),
        P(DOM),
        P(None, None, None, DOM),
        P(None, DOM),
        P(DOM),
        P(None, None, DOM),
    )
    out_specs = (P(None, DOM), P(None, DOM), P(None, DOM))
    return jax.shard_map(
        on_device, mesh=finer, in_specs=in_specs, out_specs=out_specs, check_vma=False
    )
```

time: 177 us -> 134 us (0.76)
  Pallas kernels: 56.7 us -> 25.1 us
  blocking collectives: 59.8 us -> 36.2 us
  starting transfers between devices: 28.9 us -> 40.4 us
  waiting for transfers between devices: 24.8 us -> 27.4 us
  other arithmetic: 2.18 us -> 0 us
    pallas_call x7 -> x12, Pallas kernels: 52.7 us -> 23.3 us  [the longest x1 8.57 us: transfer(): pl.pallas_call(transfer_kernel, out_shape=(jax.ShapeDtypeStruct(coords.sh...]
    all_to_all x3 -> x2, blocking collectives: 59.8 us -> 36.2 us  [to_all(): return lax.all_to_all(x, DOM, split_axis=0, concat_axis=0, tiled=True)]
    all_to_all x1 -> x2, starting transfers between devices: 19.5 us -> 30.9 us  [to_all(): return lax.all_to_all(x, DOM, split_axis=0, concat_axis=0, tiled=True)]
    all_to_all x1 -> x2, waiting for transfers between devices: 8.65 us -> 14.4 us  [to_all(): return lax.all_to_all(x, DOM, split_axis=0, concat_axis=0, tiled=True)]
    ppermute x8, waiting for transfers between devices: 16.2 us -> 13 us  [the longest x4 8.53 us: to_far(): lax.ppermute(send, DOM, [(i, i + 1) for i in odd] + [(i + 1, i) for i in...]
    another operation x2 -> x0, other arithmetic: 2.18 us -> none  [the longest x1 1.48 us: on_device(): basis = jnp.stack(basis)]
    unnamed x32 -> x11, local copies, waits for them, and re-layouts: 3.04 us -> 4.11 us
  transfers between devices with their start and end apart: 9 -> 10, of which waited for: 9 -> 10; matrix products, arithmetic and copies ran while one was open for 1% -> 0% of each run, Pallas kernels for 0% -> 4%
where the time goes in v2:
time: 134 us
  starting transfers between devices  40.4 us (30%)
  blocking collectives  36.2 us (27%)
  waiting for transfers between devices  27.4 us (20%)
  Pallas kernels  25.1 us (19%)
  local copies, waits for them, and re-layouts  4.11 us (3%)
    all_to_all x2, blocking collectives, to_all(): return lax.all_to_all(x, DOM, split_axis=0, concat_axis=0, tiled=True)  36.2 us
    all_to_all x2, starting transfers between devices, to_all(): return lax.all_to_all(x, DOM, split_axis=0, concat_axis=0, tiled=True)  30.9 us
    all_to_all x2, waiting for transfers between devices, to_all(): return lax.all_to_all(x, DOM, split_axis=0, concat_axis=0, tiled=True)  14.4 us
    pallas_call x1, Pallas kernels, transfer(): pl.pallas_call(transfer_kernel, out_shape=(jax.ShapeDtypeStruct(coords.sh...  8.57 us
    ppermute x4, waiting for transfers between devices, to_far(): lax.ppermute(send, DOM, [(i, i + 1) for i in odd] + [(i + 1, i) for i in...  8.53 us
    ppermute x4, starting transfers between devices, to_far(): lax.ppermute(send, DOM, [(i, i + 1) for i in odd] + [(i + 1, i) for i in...  8.1 us
    pallas_call x3, Pallas kernels, step(): pl.pallas_call(step_kernel, out_shape=(shape, shape, pltpu.VMEM(far.shape...  5.28 us
    ppermute x4, waiting for transfers between devices, to_near(): return lax.ppermute(send, DOM, [(i, i ^ 1) for i in range(devices)])  4.44 us
  transfers between devices with their start and end apart: 10, of which 10 were waited for; matrix products, arithmetic and copies ran while one was open for 0% of the time, Pallas kernels for 4%

profile of v2, /device:TPU:1, one launch (start us, length us, event | category | flops | bytes accessed | tf_op | source)
XLA Modules:
  0.0 133.9 jit_solution(10651454750598032922)
XLA Ops:
  0.6 0.0 copy-start.1
  0.6 0.7 copy-done.1
  1.3 0.0 copy-start.2
  1.3 0.7 copy-done.2
  2.0 1.1 slots.1
  3.1 11.5 %all-to-all-start = ((f32[128,1,128]{2,1,0:T(1,128)}), f32[128,1,128]{2,1,0:T(1,128)S(1)}, u32[]{:S(2)}, u32[]{:S(2)}) async-start(f32[128,1,128]{2,1,0:T(1,128)} %bitcast.3), calls=%async_computation | async-start | bytes 131072 | tf_op jit(solution)/shard_map/all_to_all | solution.py:446
  14.6 0.0 copy-start.3
  14.6 0.7 copy-done.3
  15.2 0.0 copy-start.4
  15.2 0.7 copy-done.4
  15.9 2.4 %prepare.1 = (f32[4,6,128,128]{3,2,1,0:T(8,128)S(1)}, bf16[2,128,128]{2,1,0:T(8,128)(2,1)S(1)}, bf16[2,32,128]{2,1,0:T(8,128)(2,1)S(1)}, bf16[16,128]{1,0:T(8,128)(2,1)S(1)}) custom-call(s32[16]{0:T(128)S(1)} %copy-done.4, s32[1]{0:T(128)} %bitcast.6.parity_ref, s32[2,128]{1,0:T(2,128)S(1)} %copy-done.3, f32[128,128]{1,0:T(8,128)} %get-tuple-element.47.after_ref, ...), custom_call_target="tpu_custom_call" | custom-call | bytes 3145728 | tf_op jit(solution)/shard_map/prepare/pallas_call | solution.py:133
  18.3 5.6 %all-to-all-done = f32[128,1,128]{2,1,0:T(1,128)S(1)} async-done(((f32[128,1,128]{2,1,0:T(1,128)}), f32[128,1,128]{2,1,0:T(1,128)S(1)}, u32[]{:S(2)}, u32[]{:S(2)}) %all-to-all-start) | async-done | bytes 65568 | tf_op jit(solution)/shard_map/all_to_all | solution.py:446
  23.9 0.0 copy-start
  23.9 0.8 copy-done
  24.7 0.7 answer.1
  25.4 18.1 %all_to_all.32 = f32[128,8,128]{2,1,0:T(8,128)S(1)} all-to-all(f32[128,8,128]{2,1,0:T(8,128)S(1)} %bitcast.21), channel_id=1, replica_groups=mesh['dom_0'=4,'dom_1'=4,'dom_2'=4,'dom_3'=2] {'dom_0','dom_1','dom_2','..., dimensions={0} | all-to-all | bytes 1048576 | tf_op jit(solution)/shard_map/all_to_all | solution.py:446
  43.5 8.6 %transfer.1 = (f32[1024,128]{1,0:T(8,128)S(1)}, f32[3,96,96,128]{3,2,1,0:T(8,128)S(1)}, f32[96,96,128]{2,1,0:T(8,128)S(1)}) custom-call(s32[1,512]{1,0:T(1,128)S(1)} %get-tuple-element.46.slot_ref, f32[1024,128]{1,0:T(8,128)S(1)} %bitcast.18, f32[4,6,128,128]{3,2,1,0:T(8,128)S(1)} %get-tuple-element.50.turned_ref, f32[3,96,96,128]{3,2,1,0:T(8,128)} %blocks_ref.1, ...), custom_call_target="tpu_custom_call" | custom-call | tf_op jit(solution)/shard_map/transfer/pallas_call | solution.py:222
  52.1 18.1 %all_to_all.33 = f32[128,8,128]{2,1,0:T(8,128)S(1)} all-to-all(f32[128,8,128]{2,1,0:T(8,128)S(1)} %bitcast.20), channel_id=1, replica_groups=mesh['dom_0'=4,'dom_1'=4,'dom_2'=4,'dom_3'=2] {'dom_0','dom_1','dom_2','..., dimensions={0} | all-to-all | bytes 1048576 | tf_op jit(solution)/shard_map/all_to_all | solution.py:446
  70.2 1.1 start.1
  71.2 1.3 collective-permute-start
  72.5 0.8 collective-permute-done.near_ref
  73.4 2.0 %collective-permute-start.1 = (f32[16,128]{1,0:T(8,128)S(1)}, f32[16,128]{1,0:T(8,128)S(1)}, u32[]{:S(2)}, u32[]{:S(2)}) collective-permute-start(f32[16,128]{1,0:T(8,128)S(1)} %get-tuple-element.63), channel_id=1, source_target_pairs={{1,2},{3,4},{5,6},{7,8},{9,10},{11,12},{13,14},{15,16},{17,18},{19... | collective-permute-start | bytes 24584 | tf_op jit(solution)/shard_map/ppermute | solution.py:442
  75.4 0.8 inside.4
  76.2 2.1 %collective-permute-done.1.far_ref = f32[16,128]{1,0:T(8,128)S(1)} collective-permute-done((f32[16,128]{1,0:T(8,128)S(1)}, f32[16,128]{1,0:T(8,128)S(1)}, u32[]{:S(2)}, u32[]{:S(2)}) %collective-permute-start.1) | collective-permute-done | bytes 8224 | tf_op jit(solution)/shard_map/ppermute | solution.py:442
  78.3 1.8 %step.3 = (f32[96,128]{1,0:T(8,128)S(1)}, f32[96,128]{1,0:T(8,128)S(1)}, f32[16,128]{1,0:T(8,128)S(1)}) custom-call(f32[3,96,96,128]{3,2,1,0:T(8,128)S(1)} %get-tuple-element.55.blocks_ref, f32[96,96,128]{2,1,0:T(8,128)S(1)} %get-tuple-element.53.precond_ref, bf16[2,32,128]{2,1,0:T(8,128)(2,1)S(1)} %get-tuple-element.56.outer_ref, ...), custom_call_target="tpu_custom_call" | custom-call | tf_op jit(solution)/shard_map/step/pallas_call | solution.py:334
  80.1 0.0 collective-permute-start.2
  80.1 1.2 collective-permute-done.2.near_ref
  81.3 2.0 %collective-permute-start.3 = (f32[16,128]{1,0:T(8,128)S(1)}, f32[16,128]{1,0:T(8,128)S(1)}, u32[]{:S(2)}, u32[]{:S(2)}) collective-permute-start(f32[16,128]{1,0:T(8,128)S(1)} %get-tuple-element.70), channel_id=1, source_target_pairs={{1,2},{3,4},{5,6},{7,8},{9,10},{11,12},{13,14},{15,16},{17,18},{19... | collective-permute-start | bytes 24584 | tf_op jit(solution)/shard_map/ppermute | solution.py:442
  83.4 0.8 inside.5
  84.1 2.1 %collective-permute-done.3.far_ref = f32[16,128]{1,0:T(8,128)S(1)} collective-permute-done((f32[16,128]{1,0:T(8,128)S(1)}, f32[16,128]{1,0:T(8,128)S(1)}, u32[]{:S(2)}, u32[]{:S(2)}) %collective-permute-start.3) | collective-permute-done | bytes 8224 | tf_op jit(solution)/shard_map/ppermute | solution.py:442
  86.3 1.8 %step.4 = (f32[96,128]{1,0:T(8,128)S(1)}, f32[96,128]{1,0:T(8,128)S(1)}, f32[16,128]{1,0:T(8,128)S(1)}) custom-call(f32[3,96,96,128]{3,2,1,0:T(8,128)S(1)} %get-tuple-element.55.blocks_ref, f32[96,96,128]{2,1,0:T(8,128)S(1)} %get-tuple-element.53.precond_ref, bf16[2,32,128]{2,1,0:T(8,128)(2,1)S(1)} %get-tuple-element.56.outer_ref, ...), custom_call_target="tpu_custom_call" | custom-call | tf_op jit(solution)/shard_map/step/pallas_call | solution.py:334
  88.0 0.0 collective-permute-start.4
  88.1 1.2 collective-permute-done.4.near_ref
  89.3 2.0 %collective-permute-start.5 = (f32[16,128]{1,0:T(8,128)S(1)}, f32[16,128]{1,0:T(8,128)S(1)}, u32[]{:S(2)}, u32[]{:S(2)}) collective-permute-start(f32[16,128]{1,0:T(8,128)S(1)} %get-tuple-element.77), channel_id=1, source_target_pairs={{1,2},{3,4},{5,6},{7,8},{9,10},{11,12},{13,14},{15,16},{17,18},{19... | collective-permute-start | bytes 24584 | tf_op jit(solution)/shard_map/ppermute | solution.py:442
  91.3 0.8 inside.6
  92.1 2.1 %collective-permute-done.5.far_ref = f32[16,128]{1,0:T(8,128)S(1)} collective-permute-done((f32[16,128]{1,0:T(8,128)S(1)}, f32[16,128]{1,0:T(8,128)S(1)}, u32[]{:S(2)}, u32[]{:S(2)}) %collective-permute-start.5) | collective-permute-done | bytes 8224 | tf_op jit(solution)/shard_map/ppermute | solution.py:442
  94.2 1.8 %step.5 = (f32[96,128]{1,0:T(8,128)S(1)}, f32[96,128]{1,0:T(8,128)S(1)}, f32[16,128]{1,0:T(8,128)S(1)}) custom-call(f32[3,96,96,128]{3,2,1,0:T(8,128)S(1)} %get-tuple-element.55.blocks_ref, f32[96,96,128]{2,1,0:T(8,128)S(1)} %get-tuple-element.53.precond_ref, bf16[2,32,128]{2,1,0:T(8,128)(2,1)S(1)} %get-tuple-element.56.outer_ref, ...), custom_call_target="tpu_custom_call" | custom-call | tf_op jit(solution)/shard_map/step/pallas_call | solution.py:334
  96.0 0.0 collective-permute-start.6
  96.0 1.2 collective-permute-done.6.near_ref
  97.2 2.0 %collective-permute-start.7 = (f32[16,128]{1,0:T(8,128)S(1)}, f32[16,128]{1,0:T(8,128)S(1)}, u32[]{:S(2)}, u32[]{:S(2)}) collective-permute-start(f32[16,128]{1,0:T(8,128)S(1)} %get-tuple-element.84), channel_id=1, source_target_pairs={{1,2},{3,4},{5,6},{7,8},{9,10},{11,12},{13,14},{15,16},{17,18},{19... | collective-permute-start | bytes 24584 | tf_op jit(solution)/shard_map/ppermute | solution.py:442
  99.3 0.8 inside.7
  100.1 2.1 %collective-permute-done.7.far_ref = f32[16,128]{1,0:T(8,128)S(1)} collective-permute-done((f32[16,128]{1,0:T(8,128)S(1)}, f32[16,128]{1,0:T(8,128)S(1)}, u32[]{:S(2)}, u32[]{:S(2)}) %collective-permute-start.7) | collective-permute-done | bytes 8224 | tf_op jit(solution)/shard_map/ppermute | solution.py:442
  102.2 2.0 %last.1 = (f32[96,128]{1,0:T(8,128)S(1)}, f32[128,128]{1,0:T(8,128)}) custom-call(f32[3,96,96,128]{3,2,1,0:T(8,128)S(1)} %get-tuple-element.55.blocks_ref, bf16[2,32,128]{2,1,0:T(8,128)(2,1)S(1)} %get-tuple-element.56.outer_ref, f32[96,128]{1,0:T(8,128)S(1)} %get-tuple-element.82.part_ref, f32[2,96,128]{2,1,0:T(8,128)S(1)} %get-tuple-element.83.taken_ref, ...), custom_call_target="tpu_custom_call" | custom-call | tf_op jit(solution)/shard_map/last/pallas_call | solution.py:360
  104.2 19.5 %all-to-all-start.3 = ((f32[128,1,128]{2,1,0:T(1,128)}), f32[128,1,128]{2,1,0:T(1,128)S(1)}, u32[]{:S(2)}, u32[]{:S(2)}) async-start(f32[128,1,128]{2,1,0:T(1,128)} %bitcast.14), calls=%async_computation.3 | async-start | bytes 131072 | tf_op jit(solution)/shard_map/all_to_all | solution.py:446
  123.6 0.6 copy.14
  124.3 8.8 %all-to-all-done.3 = f32[128,1,128]{2,1,0:T(1,128)S(1)} async-done(((f32[128,1,128]{2,1,0:T(1,128)}), f32[128,1,128]{2,1,0:T(1,128)S(1)}, u32[]{:S(2)}, u32[]{:S(2)}) %all-to-all-start.3) | async-done | bytes 65568 | tf_op jit(solution)/shard_map/all_to_all | solution.py:446
  133.0 0.9 finish.1
Async XLA Ops:
  0.6 0.7 copy-start.1
  1.3 0.7 copy-start.2
  3.1 20.9 %all-to-all-start = ((f32[128,1,128]{2,1,0:T(1,128)}), f32[128,1,128]{2,1,0:T(1,128)S(1)}, u32[]{:S(2)}, u32[]{:S(2)}) async-start(f32[128,1,128]{2,1,0:T(1,128)} %bitcast.3), calls=%async_computation | async-start | bytes 131072 | tf_op jit(solution)/shard_map/all_to_all | solution.py:446
  14.6 0.7 copy-start.3
  15.2 0.7 copy-start.4
  23.9 0.8 copy-start
  71.2 2.1 %collective-permute-start = (f32[16,128]{1,0:T(8,128)S(1)}, f32[16,128]{1,0:T(8,128)S(1)}, u32[]{:S(2)}, u32[]{:S(2)}) collective-permute-start(f32[16,128]{1,0:T(8,128)S(1)} %get-tuple-element.63), channel_id=1, source_target_pairs={{0,1},{1,0},{2,3},{3,2},{4,5},{5,4},{6,7},{7,6},{8,9},{9,8},{10,11... | collective-permute-start | bytes 24584 | tf_op jit(solution)/shard_map/ppermute | solution.py:437
  73.4 5.0 %collective-permute-start.1 = (f32[16,128]{1,0:T(8,128)S(1)}, f32[16,128]{1,0:T(8,128)S(1)}, u32[]{:S(2)}, u32[]{:S(2)}) collective-permute-start(f32[16,128]{1,0:T(8,128)S(1)} %get-tuple-element.63), channel_id=1, source_target_pairs={{1,2},{3,4},{5,6},{7,8},{9,10},{11,12},{13,14},{15,16},{17,18},{19... | collective-permute-start | bytes 24584 | tf_op jit(solution)/shard_map/ppermute | solution.py:442
  80.1 1.2 collective-permute-start.2
  81.3 5.0 %collective-permute-start.3 = (f32[16,128]{1,0:T(8,128)S(1)}, f32[16,128]{1,0:T(8,128)S(1)}, u32[]{:S(2)}, u32[]{:S(2)}) collective-permute-start(f32[16,128]{1,0:T(8,128)S(1)} %get-tuple-element.70), channel_id=1, source_target_pairs={{1,2},{3,4},{5,6},{7,8},{9,10},{11,12},{13,14},{15,16},{17,18},{19... | collective-permute-start | bytes 24584 | tf_op jit(solution)/shard_map/ppermute | solution.py:442
  88.0 1.2 collective-permute-start.4
  89.3 5.0 %collective-permute-start.5 = (f32[16,128]{1,0:T(8,128)S(1)}, f32[16,128]{1,0:T(8,128)S(1)}, u32[]{:S(2)}, u32[]{:S(2)}) collective-permute-start(f32[16,128]{1,0:T(8,128)S(1)} %get-tuple-element.77), channel_id=1, source_target_pairs={{1,2},{3,4},{5,6},{7,8},{9,10},{11,12},{13,14},{15,16},{17,18},{19... | collective-permute-start | bytes 24584 | tf_op jit(solution)/shard_map/ppermute | solution.py:442
  96.0 1.2 collective-permute-start.6
  97.2 5.0 %collective-permute-start.7 = (f32[16,128]{1,0:T(8,128)S(1)}, f32[16,128]{1,0:T(8,128)S(1)}, u32[]{:S(2)}, u32[]{:S(2)}) collective-permute-start(f32[16,128]{1,0:T(8,128)S(1)} %get-tuple-element.84), channel_id=1, source_target_pairs={{1,2},{3,4},{5,6},{7,8},{9,10},{11,12},{13,14},{15,16},{17,18},{19... | collective-permute-start | bytes 24584 | tf_op jit(solution)/shard_map/ppermute | solution.py:442
  104.2 28.8 %all-to-all-start.3 = ((f32[128,1,128]{2,1,0:T(1,128)}), f32[128,1,128]{2,1,0:T(1,128)S(1)}, u32[]{:S(2)}, u32[]{:S(2)}) async-start(f32[128,1,128]{2,1,0:T(1,128)} %bitcast.14), calls=%async_computation.3 | async-start | bytes 131072 | tf_op jit(solution)/shard_map/all_to_all | solution.py:446

commit v3 on v2

--- a/solution.py
+++ b/solution.py
@@ -94,12 +94,12 @@
         ),
         compiler_params=limit(2),
         name="slots",
-    )(dest, target)
+    )(*in_hbm(dest, target))
 
 
 def prepare_kernel(
-    halo_ref, parity_ref, columns_ref, after_ref, fluid_ref, force_ref,
-    turned_ref, local_ref, outer_ref, listed_ref,
+    halo_ref, parity_ref, columns_ref, coords_ref, after_ref, fluid_ref, force_ref,
+    turned_ref, coords_out, local_ref, outer_ref, listed_ref,
     points, sems,
 ):
     copies = [
@@ -108,6 +108,7 @@
     ]
     for copy in copies:
         copy.start()
+    coords_out[...] = pad_rows(coords_ref[...], LANES)
     flip = (1 - parity_ref[0]) * listed_ref.shape[0]
     for neighbor in range(2):
         column = columns_ref[pl.ds(neighbor, 1), :]
@@ -127,27 +128,28 @@
                 turned_ref[group, 3 * kind + c] = points[kind, c, lanes, :].T * factor
 
 
-def prepare(halo_list, parity, columns, after, fluid, force):
+def prepare(halo_list, parity, columns, coords, after, fluid, force):
     count, nodes = fluid.shape[1:]
     halo = halo_list.shape[0]
     return pl.pallas_call(
         prepare_kernel,
         out_shape=(
             pltpu.VMEM((count // LANES, 6, nodes, LANES), F32),
+            pltpu.VMEM((LANES, LANES), F32),
             pltpu.VMEM((2, LANES, LANES), BF16),
             pltpu.VMEM((2, 2 * halo, LANES), BF16),
             pltpu.VMEM((halo, LANES), BF16),
         ),
-        in_specs=[SMEM, SMEM, VMEM] + [ANY] * 3,
-        out_specs=[VMEM] * 4,
+        in_specs=[SMEM, SMEM, VMEM, VMEM] + [ANY] * 3,
+        out_specs=[VMEM] * 5,
         scratch_shapes=[pltpu.VMEM((2, 3, count, nodes), F32), pltpu.SemaphoreType.DMA((2,))],
         compiler_params=limit(4),
         cost_estimate=pl.CostEstimate(flops=0, bytes_accessed=3 * MIB, transcendentals=0),
         name="prepare",
-    )(halo_list, parity, columns, *in_hbm(after, fluid, force))
-
-
-def answer_kernel(labels_ref, coords_ref, after_ref, onehot_ref, out_ref):
+    )(*in_hbm(halo_list, parity, columns, coords, after, fluid, force))
+
+
+def answer_kernel(labels_ref, coords_ref, onehot_ref, out_ref):
     rows = out_ref.shape[0]
     parts = labels_ref.shape[0]
     repeat = flag(iota((rows, parts), 0) // CAP == iota((rows, parts), 1))
@@ -157,10 +159,10 @@
     label = dot(own_label, jnp.ones((LANES, LANES), BF16), NN)
     onehot = flag(label == (iota((rows, LANES), 1) + 1).astype(F32))
     onehot_ref[...] = onehot
-    out_ref[...] = pick_from(onehot, pad_rows(coords_ref[...], LANES), NT)
-
-
-def answer(labels, coords, after):
+    out_ref[...] = pick_from(onehot, coords_ref[...], NT)
+
+
+def answer(labels, coords):
     rows = labels.shape[0] * CAP
     return pl.pallas_call(
         answer_kernel,
@@ -168,10 +170,10 @@
             jax.ShapeDtypeStruct((rows, LANES), BF16),
             jax.ShapeDtypeStruct((rows, LANES), F32),
         ),
-        in_specs=[VMEM, VMEM, ANY],
+        in_specs=[VMEM, VMEM],
         compiler_params=limit(6),
         name="answer",
-    )(labels, coords, after)
+    )(labels, *near_core(coords))
 
 
 def transfer_kernel(
@@ -455,17 +457,18 @@
     fluid = jnp.transpose(fluid_coords, (1, 0, 2))
     coords = struct_coords.reshape(-1, struct_coords.shape[2])
     wanted, slot = slots(dest.reshape(1, -1), target.reshape(1, -1), parts)
-    turned, local, outer, listed = prepare(halo_list, parity, columns, wanted, fluid, force)
-    onehot, answered = answer(to_all(wanted), coords, listed)
+    turned, coords, local, outer, listed = prepare(
+        halo_list, parity, columns, coords, wanted, fluid, force
+    )
+    onehot, answered = answer(to_all(wanted), coords)
     answered = to_all(answered.reshape(parts, CAP, LANES)).reshape(parts * CAP, LANES)
     mapped, blocks, precond = transfer(slot, answered, turned, blocks, precond)
     mapped = to_all(mapped.reshape(parts, CAP, LANES)).reshape(parts * CAP, LANES)
     load, pre, send = start(mapped, onehot, precond, listed)
     basis, pres = [load], [pre]
     for j in range(STEPS):
+        far = to_far(send)
         near = to_near(send)
-        send, near = lax.optimization_barrier((send, near))
-        far = to_far(send)
         part, taken = inside(blocks, local, outer, basis[-1], pres[-1], near)
         if j < STEPS - 1:
             new, pre, send = step(blocks, precond, outer, listed, part, taken, far)

time: 134 us -> 128 us (0.955)
  waiting for transfers between devices: 27.4 us -> 22.8 us
  local copies, waits for them, and re-layouts: 4.11 us -> 0.62 us
    ppermute x4, waiting for transfers between devices: 4.44 us -> 0.01 us  [to_near(): return lax.ppermute(send, DOM, [(i, i ^ 1) for i in range(devices)])]
    unnamed x11 -> x1, local copies, waits for them, and re-layouts: 4.11 us -> 0.62 us
  transfers between devices with their start and end apart: 10 -> 10, of which waited for: 10 -> 6; matrix products, arithmetic and copies ran while one was open for 0% -> 0% of each run, Pallas kernels for 4% -> 5%
where the time goes in v3:
time: 128 us
  starting transfers between devices  41.6 us (32%)
  blocking collectives  36.2 us (28%)
  Pallas kernels  26 us (20%)
  waiting for transfers between devices  22.8 us (18%)
    all_to_all x2, blocking collectives, to_all(): return lax.all_to_all(x, DOM, split_axis=0, concat_axis=0, tiled=True)  36.2 us
    all_to_all x2, starting transfers between devices, to_all(): return lax.all_to_all(x, DOM, split_axis=0, concat_axis=0, tiled=True)  30.9 us
    all_to_all x2, waiting for transfers between devices, to_all(): return lax.all_to_all(x, DOM, split_axis=0, concat_axis=0, tiled=True)  15.4 us
    ppermute x4, starting transfers between devices, to_far(): lax.ppermute(send, DOM, [(i, i + 1) for i in odd] + [(i + 1, i) for i in...  9.32 us
    pallas_call x1, Pallas kernels, transfer(): pl.pallas_call(transfer_kernel, out_shape=(jax.ShapeDtypeStruct(coords.sh...  8.58 us
    ppermute x4, waiting for transfers between devices, to_far(): lax.ppermute(send, DOM, [(i, i + 1) for i in odd] + [(i + 1, i) for i in...  7.37 us
    pallas_call x3, Pallas kernels, step(): pl.pallas_call(step_kernel, out_shape=(shape, shape, pltpu.VMEM(far.shape...  5.28 us
    pallas_call x4, Pallas kernels, inside(): pl.pallas_call(inside_kernel, out_shape=(pltpu.VMEM(old.shape, F32), pltp...  3.14 us
  transfers between devices with their start and end apart: 10, of which 6 were waited for; matrix products, arithmetic and copies ran while one was open for 0% of the time, Pallas kernels for 5%

profile of v3, /device:TPU:1, one launch (start us, length us, event | category | flops | bytes accessed | tf_op | source)
XLA Modules:
  0.0 128.1 jit_solution(3658529850694979221)
XLA Ops:
  0.6 1.8 %slots.1 = (f32[128,128]{1,0:T(8,128)}, s32[1,512]{1,0:T(1,128)S(1)}) custom-call(s32[1,512]{1,0:T(1,128)} %bitcast.27, s32[1,512]{1,0:T(1,128)} %bitcast.28), custom_call_target="tpu_custom_call" | custom-call | tf_op jit(solution)/shard_map/slots/pallas_call | solution.py:89
  2.4 11.5 %all-to-all-start = ((f32[128,1,128]{2,1,0:T(1,128)}), f32[128,1,128]{2,1,0:T(1,128)S(1)}, u32[]{:S(2)}, u32[]{:S(2)}) async-start(f32[128,1,128]{2,1,0:T(1,128)} %bitcast.3), calls=%async_computation | async-start | bytes 131072 | tf_op jit(solution)/shard_map/all_to_all | solution.py:448
  13.9 2.7 %prepare.1 = (f32[4,6,128,128]{3,2,1,0:T(8,128)S(1)}, f32[128,128]{1,0:T(8,128)S(1)}, bf16[2,128,128]{2,1,0:T(8,128)(2,1)S(1)}, bf16[2,32,128]{2,1,0:T(8,128)(2,1)S(1)}, bf16[16,128]{1,0:T(8,128)(2,1)S(1)}) custom-call(s32[16]{0:T(128)} %halo_ref.1, s32[1]{0:T(128)} %bitcast.5.parity_ref, s32[2,128]{1,0:T(2,128)} %columns_ref.1, f32[96,128]{1,0:T(8,128)} %bitcast.26, ...), custom_call_target="tpu_custom_call" | custom-call | bytes 3145728 | tf_op jit(solution)/shard_map/prepare/pallas_call | solution.py:134
  16.6 6.7 %all-to-all-done = f32[128,1,128]{2,1,0:T(1,128)S(1)} async-done(((f32[128,1,128]{2,1,0:T(1,128)}), f32[128,1,128]{2,1,0:T(1,128)S(1)}, u32[]{:S(2)}, u32[]{:S(2)}) %all-to-all-start) | async-done | bytes 65568 | tf_op jit(solution)/shard_map/all_to_all | solution.py:448
  23.3 0.7 answer.1
  23.9 18.1 %all_to_all.32 = f32[128,8,128]{2,1,0:T(8,128)S(1)} all-to-all(f32[128,8,128]{2,1,0:T(8,128)S(1)} %bitcast.21), channel_id=1, replica_groups=mesh['dom_0'=4,'dom_1'=4,'dom_2'=4,'dom_3'=2] {'dom_0','dom_1','dom_2','..., dimensions={0} | all-to-all | bytes 1048576 | tf_op jit(solution)/shard_map/all_to_all | solution.py:448
  42.0 8.6 %transfer.1 = (f32[1024,128]{1,0:T(8,128)S(1)}, f32[3,96,96,128]{3,2,1,0:T(8,128)S(1)}, f32[96,96,128]{2,1,0:T(8,128)S(1)}) custom-call(s32[1,512]{1,0:T(1,128)S(1)} %get-tuple-element.39.slot_ref, f32[1024,128]{1,0:T(8,128)S(1)} %bitcast.18, f32[4,6,128,128]{3,2,1,0:T(8,128)S(1)} %get-tuple-element.43.turned_ref, f32[3,96,96,128]{3,2,1,0:T(8,128)} %blocks_ref.1, ...), custom_call_target="tpu_custom_call" | custom-call | tf_op jit(solution)/shard_map/transfer/pallas_call | solution.py:224
  50.6 18.1 %all_to_all.33 = f32[128,8,128]{2,1,0:T(8,128)S(1)} all-to-all(f32[128,8,128]{2,1,0:T(8,128)S(1)} %bitcast.20), channel_id=1, replica_groups=mesh['dom_0'=4,'dom_1'=4,'dom_2'=4,'dom_3'=2] {'dom_0','dom_1','dom_2','..., dimensions={0} | all-to-all | bytes 1048576 | tf_op jit(solution)/shard_map/all_to_all | solution.py:448
  68.7 1.1 start.1
  69.8 1.3 %collective-permute-start = (f32[16,128]{1,0:T(8,128)S(1)}, f32[16,128]{1,0:T(8,128)S(1)}, u32[]{:S(2)}, u32[]{:S(2)}) collective-permute-start(f32[16,128]{1,0:T(8,128)S(1)} %get-tuple-element.53), channel_id=1, source_target_pairs={{0,1},{1,0},{2,3},{3,2},{4,5},{5,4},{6,7},{7,6},{8,9},{9,8},{10,11... | collective-permute-start | bytes 24584 | tf_op jit(solution)/shard_map/ppermute | solution.py:439
  71.1 1.9 %collective-permute-start.1 = (f32[16,128]{1,0:T(8,128)S(1)}, f32[16,128]{1,0:T(8,128)S(1)}, u32[]{:S(2)}, u32[]{:S(2)}) collective-permute-start(f32[16,128]{1,0:T(8,128)S(1)} %get-tuple-element.53), channel_id=1, source_target_pairs={{1,2},{3,4},{5,6},{7,8},{9,10},{11,12},{13,14},{15,16},{17,18},{19... | collective-permute-start | bytes 24584 | tf_op jit(solution)/shard_map/ppermute | solution.py:444
  73.0 0.0 collective-permute-done.near_ref
  73.0 0.8 inside.4
  73.8 2.2 %collective-permute-done.1.far_ref = f32[16,128]{1,0:T(8,128)S(1)} collective-permute-done((f32[16,128]{1,0:T(8,128)S(1)}, f32[16,128]{1,0:T(8,128)S(1)}, u32[]{:S(2)}, u32[]{:S(2)}) %collective-permute-start.1) | collective-permute-done | bytes 8224 | tf_op jit(solution)/shard_map/ppermute | solution.py:444
  76.0 1.8 %step.3 = (f32[96,128]{1,0:T(8,128)S(1)}, f32[96,128]{1,0:T(8,128)S(1)}, f32[16,128]{1,0:T(8,128)S(1)}) custom-call(f32[3,96,96,128]{3,2,1,0:T(8,128)S(1)} %get-tuple-element.49.blocks_ref, f32[96,96,128]{2,1,0:T(8,128)S(1)} %get-tuple-element.46.precond_ref, bf16[2,32,128]{2,1,0:T(8,128)(2,1)S(1)} %get-tuple-element.50.outer_ref, ...), custom_call_target="tpu_custom_call" | custom-call | tf_op jit(solution)/shard_map/step/pallas_call | solution.py:336
  77.8 0.0 collective-permute-start.2
  77.8 2.2 %collective-permute-start.3 = (f32[16,128]{1,0:T(8,128)S(1)}, f32[16,128]{1,0:T(8,128)S(1)}, u32[]{:S(2)}, u32[]{:S(2)}) collective-permute-start(f32[16,128]{1,0:T(8,128)S(1)} %get-tuple-element.58), channel_id=1, source_target_pairs={{1,2},{3,4},{5,6},{7,8},{9,10},{11,12},{13,14},{15,16},{17,18},{19... | collective-permute-start | bytes 24584 | tf_op jit(solution)/shard_map/ppermute | solution.py:444
  80.1 0.0 collective-permute-done.2.near_ref
  80.1 0.8 inside.5
  80.9 2.0 %collective-permute-done.3.far_ref = f32[16,128]{1,0:T(8,128)S(1)} collective-permute-done((f32[16,128]{1,0:T(8,128)S(1)}, f32[16,128]{1,0:T(8,128)S(1)}, u32[]{:S(2)}, u32[]{:S(2)}) %collective-permute-start.3) | collective-permute-done | bytes 8224 | tf_op jit(solution)/shard_map/ppermute | solution.py:444
  82.8 1.8 %step.4 = (f32[96,128]{1,0:T(8,128)S(1)}, f32[96,128]{1,0:T(8,128)S(1)}, f32[16,128]{1,0:T(8,128)S(1)}) custom-call(f32[3,96,96,128]{3,2,1,0:T(8,128)S(1)} %get-tuple-element.49.blocks_ref, f32[96,96,128]{2,1,0:T(8,128)S(1)} %get-tuple-element.46.precond_ref, bf16[2,32,128]{2,1,0:T(8,128)(2,1)S(1)} %get-tuple-element.50.outer_ref, ...), custom_call_target="tpu_custom_call" | custom-call | tf_op jit(solution)/shard_map/step/pallas_call | solution.py:336
  84.6 0.0 collective-permute-start.4
  84.6 2.5 %collective-permute-start.5 = (f32[16,128]{1,0:T(8,128)S(1)}, f32[16,128]{1,0:T(8,128)S(1)}, u32[]{:S(2)}, u32[]{:S(2)}) collective-permute-start(f32[16,128]{1,0:T(8,128)S(1)} %get-tuple-element.63), channel_id=1, source_target_pairs={{1,2},{3,4},{5,6},{7,8},{9,10},{11,12},{13,14},{15,16},{17,18},{19... | collective-permute-start | bytes 24584 | tf_op jit(solution)/shard_map/ppermute | solution.py:444
  87.1 0.0 collective-permute-done.4.near_ref
  87.1 0.8 inside.6
  87.9 1.7 %collective-permute-done.5.far_ref = f32[16,128]{1,0:T(8,128)S(1)} collective-permute-done((f32[16,128]{1,0:T(8,128)S(1)}, f32[16,128]{1,0:T(8,128)S(1)}, u32[]{:S(2)}, u32[]{:S(2)}) %collective-permute-start.5) | collective-permute-done | bytes 8224 | tf_op jit(solution)/shard_map/ppermute | solution.py:444
  89.6 1.8 %step.5 = (f32[96,128]{1,0:T(8,128)S(1)}, f32[96,128]{1,0:T(8,128)S(1)}, f32[16,128]{1,0:T(8,128)S(1)}) custom-call(f32[3,96,96,128]{3,2,1,0:T(8,128)S(1)} %get-tuple-element.49.blocks_ref, f32[96,96,128]{2,1,0:T(8,128)S(1)} %get-tuple-element.46.precond_ref, bf16[2,32,128]{2,1,0:T(8,128)(2,1)S(1)} %get-tuple-element.50.outer_ref, ...), custom_call_target="tpu_custom_call" | custom-call | tf_op jit(solution)/shard_map/step/pallas_call | solution.py:336
  91.4 0.0 collective-permute-start.6
  91.4 2.7 %collective-permute-start.7 = (f32[16,128]{1,0:T(8,128)S(1)}, f32[16,128]{1,0:T(8,128)S(1)}, u32[]{:S(2)}, u32[]{:S(2)}) collective-permute-start(f32[16,128]{1,0:T(8,128)S(1)} %get-tuple-element.68), channel_id=1, source_target_pairs={{1,2},{3,4},{5,6},{7,8},{9,10},{11,12},{13,14},{15,16},{17,18},{19... | collective-permute-start | bytes 24584 | tf_op jit(solution)/shard_map/ppermute | solution.py:444
  94.1 0.0 collective-permute-done.6.near_ref
  94.1 0.8 inside.7
  94.9 1.5 %collective-permute-done.7.far_ref = f32[16,128]{1,0:T(8,128)S(1)} collective-permute-done((f32[16,128]{1,0:T(8,128)S(1)}, f32[16,128]{1,0:T(8,128)S(1)}, u32[]{:S(2)}, u32[]{:S(2)}) %collective-permute-start.7) | collective-permute-done | bytes 8224 | tf_op jit(solution)/shard_map/ppermute | solution.py:444
  96.4 2.0 %last.1 = (f32[96,128]{1,0:T(8,128)S(1)}, f32[128,128]{1,0:T(8,128)}) custom-call(f32[3,96,96,128]{3,2,1,0:T(8,128)S(1)} %get-tuple-element.49.blocks_ref, bf16[2,32,128]{2,1,0:T(8,128)(2,1)S(1)} %get-tuple-element.50.outer_ref, f32[96,128]{1,0:T(8,128)S(1)} %get-tuple-element.69.part_ref, f32[2,96,128]{2,1,0:T(8,128)S(1)} %get-tuple-element.70.taken_ref, ...), custom_call_target="tpu_custom_call" | custom-call | tf_op jit(solution)/shard_map/last/pallas_call | solution.py:362
  98.4 19.5 %all-to-all-start.3 = ((f32[128,1,128]{2,1,0:T(1,128)}), f32[128,1,128]{2,1,0:T(1,128)S(1)}, u32[]{:S(2)}, u32[]{:S(2)}) async-start(f32[128,1,128]{2,1,0:T(1,128)} %bitcast.14), calls=%async_computation.3 | async-start | bytes 131072 | tf_op jit(solution)/shard_map/all_to_all | solution.py:448
  117.8 0.6 copy.14
  118.5 8.8 %all-to-all-done.3 = f32[128,1,128]{2,1,0:T(1,128)S(1)} async-done(((f32[128,1,128]{2,1,0:T(1,128)}), f32[128,1,128]{2,1,0:T(1,128)S(1)}, u32[]{:S(2)}, u32[]{:S(2)}) %all-to-all-start.3) | async-done | bytes 65568 | tf_op jit(solution)/shard_map/all_to_all | solution.py:448
  127.2 0.9 finish.1
Async XLA Ops:
  2.4 20.9 %all-to-all-start = ((f32[128,1,128]{2,1,0:T(1,128)}), f32[128,1,128]{2,1,0:T(1,128)S(1)}, u32[]{:S(2)}, u32[]{:S(2)}) async-start(f32[128,1,128]{2,1,0:T(1,128)} %bitcast.3), calls=%async_computation | async-start | bytes 131072 | tf_op jit(solution)/shard_map/all_to_all | solution.py:448
  69.8 3.2 %collective-permute-start = (f32[16,128]{1,0:T(8,128)S(1)}, f32[16,128]{1,0:T(8,128)S(1)}, u32[]{:S(2)}, u32[]{:S(2)}) collective-permute-start(f32[16,128]{1,0:T(8,128)S(1)} %get-tuple-element.53), channel_id=1, source_target_pairs={{0,1},{1,0},{2,3},{3,2},{4,5},{5,4},{6,7},{7,6},{8,9},{9,8},{10,11... | collective-permute-start | bytes 24584 | tf_op jit(solution)/shard_map/ppermute | solution.py:439
  71.1 5.0 %collective-permute-start.1 = (f32[16,128]{1,0:T(8,128)S(1)}, f32[16,128]{1,0:T(8,128)S(1)}, u32[]{:S(2)}, u32[]{:S(2)}) collective-permute-start(f32[16,128]{1,0:T(8,128)S(1)} %get-tuple-element.53), channel_id=1, source_target_pairs={{1,2},{3,4},{5,6},{7,8},{9,10},{11,12},{13,14},{15,16},{17,18},{19... | collective-permute-start | bytes 24584 | tf_op jit(solution)/shard_map/ppermute | solution.py:444
  77.8 2.3 %collective-permute-start.2 = (f32[16,128]{1,0:T(8,128)S(1)}, f32[16,128]{1,0:T(8,128)S(1)}, u32[]{:S(2)}, u32[]{:S(2)}) collective-permute-start(f32[16,128]{1,0:T(8,128)S(1)} %get-tuple-element.58), channel_id=1, source_target_pairs={{0,1},{1,0},{2,3},{3,2},{4,5},{5,4},{6,7},{7,6},{8,9},{9,8},{10,11... | collective-permute-start | bytes 24584 | tf_op jit(solution)/shard_map/ppermute | solution.py:439
  77.8 5.0 %collective-permute-start.3 = (f32[16,128]{1,0:T(8,128)S(1)}, f32[16,128]{1,0:T(8,128)S(1)}, u32[]{:S(2)}, u32[]{:S(2)}) collective-permute-start(f32[16,128]{1,0:T(8,128)S(1)} %get-tuple-element.58), channel_id=1, source_target_pairs={{1,2},{3,4},{5,6},{7,8},{9,10},{11,12},{13,14},{15,16},{17,18},{19... | collective-permute-start | bytes 24584 | tf_op jit(solution)/shard_map/ppermute | solution.py:444
  84.6 2.5 %collective-permute-start.4 = (f32[16,128]{1,0:T(8,128)S(1)}, f32[16,128]{1,0:T(8,128)S(1)}, u32[]{:S(2)}, u32[]{:S(2)}) collective-permute-start(f32[16,128]{1,0:T(8,128)S(1)} %get-tuple-element.63), channel_id=1, source_target_pairs={{0,1},{1,0},{2,3},{3,2},{4,5},{5,4},{6,7},{7,6},{8,9},{9,8},{10,11... | collective-permute-start | bytes 24584 | tf_op jit(solution)/shard_map/ppermute | solution.py:439
  84.6 5.0 %collective-permute-start.5 = (f32[16,128]{1,0:T(8,128)S(1)}, f32[16,128]{1,0:T(8,128)S(1)}, u32[]{:S(2)}, u32[]{:S(2)}) collective-permute-start(f32[16,128]{1,0:T(8,128)S(1)} %get-tuple-element.63), channel_id=1, source_target_pairs={{1,2},{3,4},{5,6},{7,8},{9,10},{11,12},{13,14},{15,16},{17,18},{19... | collective-permute-start | bytes 24584 | tf_op jit(solution)/shard_map/ppermute | solution.py:444
  91.4 2.8 %collective-permute-start.6 = (f32[16,128]{1,0:T(8,128)S(1)}, f32[16,128]{1,0:T(8,128)S(1)}, u32[]{:S(2)}, u32[]{:S(2)}) collective-permute-start(f32[16,128]{1,0:T(8,128)S(1)} %get-tuple-element.68), channel_id=1, source_target_pairs={{0,1},{1,0},{2,3},{3,2},{4,5},{5,4},{6,7},{7,6},{8,9},{9,8},{10,11... | collective-permute-start | bytes 24584 | tf_op jit(solution)/shard_map/ppermute | solution.py:439
  91.4 5.0 %collective-permute-start.7 = (f32[16,128]{1,0:T(8,128)S(1)}, f32[16,128]{1,0:T(8,128)S(1)}, u32[]{:S(2)}, u32[]{:S(2)}) collective-permute-start(f32[16,128]{1,0:T(8,128)S(1)} %get-tuple-element.68), channel_id=1, source_target_pairs={{1,2},{3,4},{5,6},{7,8},{9,10},{11,12},{13,14},{15,16},{17,18},{19... | collective-permute-start | bytes 24584 | tf_op jit(solution)/shard_map/ppermute | solution.py:444
  98.4 28.8 %all-to-all-start.3 = ((f32[128,1,128]{2,1,0:T(1,128)}), f32[128,1,128]{2,1,0:T(1,128)S(1)}, u32[]{:S(2)}, u32[]{:S(2)}) async-start(f32[128,1,128]{2,1,0:T(1,128)} %bitcast.14), calls=%async_computation.3 | async-start | bytes 131072 | tf_op jit(solution)/shard_map/all_to_all | solution.py:448

commit v4 on v3

--- a/solution.py
+++ b/solution.py
@@ -1,12 +1,13 @@
+import functools
+
 import jax
 import jax.numpy as jnp
 from jax import lax
 from jax.experimental import pallas as pl
 from jax.experimental.pallas import tpu as pltpu
-from jax.sharding import Mesh
 from jax.sharding import PartitionSpec as P
 
-DOM = ("dom_0", "dom_1", "dom_2", "dom_3")
+DOM = "dom"
 SUPPORT = 0.9
 CAP = 8
 LANES = 128
@@ -98,7 +99,7 @@
 
 
 def prepare_kernel(
-    halo_ref, parity_ref, columns_ref, coords_ref, after_ref, fluid_ref, force_ref,
+    parts, halo_ref, place_ref, columns_ref, coords_ref, after_ref, fluid_ref, force_ref,
     turned_ref, coords_out, local_ref, outer_ref, listed_ref,
     points, sems,
 ):
@@ -109,11 +110,16 @@
     for copy in copies:
         copy.start()
     coords_out[...] = pad_rows(coords_ref[...], LANES)
-    flip = (1 - parity_ref[0]) * listed_ref.shape[0]
+    halo = listed_ref.shape[0]
+    core = place_ref[0] % 2
+    at_end = jnp.logical_or(place_ref[0] == 0, place_ref[0] == parts - 1)
+    held = jnp.where(at_end, halo, 2 * halo)
     for neighbor in range(2):
         column = columns_ref[pl.ds(neighbor, 1), :]
         local_ref[neighbor] = flag(iota((LANES, LANES), 0) == column)
-        outer_ref[neighbor] = flag(iota(outer_ref.shape[1:], 0) == ((column - LANES) ^ flip))
+        outer = (column - LANES) ^ ((1 - core) * halo)
+        outer = jnp.where(outer < held, outer, -1)
+        outer_ref[neighbor] = flag(iota(outer_ref.shape[1:], 0) == outer)
     rows = iota(listed_ref.shape, 0)
     column = jnp.zeros(listed_ref.shape, jnp.int32)
     for h in range(listed_ref.shape[0]):
@@ -128,11 +134,11 @@
                 turned_ref[group, 3 * kind + c] = points[kind, c, lanes, :].T * factor
 
 
-def prepare(halo_list, parity, columns, coords, after, fluid, force):
+def prepare(halo_list, place, columns, coords, after, fluid, force):
     count, nodes = fluid.shape[1:]
     halo = halo_list.shape[0]
     return pl.pallas_call(
-        prepare_kernel,
+        functools.partial(prepare_kernel, after.shape[0]),
         out_shape=(
             pltpu.VMEM((count // LANES, 6, nodes, LANES), F32),
             pltpu.VMEM((LANES, LANES), F32),
@@ -146,7 +152,7 @@
         compiler_params=limit(4),
         cost_estimate=pl.CostEstimate(flops=0, bytes_accessed=3 * MIB, transcendentals=0),
         name="prepare",
-    )(*in_hbm(halo_list, parity, columns, coords, after, fluid, force))
+    )(*in_hbm(halo_list, place, columns, coords, after, fluid, force))
 
 
 def answer_kernel(labels_ref, coords_ref, onehot_ref, out_ref):
@@ -440,8 +446,9 @@
 
 
 def to_far(send):
-    odd = range(1, lax.axis_size(DOM) - 1, 2)
-    return lax.ppermute(send, DOM, [(i, i + 1) for i in odd] + [(i + 1, i) for i in odd])
+    devices = lax.axis_size(DOM)
+    pairs = [(i, (i + 1) % devices) for i in range(1, devices, 2)]
+    return lax.ppermute(send, DOM, pairs + [(j, i) for i, j in pairs])
 
 
 def to_all(x):
@@ -452,13 +459,13 @@
     traction, fluid_coords, struct_coords, dest, target, blocks, columns, halo_list, precond
 ):
     parts = lax.axis_size(DOM)
-    parity = lax.axis_index("dom_3").astype(jnp.int32).reshape(1)
+    place = lax.axis_index(DOM).astype(jnp.int32).reshape(1)
     force = jnp.transpose(traction, (1, 0, 2))
     fluid = jnp.transpose(fluid_coords, (1, 0, 2))
     coords = struct_coords.reshape(-1, struct_coords.shape[2])
     wanted, slot = slots(dest.reshape(1, -1), target.reshape(1, -1), parts)
     turned, coords, local, outer, listed = prepare(
-        halo_list, parity, columns, coords, wanted, fluid, force
+        halo_list, place, columns, coords, wanted, fluid, force
     )
     onehot, answered = answer(to_all(wanted), coords)
     answered = to_all(answered.reshape(parts, CAP, LANES)).reshape(parts * CAP, LANES)
@@ -481,7 +488,6 @@
 
 
 def solution(mesh):
-    finer = Mesh(mesh.devices.reshape(4, 4, 4, 2), DOM)
     in_specs = (
         P(DOM, None, None),
         P(DOM, None, None),
@@ -495,5 +501,5 @@
     )
     out_specs = (P(None, DOM), P(None, DOM), P(None, DOM))
     return jax.shard_map(
-        on_device, mesh=finer, in_specs=in_specs, out_specs=out_specs, check_vma=False
+        on_device, mesh=mesh, in_specs=in_specs, out_specs=out_specs, check_vma=False
     )

time: 128 us -> 127 us (level)
  starting transfers between devices: 41.6 us -> 38.3 us
  waiting for transfers between devices: 22.8 us -> 24.7 us
    ppermute x4, starting transfers between devices: 1.38 us -> 17.9 us  [to_near(): return lax.ppermute(send, DOM, [(i, i ^ 1) for i in range(devices)])]
    all_to_all x2, starting transfers between devices: 30.9 us -> 20.4 us  [to_all(): return lax.all_to_all(x, DOM, split_axis=0, concat_axis=0, tiled=True)]
    ppermute x4, starting transfers between devices: 9.32 us -> 0.01 us  [to_far(): return lax.ppermute(send, DOM, pairs + [(j, i) for i, j in pairs])]
    ppermute x4, waiting for transfers between devices: 0.01 us -> 3.3 us  [to_near(): return lax.ppermute(send, DOM, [(i, i ^ 1) for i in range(devices)])]
    ppermute x4, waiting for transfers between devices: 7.37 us -> 5.86 us  [to_far(): return lax.ppermute(send, DOM, pairs + [(j, i) for i, j in pairs])]
  transfers between devices with their start and end apart: 10 -> 10, of which waited for: 6 -> 10; matrix products, arithmetic and copies ran while one was open for 0% -> 0% of each run, Pallas kernels for 5% -> 5%
where the time goes in v4:
time: 127 us
  starting transfers between devices  38.3 us (30%)
  blocking collectives  36.2 us (29%)
  Pallas kernels  26 us (20%)
  waiting for transfers between devices  24.7 us (19%)
    all_to_all x2, blocking collectives, to_all(): return lax.all_to_all(x, DOM, split_axis=0, concat_axis=0, tiled=True)  36.2 us
    all_to_all x2, starting transfers between devices, to_all(): return lax.all_to_all(x, DOM, split_axis=0, concat_axis=0, tiled=True)  20.4 us
    ppermute x4, starting transfers between devices, to_near(): return lax.ppermute(send, DOM, [(i, i ^ 1) for i in range(devices)])  17.9 us
    all_to_all x2, waiting for transfers between devices, to_all(): return lax.all_to_all(x, DOM, split_axis=0, concat_axis=0, tiled=True)  15.6 us
    pallas_call x1, Pallas kernels, transfer(): pl.pallas_call(transfer_kernel, out_shape=(jax.ShapeDtypeStruct(coords.sh...  8.58 us
    ppermute x4, waiting for transfers between devices, to_far(): return lax.ppermute(send, DOM, pairs + [(j, i) for i, j in pairs])  5.86 us
    pallas_call x3, Pallas kernels, step(): pl.pallas_call(step_kernel, out_shape=(shape, shape, pltpu.VMEM(far.shape...  5.28 us
    ppermute x4, waiting for transfers between devices, to_near(): return lax.ppermute(send, DOM, [(i, i ^ 1) for i in range(devices)])  3.3 us
  transfers between devices with their start and end apart: 10, of which 10 were waited for; matrix products, arithmetic and copies ran while one was open for 0% of the time, Pallas kernels for 5%

profile of v4, /device:TPU:1, one launch (start us, length us, event | category | flops | bytes accessed | tf_op | source)
XLA Modules:
  0.0 126.6 jit_solution(7316450169295067715)
XLA Ops:
  0.6 1.8 %slots.1 = (f32[128,128]{1,0:T(8,128)}, s32[1,512]{1,0:T(1,128)S(1)}) custom-call(s32[1,512]{1,0:T(1,128)} %bitcast.27, s32[1,512]{1,0:T(1,128)} %bitcast.28), custom_call_target="tpu_custom_call" | custom-call | tf_op jit(solution)/shard_map/slots/pallas_call | solution.py:90
  2.4 11.5 %all-to-all-start = ((f32[128,1,128]{2,1,0:T(1,128)}), f32[128,1,128]{2,1,0:T(1,128)S(1)}, u32[]{:S(2)}, u32[]{:S(2)}) async-start(f32[128,1,128]{2,1,0:T(1,128)} %bitcast.3), calls=%async_computation | async-start | bytes 131072 | tf_op jit(solution)/shard_map/all_to_all | solution.py:455
  13.9 2.7 %prepare.1 = (f32[4,6,128,128]{3,2,1,0:T(8,128)S(1)}, f32[128,128]{1,0:T(8,128)S(1)}, bf16[2,128,128]{2,1,0:T(8,128)(2,1)S(1)}, bf16[2,32,128]{2,1,0:T(8,128)(2,1)S(1)}, bf16[16,128]{1,0:T(8,128)(2,1)S(1)}) custom-call(s32[16]{0:T(128)} %halo_ref.1, s32[1]{0:T(128)} %bitcast.5.place_ref, s32[2,128]{1,0:T(2,128)} %columns_ref.1, f32[96,128]{1,0:T(8,128)} %bitcast.26, ...), custom_call_target="tpu_custom_call" | custom-call | bytes 3145728 | tf_op jit(solution)/shard_map/prepare/pallas_call | solution.py:140
  16.6 6.7 %all-to-all-done = f32[128,1,128]{2,1,0:T(1,128)S(1)} async-done(((f32[128,1,128]{2,1,0:T(1,128)}), f32[128,1,128]{2,1,0:T(1,128)S(1)}, u32[]{:S(2)}, u32[]{:S(2)}) %all-to-all-start) | async-done | bytes 65568 | tf_op jit(solution)/shard_map/all_to_all | solution.py:455
  23.3 0.7 answer.1
  23.9 18.1 %all_to_all.32 = f32[128,8,128]{2,1,0:T(8,128)S(1)} all-to-all(f32[128,8,128]{2,1,0:T(8,128)S(1)} %bitcast.21), channel_id=1, replica_groups=mesh['dom'=128] {'dom'}, dimensions={0} | all-to-all | bytes 1048576 | tf_op jit(solution)/shard_map/all_to_all | solution.py:455
  42.0 8.6 %transfer.1 = (f32[1024,128]{1,0:T(8,128)S(1)}, f32[3,96,96,128]{3,2,1,0:T(8,128)S(1)}, f32[96,96,128]{2,1,0:T(8,128)S(1)}) custom-call(s32[1,512]{1,0:T(1,128)S(1)} %get-tuple-element.39.slot_ref, f32[1024,128]{1,0:T(8,128)S(1)} %bitcast.18, f32[4,6,128,128]{3,2,1,0:T(8,128)S(1)} %get-tuple-element.43.turned_ref, f32[3,96,96,128]{3,2,1,0:T(8,128)} %blocks_ref.1, ...), custom_call_target="tpu_custom_call" | custom-call | tf_op jit(solution)/shard_map/transfer/pallas_call | solution.py:230
  50.6 18.1 %all_to_all.33 = f32[128,8,128]{2,1,0:T(8,128)S(1)} all-to-all(f32[128,8,128]{2,1,0:T(8,128)S(1)} %bitcast.20), channel_id=1, replica_groups=mesh['dom'=128] {'dom'}, dimensions={0} | all-to-all | bytes 1048576 | tf_op jit(solution)/shard_map/all_to_all | solution.py:455
  68.7 1.1 start.1
  69.8 1.3 %collective-permute-start = (f32[16,128]{1,0:T(8,128)S(1)}, f32[16,128]{1,0:T(8,128)S(1)}, u32[]{:S(2)}, u32[]{:S(2)}) collective-permute-start(f32[16,128]{1,0:T(8,128)S(1)} %get-tuple-element.53), channel_id=1, source_target_pairs={{0,1},{1,0},{2,3},{3,2},{4,5},{5,4},{6,7},{7,6},{8,9},{9,8},{10,11... | collective-permute-start | bytes 24584 | tf_op jit(solution)/shard_map/ppermute | solution.py:445
  71.1 0.0 collective-permute-start.1
  71.1 0.8 collective-permute-done.near_ref
  71.9 0.8 inside.4
  72.7 1.5 %collective-permute-done.1.far_ref = f32[16,128]{1,0:T(8,128)S(1)} collective-permute-done((f32[16,128]{1,0:T(8,128)S(1)}, f32[16,128]{1,0:T(8,128)S(1)}, u32[]{:S(2)}, u32[]{:S(2)}) %collective-permute-start.1) | collective-permute-done | bytes 8224 | tf_op jit(solution)/shard_map/ppermute | solution.py:451
  74.1 1.8 %step.3 = (f32[96,128]{1,0:T(8,128)S(1)}, f32[96,128]{1,0:T(8,128)S(1)}, f32[16,128]{1,0:T(8,128)S(1)}) custom-call(f32[3,96,96,128]{3,2,1,0:T(8,128)S(1)} %get-tuple-element.49.blocks_ref, f32[96,96,128]{2,1,0:T(8,128)S(1)} %get-tuple-element.46.precond_ref, bf16[2,32,128]{2,1,0:T(8,128)(2,1)S(1)} %get-tuple-element.50.outer_ref, ...), custom_call_target="tpu_custom_call" | custom-call | tf_op jit(solution)/shard_map/step/pallas_call | solution.py:342
  75.9 5.5 %collective-permute-start.2 = (f32[16,128]{1,0:T(8,128)S(1)}, f32[16,128]{1,0:T(8,128)S(1)}, u32[]{:S(2)}, u32[]{:S(2)}) collective-permute-start(f32[16,128]{1,0:T(8,128)S(1)} %get-tuple-element.58), channel_id=1, source_target_pairs={{0,1},{1,0},{2,3},{3,2},{4,5},{5,4},{6,7},{7,6},{8,9},{9,8},{10,11... | collective-permute-start | bytes 24584 | tf_op jit(solution)/shard_map/ppermute | solution.py:445
  81.5 0.0 collective-permute-start.3
  81.5 0.8 collective-permute-done.2.near_ref
  82.3 0.8 inside.5
  83.1 1.5 %collective-permute-done.3.far_ref = f32[16,128]{1,0:T(8,128)S(1)} collective-permute-done((f32[16,128]{1,0:T(8,128)S(1)}, f32[16,128]{1,0:T(8,128)S(1)}, u32[]{:S(2)}, u32[]{:S(2)}) %collective-permute-start.3) | collective-permute-done | bytes 8224 | tf_op jit(solution)/shard_map/ppermute | solution.py:451
  84.5 1.8 %step.4 = (f32[96,128]{1,0:T(8,128)S(1)}, f32[96,128]{1,0:T(8,128)S(1)}, f32[16,128]{1,0:T(8,128)S(1)}) custom-call(f32[3,96,96,128]{3,2,1,0:T(8,128)S(1)} %get-tuple-element.49.blocks_ref, f32[96,96,128]{2,1,0:T(8,128)S(1)} %get-tuple-element.46.precond_ref, bf16[2,32,128]{2,1,0:T(8,128)(2,1)S(1)} %get-tuple-element.50.outer_ref, ...), custom_call_target="tpu_custom_call" | custom-call | tf_op jit(solution)/shard_map/step/pallas_call | solution.py:342
  86.3 5.5 %collective-permute-start.4 = (f32[16,128]{1,0:T(8,128)S(1)}, f32[16,128]{1,0:T(8,128)S(1)}, u32[]{:S(2)}, u32[]{:S(2)}) collective-permute-start(f32[16,128]{1,0:T(8,128)S(1)} %get-tuple-element.63), channel_id=1, source_target_pairs={{0,1},{1,0},{2,3},{3,2},{4,5},{5,4},{6,7},{7,6},{8,9},{9,8},{10,11... | collective-permute-start | bytes 24584 | tf_op jit(solution)/shard_map/ppermute | solution.py:445
  91.8 0.0 collective-permute-start.5
  91.8 0.8 collective-permute-done.4.near_ref
  92.7 0.8 inside.6
  93.4 1.5 %collective-permute-done.5.far_ref = f32[16,128]{1,0:T(8,128)S(1)} collective-permute-done((f32[16,128]{1,0:T(8,128)S(1)}, f32[16,128]{1,0:T(8,128)S(1)}, u32[]{:S(2)}, u32[]{:S(2)}) %collective-permute-start.5) | collective-permute-done | bytes 8224 | tf_op jit(solution)/shard_map/ppermute | solution.py:451
  94.9 1.8 %step.5 = (f32[96,128]{1,0:T(8,128)S(1)}, f32[96,128]{1,0:T(8,128)S(1)}, f32[16,128]{1,0:T(8,128)S(1)}) custom-call(f32[3,96,96,128]{3,2,1,0:T(8,128)S(1)} %get-tuple-element.49.blocks_ref, f32[96,96,128]{2,1,0:T(8,128)S(1)} %get-tuple-element.46.precond_ref, bf16[2,32,128]{2,1,0:T(8,128)(2,1)S(1)} %get-tuple-element.50.outer_ref, ...), custom_call_target="tpu_custom_call" | custom-call | tf_op jit(solution)/shard_map/step/pallas_call | solution.py:342
  96.7 5.5 %collective-permute-start.6 = (f32[16,128]{1,0:T(8,128)S(1)}, f32[16,128]{1,0:T(8,128)S(1)}, u32[]{:S(2)}, u32[]{:S(2)}) collective-permute-start(f32[16,128]{1,0:T(8,128)S(1)} %get-tuple-element.68), channel_id=1, source_target_pairs={{0,1},{1,0},{2,3},{3,2},{4,5},{5,4},{6,7},{7,6},{8,9},{9,8},{10,11... | collective-permute-start | bytes 24584 | tf_op jit(solution)/shard_map/ppermute | solution.py:445
  102.2 0.0 collective-permute-start.7
  102.2 0.8 collective-permute-done.6.near_ref
  103.0 0.8 inside.7
  103.8 1.5 %collective-permute-done.7.far_ref = f32[16,128]{1,0:T(8,128)S(1)} collective-permute-done((f32[16,128]{1,0:T(8,128)S(1)}, f32[16,128]{1,0:T(8,128)S(1)}, u32[]{:S(2)}, u32[]{:S(2)}) %collective-permute-start.7) | collective-permute-done | bytes 8224 | tf_op jit(solution)/shard_map/ppermute | solution.py:451
  105.3 2.0 %last.1 = (f32[96,128]{1,0:T(8,128)S(1)}, f32[128,128]{1,0:T(8,128)}) custom-call(f32[3,96,96,128]{3,2,1,0:T(8,128)S(1)} %get-tuple-element.49.blocks_ref, bf16[2,32,128]{2,1,0:T(8,128)(2,1)S(1)} %get-tuple-element.50.outer_ref, f32[96,128]{1,0:T(8,128)S(1)} %get-tuple-element.69.part_ref, f32[2,96,128]{2,1,0:T(8,128)S(1)} %get-tuple-element.70.taken_ref, ...), custom_call_target="tpu_custom_call" | custom-call | tf_op jit(solution)/shard_map/last/pallas_call | solution.py:368
  107.3 8.9 %all-to-all-start.3 = ((f32[128,1,128]{2,1,0:T(1,128)}), f32[128,1,128]{2,1,0:T(1,128)S(1)}, u32[]{:S(2)}, u32[]{:S(2)}) async-start(f32[128,1,128]{2,1,0:T(1,128)} %bitcast.14), calls=%async_computation.3 | async-start | bytes 131072 | tf_op jit(solution)/shard_map/all_to_all | solution.py:455
  116.2 0.6 copy.14
  116.8 8.9 %all-to-all-done.3 = f32[128,1,128]{2,1,0:T(1,128)S(1)} async-done(((f32[128,1,128]{2,1,0:T(1,128)}), f32[128,1,128]{2,1,0:T(1,128)S(1)}, u32[]{:S(2)}, u32[]{:S(2)}) %all-to-all-start.3) | async-done | bytes 65568 | tf_op jit(solution)/shard_map/all_to_all | solution.py:455
  125.7 0.9 finish.1
Async XLA Ops:
  2.4 20.9 %all-to-all-start = ((f32[128,1,128]{2,1,0:T(1,128)}), f32[128,1,128]{2,1,0:T(1,128)S(1)}, u32[]{:S(2)}, u32[]{:S(2)}) async-start(f32[128,1,128]{2,1,0:T(1,128)} %bitcast.3), calls=%async_computation | async-start | bytes 131072 | tf_op jit(solution)/shard_map/all_to_all | solution.py:455
  69.8 2.1 %collective-permute-start = (f32[16,128]{1,0:T(8,128)S(1)}, f32[16,128]{1,0:T(8,128)S(1)}, u32[]{:S(2)}, u32[]{:S(2)}) collective-permute-start(f32[16,128]{1,0:T(8,128)S(1)} %get-tuple-element.53), channel_id=1, source_target_pairs={{0,1},{1,0},{2,3},{3,2},{4,5},{5,4},{6,7},{7,6},{8,9},{9,8},{10,11... | collective-permute-start | bytes 24584 | tf_op jit(solution)/shard_map/ppermute | solution.py:445
  71.1 3.1 %collective-permute-start.1 = (f32[16,128]{1,0:T(8,128)S(1)}, f32[16,128]{1,0:T(8,128)S(1)}, u32[]{:S(2)}, u32[]{:S(2)}) collective-permute-start(f32[16,128]{1,0:T(8,128)S(1)} %get-tuple-element.53), channel_id=1, source_target_pairs={{1,2},{3,4},{5,6},{7,8},{9,10},{11,12},{13,14},{15,16},{17,18},{19... | collective-permute-start | bytes 24584 | tf_op jit(solution)/shard_map/ppermute | solution.py:451
  75.9 6.4 %collective-permute-start.2 = (f32[16,128]{1,0:T(8,128)S(1)}, f32[16,128]{1,0:T(8,128)S(1)}, u32[]{:S(2)}, u32[]{:S(2)}) collective-permute-start(f32[16,128]{1,0:T(8,128)S(1)} %get-tuple-element.58), channel_id=1, source_target_pairs={{0,1},{1,0},{2,3},{3,2},{4,5},{5,4},{6,7},{7,6},{8,9},{9,8},{10,11... | collective-permute-start | bytes 24584 | tf_op jit(solution)/shard_map/ppermute | solution.py:445
  81.5 3.1 %collective-permute-start.3 = (f32[16,128]{1,0:T(8,128)S(1)}, f32[16,128]{1,0:T(8,128)S(1)}, u32[]{:S(2)}, u32[]{:S(2)}) collective-permute-start(f32[16,128]{1,0:T(8,128)S(1)} %get-tuple-element.58), channel_id=1, source_target_pairs={{1,2},{3,4},{5,6},{7,8},{9,10},{11,12},{13,14},{15,16},{17,18},{19... | collective-permute-start | bytes 24584 | tf_op jit(solution)/shard_map/ppermute | solution.py:451
  86.3 6.4 %collective-permute-start.4 = (f32[16,128]{1,0:T(8,128)S(1)}, f32[16,128]{1,0:T(8,128)S(1)}, u32[]{:S(2)}, u32[]{:S(2)}) collective-permute-start(f32[16,128]{1,0:T(8,128)S(1)} %get-tuple-element.63), channel_id=1, source_target_pairs={{0,1},{1,0},{2,3},{3,2},{4,5},{5,4},{6,7},{7,6},{8,9},{9,8},{10,11... | collective-permute-start | bytes 24584 | tf_op jit(solution)/shard_map/ppermute | solution.py:445
  91.8 3.1 %collective-permute-start.5 = (f32[16,128]{1,0:T(8,128)S(1)}, f32[16,128]{1,0:T(8,128)S(1)}, u32[]{:S(2)}, u32[]{:S(2)}) collective-permute-start(f32[16,128]{1,0:T(8,128)S(1)} %get-tuple-element.63), channel_id=1, source_target_pairs={{1,2},{3,4},{5,6},{7,8},{9,10},{11,12},{13,14},{15,16},{17,18},{19... | collective-permute-start | bytes 24584 | tf_op jit(solution)/shard_map/ppermute | solution.py:451
  96.7 6.4 %collective-permute-start.6 = (f32[16,128]{1,0:T(8,128)S(1)}, f32[16,128]{1,0:T(8,128)S(1)}, u32[]{:S(2)}, u32[]{:S(2)}) collective-permute-start(f32[16,128]{1,0:T(8,128)S(1)} %get-tuple-element.68), channel_id=1, source_target_pairs={{0,1},{1,0},{2,3},{3,2},{4,5},{5,4},{6,7},{7,6},{8,9},{9,8},{10,11... | collective-permute-start | bytes 24584 | tf_op jit(solution)/shard_map/ppermute | solution.py:445
  102.2 3.1 %collective-permute-start.7 = (f32[16,128]{1,0:T(8,128)S(1)}, f32[16,128]{1,0:T(8,128)S(1)}, u32[]{:S(2)}, u32[]{:S(2)}) collective-permute-start(f32[16,128]{1,0:T(8,128)S(1)} %get-tuple-element.68), channel_id=1, source_target_pairs={{1,2},{3,4},{5,6},{7,8},{9,10},{11,12},{13,14},{15,16},{17,18},{19... | collective-permute-start | bytes 24584 | tf_op jit(solution)/shard_map/ppermute | solution.py:451
  107.3 18.4 %all-to-all-start.3 = ((f32[128,1,128]{2,1,0:T(1,128)}), f32[128,1,128]{2,1,0:T(1,128)S(1)}, u32[]{:S(2)}, u32[]{:S(2)}) async-start(f32[128,1,128]{2,1,0:T(1,128)} %bitcast.14), calls=%async_computation.3 | async-start | bytes 131072 | tf_op jit(solution)/shard_map/all_to_all | solution.py:455

commit v5 on v4

--- a/solution.py
+++ b/solution.py
@@ -57,12 +57,19 @@
     return lax.dot_general(a, b, dims, preferred_element_type=F32)
 
 
+def three(product, size, axis):
+    parts = [lax.slice_in_dim(product, k * size, (k + 1) * size, axis=axis) for k in range(3)]
+    return parts[0] + (parts[1] + parts[2])
+
+
 def pick(x, onehot, dims):
-    return sum(dot(part, onehot, dims) for part in reversed(split3(x)))
-
-
-def pick_from(onehot, x, dims):
-    return sum(dot(onehot, part, dims) for part in reversed(split3(x)))
+    free = 0 if dims == NN else 1
+    stacked = jnp.concatenate(split3(x), axis=free)
+    return three(dot(stacked, onehot, dims), x.shape[free], 0)
+
+
+def pick_from(onehot, x):
+    return three(dot(onehot, jnp.concatenate(split3(x), axis=0), NT), x.shape[0], 1)
 
 
 def pad_rows(x, rows):
@@ -129,9 +136,13 @@
         copy.wait()
     for group in range(points.shape[2] // LANES):
         lanes = pl.ds(group * LANES, LANES)
-        for kind, factor in enumerate((1.0 / SUPPORT, 4.0)):
-            for c in range(3):
-                turned_ref[group, 3 * kind + c] = points[kind, c, lanes, :].T * factor
+        length = jnp.zeros(turned_ref.shape[2:], F32)
+        for c in range(3):
+            position = points[0, c, lanes, :].T * (1.0 / SUPPORT)
+            length = length + position * position
+            turned_ref[group, c] = position * -2.0
+            turned_ref[group, 3 + c] = points[1, c, lanes, :].T * 4.0
+        turned_ref[group, 6] = length
 
 
 def prepare(halo_list, place, columns, coords, after, fluid, force):
@@ -140,7 +151,7 @@
     return pl.pallas_call(
         functools.partial(prepare_kernel, after.shape[0]),
         out_shape=(
-            pltpu.VMEM((count // LANES, 6, nodes, LANES), F32),
+            pltpu.VMEM((count // LANES, 7, nodes, LANES), F32),
             pltpu.VMEM((LANES, LANES), F32),
             pltpu.VMEM((2, LANES, LANES), BF16),
             pltpu.VMEM((2, 2 * halo, LANES), BF16),
@@ -165,7 +176,7 @@
     label = dot(own_label, jnp.ones((LANES, LANES), BF16), NN)
     onehot = flag(label == (iota((rows, LANES), 1) + 1).astype(F32))
     onehot_ref[...] = onehot
-    out_ref[...] = pick_from(onehot, coords_ref[...], NT)
+    out_ref[...] = pick_from(onehot, coords_ref[...])
 
 
 def answer(labels, coords):
@@ -200,13 +211,15 @@
     for group in range(count // LANES):
         lanes = pl.ds(group * LANES, LANES)
         where = [struct[pl.ds(c * 32, 32), lanes] for c in range(3)]
+        length = where[0] * where[0] + where[1] * where[1] + where[2] * where[2]
 
         def body(step, sums):
             sums = list(sums)
             for k in range(8):
                 n = pl.ds(step * 8 + k, 1)
-                apart = [where[c] - turned_ref[group, c, n, :] for c in range(3)]
-                square = apart[0] * apart[0] + apart[1] * apart[1] + apart[2] * apart[2]
+                square = length + turned_ref[group, 6, n, :]
+                for c in range(3):
+                    square = square + where[c] * turned_ref[group, c, n, :]
                 square = jnp.maximum(square, 1e-30)
                 left = jnp.maximum(1.0 - square * lax.rsqrt(square), 0.0)
                 twice = left * left
@@ -220,7 +233,7 @@
         for c in range(3):
             mapped[pl.ds(c * 32, 32), lanes] = sums[c]
     mapped[pl.ds(96, 32), :] = jnp.zeros((32, count), F32)
-    out_ref[...] = pick_from(chosen, mapped[...], NT)
+    out_ref[...] = pick_from(chosen, mapped[...])
     for copy in tables:
         copy.wait()
 
@@ -267,7 +280,7 @@
         out_ref[pl.ds(row, 1), :] = value
 
     times([precond_ref], [vector], put)
-    send_ref[...] = pick_from(listed_ref[...], pad_rows(out_ref[...], LANES), NT)
+    send_ref[...] = pick_from(listed_ref[...], pad_rows(out_ref[...], LANES))
 
 
 def start_kernel(mapped_ref, onehot_ref, precond_ref, listed_ref, load_ref, pre_ref, send_ref):
@@ -361,7 +374,7 @@
     sums = [jnp.sum(vectors[i] * vectors[j], axis=0, keepdims=True) for i, j in PAIRS]
     sums.append(jnp.zeros((LANES - len(sums), LANES), F32))
     ones = jnp.ones((sums_ref.shape[0], LANES), BF16)
-    sums_ref[...] = pick_from(ones, jnp.concatenate(sums, axis=0), NT)
+    sums_ref[...] = pick_from(ones, jnp.concatenate(sums, axis=0))
 
 
 def last(blocks, outer, part, taken, far, basis, parts):
@@ -445,9 +458,9 @@
     return lax.ppermute(send, DOM, [(i, i ^ 1) for i in range(devices)])
 
 
-def to_far(send):
+def to_far(send, closed):
     devices = lax.axis_size(DOM)
-    pairs = [(i, (i + 1) % devices) for i in range(1, devices, 2)]
+    pairs = [(i, (i + 1) % devices) for i in range(1, devices if closed else devices - 1, 2)]
     return lax.ppermute(send, DOM, pairs + [(j, i) for i, j in pairs])
 
 
@@ -474,7 +487,7 @@
     load, pre, send = start(mapped, onehot, precond, listed)
     basis, pres = [load], [pre]
     for j in range(STEPS):
-        far = to_far(send)
+        far = to_far(send, j > 0)
         near = to_near(send)
         part, taken = inside(blocks, local, outer, basis[-1], pres[-1], near)
         if j < STEPS - 1:

time: 127 us -> 123 us (0.969)
  starting transfers between devices: 38.3 us -> 35.4 us
    ppermute x4, starting transfers between devices: 17.9 us -> 12.7 us  [to_near(): return lax.ppermute(send, DOM, [(i, i ^ 1) for i in range(devices)])]
    ppermute x4, starting transfers between devices: 0.01 us -> 2.22 us  [to_far(): return lax.ppermute(send, DOM, pairs + [(j, i) for i, j in pairs])]
  transfers between devices with their start and end apart: 10 -> 10, of which waited for: 10 -> 9; matrix products, arithmetic and copies ran while one was open for 0% -> 1% of each run, Pallas kernels for 5% -> 5%
where the time goes in v5:
time: 123 us
  blocking collectives  36.2 us (29%)
  starting transfers between devices  35.4 us (29%)
  Pallas kernels  25.5 us (21%)
  waiting for transfers between devices  24.5 us (20%)
    all_to_all x2, blocking collectives, to_all(): return lax.all_to_all(x, DOM, split_axis=0, concat_axis=0, tiled=True)  36.2 us
    all_to_all x2, starting transfers between devices, to_all(): return lax.all_to_all(x, DOM, split_axis=0, concat_axis=0, tiled=True)  20.4 us
    all_to_all x2, waiting for transfers between devices, to_all(): return lax.all_to_all(x, DOM, split_axis=0, concat_axis=0, tiled=True)  15.6 us
    ppermute x4, starting transfers between devices, to_near(): return lax.ppermute(send, DOM, [(i, i ^ 1) for i in range(devices)])  12.7 us
    pallas_call x1, Pallas kernels, transfer(): pl.pallas_call(transfer_kernel, out_shape=(jax.ShapeDtypeStruct(coords.sh...  8.05 us
    ppermute x4, waiting for transfers between devices, to_far(): return lax.ppermute(send, DOM, pairs + [(j, i) for i, j in pairs])  6.35 us
    pallas_call x3, Pallas kernels, step(): pl.pallas_call(step_kernel, out_shape=(shape, shape, pltpu.VMEM(far.shape...  5.3 us
    pallas_call x4, Pallas kernels, inside(): pl.pallas_call(inside_kernel, out_shape=(pltpu.VMEM(old.shape, F32), pltp...  3.11 us
  transfers between devices with their start and end apart: 10, of which 9 were waited for; matrix products, arithmetic and copies ran while one was open for 1% of the time, Pallas kernels for 5%

profile of v5, /device:TPU:1, one launch (start us, length us, event | category | flops | bytes accessed | tf_op | source)
XLA Modules:
  0.0 122.8 jit_solution(13926282779894467477)
XLA Ops:
  0.6 1.8 %slots.1 = (f32[128,128]{1,0:T(8,128)}, s32[1,512]{1,0:T(1,128)S(1)}) custom-call(s32[1,512]{1,0:T(1,128)} %bitcast.27, s32[1,512]{1,0:T(1,128)} %bitcast.28), custom_call_target="tpu_custom_call" | custom-call | tf_op jit(solution)/shard_map/slots/pallas_call | solution.py:97
  2.4 11.5 %all-to-all-start = ((f32[128,1,128]{2,1,0:T(1,128)}), f32[128,1,128]{2,1,0:T(1,128)S(1)}, u32[]{:S(2)}, u32[]{:S(2)}) async-start(f32[128,1,128]{2,1,0:T(1,128)} %bitcast.3), calls=%async_computation | async-start | bytes 131072 | tf_op jit(solution)/shard_map/all_to_all | solution.py:468
  13.9 2.7 %prepare.1 = (f32[4,7,128,128]{3,2,1,0:T(8,128)S(1)}, f32[128,128]{1,0:T(8,128)S(1)}, bf16[2,128,128]{2,1,0:T(8,128)(2,1)S(1)}, bf16[2,32,128]{2,1,0:T(8,128)(2,1)S(1)}, bf16[16,128]{1,0:T(8,128)(2,1)S(1)}) custom-call(s32[16]{0:T(128)} %halo_ref.1, s32[1]{0:T(128)} %bitcast.5.place_ref, s32[2,128]{1,0:T(2,128)} %columns_ref.1, f32[96,128]{1,0:T(8,128)} %bitcast.26, ...), custom_call_target="tpu_custom_call" | custom-call | bytes 3145728 | tf_op jit(solution)/shard_map/prepare/pallas_call | solution.py:151
  16.6 6.7 %all-to-all-done = f32[128,1,128]{2,1,0:T(1,128)S(1)} async-done(((f32[128,1,128]{2,1,0:T(1,128)}), f32[128,1,128]{2,1,0:T(1,128)S(1)}, u32[]{:S(2)}, u32[]{:S(2)}) %all-to-all-start) | async-done | bytes 65568 | tf_op jit(solution)/shard_map/all_to_all | solution.py:468
  23.3 0.7 answer.1
  23.9 18.1 %all_to_all.32 = f32[128,8,128]{2,1,0:T(8,128)S(1)} all-to-all(f32[128,8,128]{2,1,0:T(8,128)S(1)} %bitcast.21), channel_id=1, replica_groups=mesh['dom'=128] {'dom'}, dimensions={0} | all-to-all | bytes 1048576 | tf_op jit(solution)/shard_map/all_to_all | solution.py:468
  42.0 8.1 %transfer.1 = (f32[1024,128]{1,0:T(8,128)S(1)}, f32[3,96,96,128]{3,2,1,0:T(8,128)S(1)}, f32[96,96,128]{2,1,0:T(8,128)S(1)}) custom-call(s32[1,512]{1,0:T(1,128)S(1)} %get-tuple-element.39.slot_ref, f32[1024,128]{1,0:T(8,128)S(1)} %bitcast.18, f32[4,7,128,128]{3,2,1,0:T(8,128)S(1)} %get-tuple-element.43.turned_ref, f32[3,96,96,128]{3,2,1,0:T(8,128)} %blocks_ref.1, ...), custom_call_target="tpu_custom_call" | custom-call | tf_op jit(solution)/shard_map/transfer/pallas_call | solution.py:243
  50.1 18.1 %all_to_all.33 = f32[128,8,128]{2,1,0:T(8,128)S(1)} all-to-all(f32[128,8,128]{2,1,0:T(8,128)S(1)} %bitcast.20), channel_id=1, replica_groups=mesh['dom'=128] {'dom'}, dimensions={0} | all-to-all | bytes 1048576 | tf_op jit(solution)/shard_map/all_to_all | solution.py:468
  68.2 1.1 start.1
  69.2 1.3 %collective-permute-start = (f32[16,128]{1,0:T(8,128)S(1)}, f32[16,128]{1,0:T(8,128)S(1)}, u32[]{:S(2)}, u32[]{:S(2)}) collective-permute-start(f32[16,128]{1,0:T(8,128)S(1)} %get-tuple-element.53), channel_id=1, source_target_pairs={{0,1},{1,0},{2,3},{3,2},{4,5},{5,4},{6,7},{7,6},{8,9},{9,8},{10,11... | collective-permute-start | bytes 24584 | tf_op jit(solution)/shard_map/ppermute | solution.py:458
  70.6 1.9 %collective-permute-start.1 = (f32[16,128]{1,0:T(8,128)S(1)}, f32[16,128]{1,0:T(8,128)S(1)}, u32[]{:S(2)}, u32[]{:S(2)}) collective-permute-start(f32[16,128]{1,0:T(8,128)S(1)} %get-tuple-element.53), channel_id=1, source_target_pairs={{1,2},{3,4},{5,6},{7,8},{9,10},{11,12},{13,14},{15,16},{17,18},{19... | collective-permute-start | bytes 24584 | tf_op jit(solution)/shard_map/ppermute | solution.py:464
  72.5 0.0 collective-permute-done.near_ref
  72.5 0.8 inside.4
  73.3 2.2 %collective-permute-done.1.far_ref = f32[16,128]{1,0:T(8,128)S(1)} collective-permute-done((f32[16,128]{1,0:T(8,128)S(1)}, f32[16,128]{1,0:T(8,128)S(1)}, u32[]{:S(2)}, u32[]{:S(2)}) %collective-permute-start.1) | collective-permute-done | bytes 8224 | tf_op jit(solution)/shard_map/ppermute | solution.py:464
  75.5 1.8 %step.3 = (f32[96,128]{1,0:T(8,128)S(1)}, f32[96,128]{1,0:T(8,128)S(1)}, f32[16,128]{1,0:T(8,128)S(1)}) custom-call(f32[3,96,96,128]{3,2,1,0:T(8,128)S(1)} %get-tuple-element.49.blocks_ref, f32[96,96,128]{2,1,0:T(8,128)S(1)} %get-tuple-element.46.precond_ref, bf16[2,32,128]{2,1,0:T(8,128)(2,1)S(1)} %get-tuple-element.50.outer_ref, ...), custom_call_target="tpu_custom_call" | custom-call | tf_op jit(solution)/shard_map/step/pallas_call | solution.py:355
  77.3 0.0 collective-permute-start.2
  77.3 0.3 collective-permute-start.3
  77.6 0.9 collective-permute-done.2.near_ref
  78.5 0.8 inside.5
  79.3 1.2 collective-permute-done.3.far_ref
  80.4 1.8 %step.4 = (f32[96,128]{1,0:T(8,128)S(1)}, f32[96,128]{1,0:T(8,128)S(1)}, f32[16,128]{1,0:T(8,128)S(1)}) custom-call(f32[3,96,96,128]{3,2,1,0:T(8,128)S(1)} %get-tuple-element.49.blocks_ref, f32[96,96,128]{2,1,0:T(8,128)S(1)} %get-tuple-element.46.precond_ref, bf16[2,32,128]{2,1,0:T(8,128)(2,1)S(1)} %get-tuple-element.50.outer_ref, ...), custom_call_target="tpu_custom_call" | custom-call | tf_op jit(solution)/shard_map/step/pallas_call | solution.py:355
  82.2 5.9 %collective-permute-start.4 = (f32[16,128]{1,0:T(8,128)S(1)}, f32[16,128]{1,0:T(8,128)S(1)}, u32[]{:S(2)}, u32[]{:S(2)}) collective-permute-start(f32[16,128]{1,0:T(8,128)S(1)} %get-tuple-element.63), channel_id=1, source_target_pairs={{0,1},{1,0},{2,3},{3,2},{4,5},{5,4},{6,7},{7,6},{8,9},{9,8},{10,11... | collective-permute-start | bytes 24584 | tf_op jit(solution)/shard_map/ppermute | solution.py:458
  88.1 0.0 collective-permute-start.5
  88.1 0.8 collective-permute-done.4.near_ref
  88.9 0.8 inside.6
  89.7 1.5 %collective-permute-done.5.far_ref = f32[16,128]{1,0:T(8,128)S(1)} collective-permute-done((f32[16,128]{1,0:T(8,128)S(1)}, f32[16,128]{1,0:T(8,128)S(1)}, u32[]{:S(2)}, u32[]{:S(2)}) %collective-permute-start.5) | collective-permute-done | bytes 8224 | tf_op jit(solution)/shard_map/ppermute | solution.py:464
  91.2 1.8 %step.5 = (f32[96,128]{1,0:T(8,128)S(1)}, f32[96,128]{1,0:T(8,128)S(1)}, f32[16,128]{1,0:T(8,128)S(1)}) custom-call(f32[3,96,96,128]{3,2,1,0:T(8,128)S(1)} %get-tuple-element.49.blocks_ref, f32[96,96,128]{2,1,0:T(8,128)S(1)} %get-tuple-element.46.precond_ref, bf16[2,32,128]{2,1,0:T(8,128)(2,1)S(1)} %get-tuple-element.50.outer_ref, ...), custom_call_target="tpu_custom_call" | custom-call | tf_op jit(solution)/shard_map/step/pallas_call | solution.py:355
  92.9 5.5 %collective-permute-start.6 = (f32[16,128]{1,0:T(8,128)S(1)}, f32[16,128]{1,0:T(8,128)S(1)}, u32[]{:S(2)}, u32[]{:S(2)}) collective-permute-start(f32[16,128]{1,0:T(8,128)S(1)} %get-tuple-element.68), channel_id=1, source_target_pairs={{0,1},{1,0},{2,3},{3,2},{4,5},{5,4},{6,7},{7,6},{8,9},{9,8},{10,11... | collective-permute-start | bytes 24584 | tf_op jit(solution)/shard_map/ppermute | solution.py:458
  98.5 0.0 collective-permute-start.7
  98.5 0.8 collective-permute-done.6.near_ref
  99.3 0.8 inside.7
  100.1 1.5 %collective-permute-done.7.far_ref = f32[16,128]{1,0:T(8,128)S(1)} collective-permute-done((f32[16,128]{1,0:T(8,128)S(1)}, f32[16,128]{1,0:T(8,128)S(1)}, u32[]{:S(2)}, u32[]{:S(2)}) %collective-permute-start.7) | collective-permute-done | bytes 8224 | tf_op jit(solution)/shard_map/ppermute | solution.py:464
  101.5 2.0 %last.1 = (f32[96,128]{1,0:T(8,128)S(1)}, f32[128,128]{1,0:T(8,128)}) custom-call(f32[3,96,96,128]{3,2,1,0:T(8,128)S(1)} %get-tuple-element.49.blocks_ref, bf16[2,32,128]{2,1,0:T(8,128)(2,1)S(1)} %get-tuple-element.50.outer_ref, f32[96,128]{1,0:T(8,128)S(1)} %get-tuple-element.69.part_ref, f32[2,96,128]{2,1,0:T(8,128)S(1)} %get-tuple-element.70.taken_ref, ...), custom_call_target="tpu_custom_call" | custom-call | tf_op jit(solution)/shard_map/last/pallas_call | solution.py:381
  103.5 8.9 %all-to-all-start.3 = ((f32[128,1,128]{2,1,0:T(1,128)}), f32[128,1,128]{2,1,0:T(1,128)S(1)}, u32[]{:S(2)}, u32[]{:S(2)}) async-start(f32[128,1,128]{2,1,0:T(1,128)} %bitcast.14), calls=%async_computation.3 | async-start | bytes 131072 | tf_op jit(solution)/shard_map/all_to_all | solution.py:468
  112.4 0.6 copy.14
  113.1 8.9 %all-to-all-done.3 = f32[128,1,128]{2,1,0:T(1,128)S(1)} async-done(((f32[128,1,128]{2,1,0:T(1,128)}), f32[128,1,128]{2,1,0:T(1,128)S(1)}, u32[]{:S(2)}, u32[]{:S(2)}) %all-to-all-start.3) | async-done | bytes 65568 | tf_op jit(solution)/shard_map/all_to_all | solution.py:468
  122.0 0.9 finish.1
Async XLA Ops:
  2.4 20.9 %all-to-all-start = ((f32[128,1,128]{2,1,0:T(1,128)}), f32[128,1,128]{2,1,0:T(1,128)S(1)}, u32[]{:S(2)}, u32[]{:S(2)}) async-start(f32[128,1,128]{2,1,0:T(1,128)} %bitcast.3), calls=%async_computation | async-start | bytes 131072 | tf_op jit(solution)/shard_map/all_to_all | solution.py:468
  69.2 3.2 %collective-permute-start = (f32[16,128]{1,0:T(8,128)S(1)}, f32[16,128]{1,0:T(8,128)S(1)}, u32[]{:S(2)}, u32[]{:S(2)}) collective-permute-start(f32[16,128]{1,0:T(8,128)S(1)} %get-tuple-element.53), channel_id=1, source_target_pairs={{0,1},{1,0},{2,3},{3,2},{4,5},{5,4},{6,7},{7,6},{8,9},{9,8},{10,11... | collective-permute-start | bytes 24584 | tf_op jit(solution)/shard_map/ppermute | solution.py:458
  70.6 5.0 %collective-permute-start.1 = (f32[16,128]{1,0:T(8,128)S(1)}, f32[16,128]{1,0:T(8,128)S(1)}, u32[]{:S(2)}, u32[]{:S(2)}) collective-permute-start(f32[16,128]{1,0:T(8,128)S(1)} %get-tuple-element.53), channel_id=1, source_target_pairs={{1,2},{3,4},{5,6},{7,8},{9,10},{11,12},{13,14},{15,16},{17,18},{19... | collective-permute-start | bytes 24584 | tf_op jit(solution)/shard_map/ppermute | solution.py:464
  77.3 1.2 collective-permute-start.2
  77.3 3.2 %collective-permute-start.3 = (f32[16,128]{1,0:T(8,128)S(1)}, f32[16,128]{1,0:T(8,128)S(1)}, u32[]{:S(2)}, u32[]{:S(2)}) collective-permute-start(f32[16,128]{1,0:T(8,128)S(1)} %get-tuple-element.58), channel_id=1, source_target_pairs={{1,2},{3,4},{5,6},{7,8},{9,10},{11,12},{13,14},{15,16},{17,18},{19... | collective-permute-start | bytes 24584 | tf_op jit(solution)/shard_map/ppermute | solution.py:464
  82.2 6.7 %collective-permute-start.4 = (f32[16,128]{1,0:T(8,128)S(1)}, f32[16,128]{1,0:T(8,128)S(1)}, u32[]{:S(2)}, u32[]{:S(2)}) collective-permute-start(f32[16,128]{1,0:T(8,128)S(1)} %get-tuple-element.63), channel_id=1, source_target_pairs={{0,1},{1,0},{2,3},{3,2},{4,5},{5,4},{6,7},{7,6},{8,9},{9,8},{10,11... | collective-permute-start | bytes 24584 | tf_op jit(solution)/shard_map/ppermute | solution.py:458
  88.1 3.1 %collective-permute-start.5 = (f32[16,128]{1,0:T(8,128)S(1)}, f32[16,128]{1,0:T(8,128)S(1)}, u32[]{:S(2)}, u32[]{:S(2)}) collective-permute-start(f32[16,128]{1,0:T(8,128)S(1)} %get-tuple-element.63), channel_id=1, source_target_pairs={{1,2},{3,4},{5,6},{7,8},{9,10},{11,12},{13,14},{15,16},{17,18},{19... | collective-permute-start | bytes 24584 | tf_op jit(solution)/shard_map/ppermute | solution.py:464
  92.9 6.3 %collective-permute-start.6 = (f32[16,128]{1,0:T(8,128)S(1)}, f32[16,128]{1,0:T(8,128)S(1)}, u32[]{:S(2)}, u32[]{:S(2)}) collective-permute-start(f32[16,128]{1,0:T(8,128)S(1)} %get-tuple-element.68), channel_id=1, source_target_pairs={{0,1},{1,0},{2,3},{3,2},{4,5},{5,4},{6,7},{7,6},{8,9},{9,8},{10,11... | collective-permute-start | bytes 24584 | tf_op jit(solution)/shard_map/ppermute | solution.py:458
  98.5 3.1 %collective-permute-start.7 = (f32[16,128]{1,0:T(8,128)S(1)}, f32[16,128]{1,0:T(8,128)S(1)}, u32[]{:S(2)}, u32[]{:S(2)}) collective-permute-start(f32[16,128]{1,0:T(8,128)S(1)} %get-tuple-element.68), channel_id=1, source_target_pairs={{1,2},{3,4},{5,6},{7,8},{9,10},{11,12},{13,14},{15,16},{17,18},{19... | collective-permute-start | bytes 24584 | tf_op jit(solution)/shard_map/ppermute | solution.py:464
  103.5 18.4 %all-to-all-start.3 = ((f32[128,1,128]{2,1,0:T(1,128)}), f32[128,1,128]{2,1,0:T(1,128)S(1)}, u32[]{:S(2)}, u32[]{:S(2)}) async-start(f32[128,1,128]{2,1,0:T(1,128)} %bitcast.14), calls=%async_computation.3 | async-start | bytes 131072 | tf_op jit(solution)/shard_map/all_to_all | solution.py:468

commit v6 on v5

--- a/solution.py
+++ b/solution.py
@@ -76,6 +76,28 @@
     if x.shape[0] == rows:
         return x
     return jnp.concatenate([x, jnp.zeros((rows - x.shape[0], x.shape[1]), x.dtype)], axis=0)
+
+
+def pack(wide_ref, out_ref):
+    parts = wide_ref.shape[0] // CAP
+    free = iota((parts, LANES), 1) >= 96
+    spare = [wide_ref[pl.ds(6 + k, parts, CAP), :] for k in range(2)]
+    for r in range(6):
+        own = wide_ref[pl.ds(r, parts, CAP), :]
+        extra = pltpu.roll(spare[r // 3], 96 - 32 * (r % 3), axis=1)
+        out_ref[pl.ds(r, parts, 6), :] = jnp.where(free, extra, own)
+
+
+def unpack(packed_ref, wide_ref):
+    parts = wide_ref.shape[0] // CAP
+    lane = iota((parts, LANES), 1)
+    rows = [packed_ref[pl.ds(r, parts, 6), :] for r in range(6)]
+    for r in range(6):
+        wide_ref[pl.ds(r, parts, CAP), :] = rows[r]
+    for k in range(2):
+        first, second, third = [pltpu.roll(rows[3 * k + c], 32 * c + 32, axis=1) for c in range(3)]
+        value = jnp.where(lane < 32, first, jnp.where(lane < 64, second, third))
+        wide_ref[pl.ds(6 + k, parts, CAP), :] = value
 
 
 def slots_kernel(dest_ref, target_ref, labels_ref, slot_ref):
@@ -166,8 +188,8 @@
     )(*in_hbm(halo_list, place, columns, coords, after, fluid, force))
 
 
-def answer_kernel(labels_ref, coords_ref, onehot_ref, out_ref):
-    rows = out_ref.shape[0]
+def answer_kernel(labels_ref, coords_ref, onehot_ref, out_ref, wide):
+    rows = onehot_ref.shape[0]
     parts = labels_ref.shape[0]
     repeat = flag(iota((rows, parts), 0) // CAP == iota((rows, parts), 1))
     spread = dot(repeat, labels_ref[...].astype(BF16), NN)
@@ -176,7 +198,8 @@
     label = dot(own_label, jnp.ones((LANES, LANES), BF16), NN)
     onehot = flag(label == (iota((rows, LANES), 1) + 1).astype(F32))
     onehot_ref[...] = onehot
-    out_ref[...] = pick_from(onehot, coords_ref[...])
+    wide[...] = pick_from(onehot, coords_ref[...])
+    pack(wide, out_ref)
 
 
 def answer(labels, coords):
@@ -185,9 +208,10 @@
         answer_kernel,
         out_shape=(
             jax.ShapeDtypeStruct((rows, LANES), BF16),
-            jax.ShapeDtypeStruct((rows, LANES), F32),
+            jax.ShapeDtypeStruct((rows * 3 // 4, LANES), F32),
         ),
         in_specs=[VMEM, VMEM],
+        scratch_shapes=[pltpu.VMEM((rows, LANES), F32)],
         compiler_params=limit(6),
         name="answer",
     )(labels, *near_core(coords))
@@ -195,7 +219,7 @@
 
 def transfer_kernel(
     slot_ref, coords_ref, turned_ref, blocks_ref, precond_ref, out_ref, blocks_out, precond_out,
-    struct, mapped, sems,
+    wide, struct, mapped, sems,
 ):
     tables = [
         pltpu.make_async_copy(precond_ref, precond_out, sems.at[0]),
@@ -203,10 +227,11 @@
     ]
     for copy in tables:
         copy.start()
-    rows = coords_ref.shape[0]
+    rows = wide.shape[0]
     count = slot_ref.shape[1]
+    unpack(coords_ref, wide)
     chosen = flag(iota((rows, count), 0) == slot_ref[...])
-    struct[...] = pick(coords_ref[...], chosen, TN) * (1.0 / SUPPORT)
+    struct[...] = pick(wide[...], chosen, TN) * (1.0 / SUPPORT)
     nodes = turned_ref.shape[2]
     for group in range(count // LANES):
         lanes = pl.ds(group * LANES, LANES)
@@ -233,7 +258,8 @@
         for c in range(3):
             mapped[pl.ds(c * 32, 32), lanes] = sums[c]
     mapped[pl.ds(96, 32), :] = jnp.zeros((32, count), F32)
-    out_ref[...] = pick_from(chosen, mapped[...])
+    wide[...] = pick_from(chosen, mapped[...])
+    pack(wide, out_ref)
     for copy in tables:
         copy.wait()
 
@@ -250,6 +276,7 @@
         in_specs=[VMEM] * 3 + [ANY] * 2,
         out_specs=[VMEM] * 3,
         scratch_shapes=[
+            pltpu.VMEM((coords.shape[0] * 4 // 3, LANES), F32),
             pltpu.VMEM((LANES, count), F32),
             pltpu.VMEM((LANES, count), F32),
             pltpu.SemaphoreType.DMA((2,)),
@@ -283,8 +310,11 @@
     send_ref[...] = pick_from(listed_ref[...], pad_rows(out_ref[...], LANES))
 
 
-def start_kernel(mapped_ref, onehot_ref, precond_ref, listed_ref, load_ref, pre_ref, send_ref):
-    load = pick(mapped_ref[...], onehot_ref[...], TN)[: load_ref.shape[0]]
+def start_kernel(
+    mapped_ref, onehot_ref, precond_ref, listed_ref, load_ref, pre_ref, send_ref, wide
+):
+    unpack(mapped_ref, wide)
+    load = pick(wide[...], onehot_ref[...], TN)[: load_ref.shape[0]]
     load_ref[...] = load
     precondition(precond_ref, listed_ref, load, pre_ref, send_ref)
 
@@ -296,6 +326,7 @@
         out_shape=(shape, shape, pltpu.VMEM(listed.shape, F32)),
         in_specs=[VMEM] * 4,
         out_specs=[VMEM] * 3,
+        scratch_shapes=[pltpu.VMEM(onehot.shape, F32)],
         compiler_params=limit(6),
         name="start",
     )(mapped, onehot, *near_core(precond, listed))
@@ -481,9 +512,9 @@
         halo_list, place, columns, coords, wanted, fluid, force
     )
     onehot, answered = answer(to_all(wanted), coords)
-    answered = to_all(answered.reshape(parts, CAP, LANES)).reshape(parts * CAP, LANES)
+    answered = to_all(answered.reshape(parts, 1, -1)).reshape(answered.shape)
     mapped, blocks, precond = transfer(slot, answered, turned, blocks, precond)
-    mapped = to_all(mapped.reshape(parts, CAP, LANES)).reshape(parts * CAP, LANES)
+    mapped = to_all(mapped.reshape(parts, 1, -1)).reshape(mapped.shape)
     load, pre, send = start(mapped, onehot, precond, listed)
     basis, pres = [load], [pre]
     for j in range(STEPS):

time: 123 us -> 121 us (0.984)
  blocking collectives: 36.2 us -> 33.4 us
    all_to_all x2, blocking collectives: 36.2 us -> 33.4 us  [to_all(): return lax.all_to_all(x, DOM, split_axis=0, concat_axis=0, tiled=True)]
where the time goes in v6:
time: 121 us
  starting transfers between devices  35.3 us (29%)
  blocking collectives  33.4 us (28%)
  Pallas kernels  26.1 us (22%)
  waiting for transfers between devices  24.5 us (20%)
    all_to_all x2, blocking collectives, to_all(): return lax.all_to_all(x, DOM, split_axis=0, concat_axis=0, tiled=True)  33.4 us
    all_to_all x2, starting transfers between devices, to_all(): return lax.all_to_all(x, DOM, split_axis=0, concat_axis=0, tiled=True)  20.4 us
    all_to_all x2, waiting for transfers between devices, to_all(): return lax.all_to_all(x, DOM, split_axis=0, concat_axis=0, tiled=True)  15.6 us
    ppermute x4, starting transfers between devices, to_near(): return lax.ppermute(send, DOM, [(i, i ^ 1) for i in range(devices)])  12.7 us
    pallas_call x1, Pallas kernels, transfer(): pl.pallas_call(transfer_kernel, out_shape=(jax.ShapeDtypeStruct(coords.sh...  8.29 us
    ppermute x4, waiting for transfers between devices, to_far(): return lax.ppermute(send, DOM, pairs + [(j, i) for i, j in pairs])  6.35 us
    pallas_call x3, Pallas kernels, step(): pl.pallas_call(step_kernel, out_shape=(shape, shape, pltpu.VMEM(far.shape...  5.3 us
    pallas_call x4, Pallas kernels, inside(): pl.pallas_call(inside_kernel, out_shape=(pltpu.VMEM(old.shape, F32), pltp...  3.11 us
  transfers between devices with their start and end apart: 10, of which 9 were waited for; matrix products, arithmetic and copies ran while one was open for 1% of the time, Pallas kernels for 5%

profile of v6, /device:TPU:1, one launch (start us, length us, event | category | flops | bytes accessed | tf_op | source)
XLA Modules:
  0.0 120.6 jit_solution(12805443359935870166)
XLA Ops:
  0.6 1.8 %slots.1 = (f32[128,128]{1,0:T(8,128)}, s32[1,512]{1,0:T(1,128)S(1)}) custom-call(s32[1,512]{1,0:T(1,128)} %bitcast.27, s32[1,512]{1,0:T(1,128)} %bitcast.28), custom_call_target="tpu_custom_call" | custom-call | tf_op jit(solution)/shard_map/slots/pallas_call | solution.py:119
  2.4 11.5 %all-to-all-start = ((f32[128,1,128]{2,1,0:T(1,128)}), f32[128,1,128]{2,1,0:T(1,128)S(1)}, u32[]{:S(2)}, u32[]{:S(2)}) async-start(f32[128,1,128]{2,1,0:T(1,128)} %bitcast.3), calls=%async_computation | async-start | bytes 131072 | tf_op jit(solution)/shard_map/all_to_all | solution.py:499
  13.9 2.7 %prepare.1 = (f32[4,7,128,128]{3,2,1,0:T(8,128)S(1)}, f32[128,128]{1,0:T(8,128)S(1)}, bf16[2,128,128]{2,1,0:T(8,128)(2,1)S(1)}, bf16[2,32,128]{2,1,0:T(8,128)(2,1)S(1)}, bf16[16,128]{1,0:T(8,128)(2,1)S(1)}) custom-call(s32[16]{0:T(128)} %halo_ref.1, s32[1]{0:T(128)} %bitcast.5.place_ref, s32[2,128]{1,0:T(2,128)} %columns_ref.1, f32[96,128]{1,0:T(8,128)} %bitcast.26, ...), custom_call_target="tpu_custom_call" | custom-call | bytes 3145728 | tf_op jit(solution)/shard_map/prepare/pallas_call | solution.py:173
  16.6 6.7 %all-to-all-done = f32[128,1,128]{2,1,0:T(1,128)S(1)} async-done(((f32[128,1,128]{2,1,0:T(1,128)}), f32[128,1,128]{2,1,0:T(1,128)S(1)}, u32[]{:S(2)}, u32[]{:S(2)}) %all-to-all-start) | async-done | bytes 65568 | tf_op jit(solution)/shard_map/all_to_all | solution.py:499
  23.3 0.8 answer.1
  24.0 16.7 %all_to_all.32 = f32[128,1,768]{2,1,0:T(1,128)S(1)} all-to-all(f32[128,1,768]{2,1,0:T(1,128)S(1)} %bitcast.21), channel_id=1, replica_groups=mesh['dom'=128] {'dom'}, dimensions={0} | all-to-all | bytes 786432 | tf_op jit(solution)/shard_map/all_to_all | solution.py:499
  40.8 8.3 %transfer.1 = (f32[768,128]{1,0:T(8,128)S(1)}, f32[3,96,96,128]{3,2,1,0:T(8,128)S(1)}, f32[96,96,128]{2,1,0:T(8,128)S(1)}) custom-call(s32[1,512]{1,0:T(1,128)S(1)} %get-tuple-element.39.slot_ref, f32[768,128]{1,0:T(8,128)S(1)} %bitcast.19, f32[4,7,128,128]{3,2,1,0:T(8,128)S(1)} %get-tuple-element.43.turned_ref, f32[3,96,96,128]{3,2,1,0:T(8,128)} %blocks_ref.1, ...), custom_call_target="tpu_custom_call" | custom-call | tf_op jit(solution)/shard_map/transfer/pallas_call | solution.py:269
  49.1 16.7 %all_to_all.33 = f32[128,1,768]{2,1,0:T(1,128)S(1)} all-to-all(f32[128,1,768]{2,1,0:T(1,128)S(1)} %bitcast.20), channel_id=1, replica_groups=mesh['dom'=128] {'dom'}, dimensions={0} | all-to-all | bytes 786432 | tf_op jit(solution)/shard_map/all_to_all | solution.py:499
  65.8 1.3 %start.1 = (f32[96,128]{1,0:T(8,128)S(1)}, f32[96,128]{1,0:T(8,128)S(1)}, f32[16,128]{1,0:T(8,128)S(1)}) custom-call(f32[768,128]{1,0:T(8,128)S(1)} %bitcast.18, bf16[1024,128]{1,0:T(8,128)(2,1)S(1)} %get-tuple-element.45.onehot_ref, f32[96,96,128]{2,1,0:T(8,128)S(1)} %get-tuple-element.46.precond_ref, bf16[16,128]{1,0:T(8,128)(2,1)S(1)} %get-tuple-element.47.listed_ref), custom_call_target="tpu_custom_call" | custom-call | tf_op jit(solution)/shard_map/start/pallas_call | solution.py:324
  67.0 1.3 %collective-permute-start = (f32[16,128]{1,0:T(8,128)S(1)}, f32[16,128]{1,0:T(8,128)S(1)}, u32[]{:S(2)}, u32[]{:S(2)}) collective-permute-start(f32[16,128]{1,0:T(8,128)S(1)} %get-tuple-element.53), channel_id=1, source_target_pairs={{0,1},{1,0},{2,3},{3,2},{4,5},{5,4},{6,7},{7,6},{8,9},{9,8},{10,11... | collective-permute-start | bytes 24584 | tf_op jit(solution)/shard_map/ppermute | solution.py:489
  68.3 1.9 %collective-permute-start.1 = (f32[16,128]{1,0:T(8,128)S(1)}, f32[16,128]{1,0:T(8,128)S(1)}, u32[]{:S(2)}, u32[]{:S(2)}) collective-permute-start(f32[16,128]{1,0:T(8,128)S(1)} %get-tuple-element.53), channel_id=1, source_target_pairs={{1,2},{3,4},{5,6},{7,8},{9,10},{11,12},{13,14},{15,16},{17,18},{19... | collective-permute-start | bytes 24584 | tf_op jit(solution)/shard_map/ppermute | solution.py:495
  70.3 0.0 collective-permute-done.near_ref
  70.3 0.8 inside.4
  71.1 2.2 %collective-permute-done.1.far_ref = f32[16,128]{1,0:T(8,128)S(1)} collective-permute-done((f32[16,128]{1,0:T(8,128)S(1)}, f32[16,128]{1,0:T(8,128)S(1)}, u32[]{:S(2)}, u32[]{:S(2)}) %collective-permute-start.1) | collective-permute-done | bytes 8224 | tf_op jit(solution)/shard_map/ppermute | solution.py:495
  73.3 1.8 %step.3 = (f32[96,128]{1,0:T(8,128)S(1)}, f32[96,128]{1,0:T(8,128)S(1)}, f32[16,128]{1,0:T(8,128)S(1)}) custom-call(f32[3,96,96,128]{3,2,1,0:T(8,128)S(1)} %get-tuple-element.49.blocks_ref, f32[96,96,128]{2,1,0:T(8,128)S(1)} %get-tuple-element.46.precond_ref, bf16[2,32,128]{2,1,0:T(8,128)(2,1)S(1)} %get-tuple-element.50.outer_ref, ...), custom_call_target="tpu_custom_call" | custom-call | tf_op jit(solution)/shard_map/step/pallas_call | solution.py:386
  75.1 0.0 collective-permute-start.2
  75.1 0.3 collective-permute-start.3
  75.4 0.9 collective-permute-done.2.near_ref
  76.3 0.8 inside.5
  77.0 1.2 collective-permute-done.3.far_ref
  78.2 1.8 %step.4 = (f32[96,128]{1,0:T(8,128)S(1)}, f32[96,128]{1,0:T(8,128)S(1)}, f32[16,128]{1,0:T(8,128)S(1)}) custom-call(f32[3,96,96,128]{3,2,1,0:T(8,128)S(1)} %get-tuple-element.49.blocks_ref, f32[96,96,128]{2,1,0:T(8,128)S(1)} %get-tuple-element.46.precond_ref, bf16[2,32,128]{2,1,0:T(8,128)(2,1)S(1)} %get-tuple-element.50.outer_ref, ...), custom_call_target="tpu_custom_call" | custom-call | tf_op jit(solution)/shard_map/step/pallas_call | solution.py:386
  80.0 5.9 %collective-permute-start.4 = (f32[16,128]{1,0:T(8,128)S(1)}, f32[16,128]{1,0:T(8,128)S(1)}, u32[]{:S(2)}, u32[]{:S(2)}) collective-permute-start(f32[16,128]{1,0:T(8,128)S(1)} %get-tuple-element.63), channel_id=1, source_target_pairs={{0,1},{1,0},{2,3},{3,2},{4,5},{5,4},{6,7},{7,6},{8,9},{9,8},{10,11... | collective-permute-start | bytes 24584 | tf_op jit(solution)/shard_map/ppermute | solution.py:489
  85.9 0.0 collective-permute-start.5
  85.9 0.8 collective-permute-done.4.near_ref
  86.7 0.8 inside.6
  87.5 1.5 %collective-permute-done.5.far_ref = f32[16,128]{1,0:T(8,128)S(1)} collective-permute-done((f32[16,128]{1,0:T(8,128)S(1)}, f32[16,128]{1,0:T(8,128)S(1)}, u32[]{:S(2)}, u32[]{:S(2)}) %collective-permute-start.5) | collective-permute-done | bytes 8224 | tf_op jit(solution)/shard_map/ppermute | solution.py:495
  89.0 1.8 %step.5 = (f32[96,128]{1,0:T(8,128)S(1)}, f32[96,128]{1,0:T(8,128)S(1)}, f32[16,128]{1,0:T(8,128)S(1)}) custom-call(f32[3,96,96,128]{3,2,1,0:T(8,128)S(1)} %get-tuple-element.49.blocks_ref, f32[96,96,128]{2,1,0:T(8,128)S(1)} %get-tuple-element.46.precond_ref, bf16[2,32,128]{2,1,0:T(8,128)(2,1)S(1)} %get-tuple-element.50.outer_ref, ...), custom_call_target="tpu_custom_call" | custom-call | tf_op jit(solution)/shard_map/step/pallas_call | solution.py:386
  90.7 5.5 %collective-permute-start.6 = (f32[16,128]{1,0:T(8,128)S(1)}, f32[16,128]{1,0:T(8,128)S(1)}, u32[]{:S(2)}, u32[]{:S(2)}) collective-permute-start(f32[16,128]{1,0:T(8,128)S(1)} %get-tuple-element.68), channel_id=1, source_target_pairs={{0,1},{1,0},{2,3},{3,2},{4,5},{5,4},{6,7},{7,6},{8,9},{9,8},{10,11... | collective-permute-start | bytes 24584 | tf_op jit(solution)/shard_map/ppermute | solution.py:489
  96.3 0.0 collective-permute-start.7
  96.3 0.8 collective-permute-done.6.near_ref
  97.1 0.8 inside.7
  97.9 1.5 %collective-permute-done.7.far_ref = f32[16,128]{1,0:T(8,128)S(1)} collective-permute-done((f32[16,128]{1,0:T(8,128)S(1)}, f32[16,128]{1,0:T(8,128)S(1)}, u32[]{:S(2)}, u32[]{:S(2)}) %collective-permute-start.7) | collective-permute-done | bytes 8224 | tf_op jit(solution)/shard_map/ppermute | solution.py:495
  99.3 2.0 %last.1 = (f32[96,128]{1,0:T(8,128)S(1)}, f32[128,128]{1,0:T(8,128)}) custom-call(f32[3,96,96,128]{3,2,1,0:T(8,128)S(1)} %get-tuple-element.49.blocks_ref, bf16[2,32,128]{2,1,0:T(8,128)(2,1)S(1)} %get-tuple-element.50.outer_ref, f32[96,128]{1,0:T(8,128)S(1)} %get-tuple-element.69.part_ref, f32[2,96,128]{2,1,0:T(8,128)S(1)} %get-tuple-element.70.taken_ref, ...), custom_call_target="tpu_custom_call" | custom-call | tf_op jit(solution)/shard_map/last/pallas_call | solution.py:412
  101.3 8.9 %all-to-all-start.3 = ((f32[128,1,128]{2,1,0:T(1,128)}), f32[128,1,128]{2,1,0:T(1,128)S(1)}, u32[]{:S(2)}, u32[]{:S(2)}) async-start(f32[128,1,128]{2,1,0:T(1,128)} %bitcast.14), calls=%async_computation.3 | async-start | bytes 131072 | tf_op jit(solution)/shard_map/all_to_all | solution.py:499
  110.2 0.6 copy.16
  110.9 8.9 %all-to-all-done.3 = f32[128,1,128]{2,1,0:T(1,128)S(1)} async-done(((f32[128,1,128]{2,1,0:T(1,128)}), f32[128,1,128]{2,1,0:T(1,128)S(1)}, u32[]{:S(2)}, u32[]{:S(2)}) %all-to-all-start.3) | async-done | bytes 65568 | tf_op jit(solution)/shard_map/all_to_all | solution.py:499
  119.8 0.9 finish.1
Async XLA Ops:
  2.4 20.9 %all-to-all-start = ((f32[128,1,128]{2,1,0:T(1,128)}), f32[128,1,128]{2,1,0:T(1,128)S(1)}, u32[]{:S(2)}, u32[]{:S(2)}) async-start(f32[128,1,128]{2,1,0:T(1,128)} %bitcast.3), calls=%async_computation | async-start | bytes 131072 | tf_op jit(solution)/shard_map/all_to_all | solution.py:499
  67.0 3.2 %collective-permute-start = (f32[16,128]{1,0:T(8,128)S(1)}, f32[16,128]{1,0:T(8,128)S(1)}, u32[]{:S(2)}, u32[]{:S(2)}) collective-permute-start(f32[16,128]{1,0:T(8,128)S(1)} %get-tuple-element.53), channel_id=1, source_target_pairs={{0,1},{1,0},{2,3},{3,2},{4,5},{5,4},{6,7},{7,6},{8,9},{9,8},{10,11... | collective-permute-start | bytes 24584 | tf_op jit(solution)/shard_map/ppermute | solution.py:489
  68.3 5.0 %collective-permute-start.1 = (f32[16,128]{1,0:T(8,128)S(1)}, f32[16,128]{1,0:T(8,128)S(1)}, u32[]{:S(2)}, u32[]{:S(2)}) collective-permute-start(f32[16,128]{1,0:T(8,128)S(1)} %get-tuple-element.53), channel_id=1, source_target_pairs={{1,2},{3,4},{5,6},{7,8},{9,10},{11,12},{13,14},{15,16},{17,18},{19... | collective-permute-start | bytes 24584 | tf_op jit(solution)/shard_map/ppermute | solution.py:495
  75.1 1.2 collective-permute-start.2
  75.1 3.2 %collective-permute-start.3 = (f32[16,128]{1,0:T(8,128)S(1)}, f32[16,128]{1,0:T(8,128)S(1)}, u32[]{:S(2)}, u32[]{:S(2)}) collective-permute-start(f32[16,128]{1,0:T(8,128)S(1)} %get-tuple-element.58), channel_id=1, source_target_pairs={{1,2},{3,4},{5,6},{7,8},{9,10},{11,12},{13,14},{15,16},{17,18},{19... | collective-permute-start | bytes 24584 | tf_op jit(solution)/shard_map/ppermute | solution.py:495
  80.0 6.7 %collective-permute-start.4 = (f32[16,128]{1,0:T(8,128)S(1)}, f32[16,128]{1,0:T(8,128)S(1)}, u32[]{:S(2)}, u32[]{:S(2)}) collective-permute-start(f32[16,128]{1,0:T(8,128)S(1)} %get-tuple-element.63), channel_id=1, source_target_pairs={{0,1},{1,0},{2,3},{3,2},{4,5},{5,4},{6,7},{7,6},{8,9},{9,8},{10,11... | collective-permute-start | bytes 24584 | tf_op jit(solution)/shard_map/ppermute | solution.py:489
  85.9 3.1 %collective-permute-start.5 = (f32[16,128]{1,0:T(8,128)S(1)}, f32[16,128]{1,0:T(8,128)S(1)}, u32[]{:S(2)}, u32[]{:S(2)}) collective-permute-start(f32[16,128]{1,0:T(8,128)S(1)} %get-tuple-element.63), channel_id=1, source_target_pairs={{1,2},{3,4},{5,6},{7,8},{9,10},{11,12},{13,14},{15,16},{17,18},{19... | collective-permute-start | bytes 24584 | tf_op jit(solution)/shard_map/ppermute | solution.py:495
  90.7 6.3 %collective-permute-start.6 = (f32[16,128]{1,0:T(8,128)S(1)}, f32[16,128]{1,0:T(8,128)S(1)}, u32[]{:S(2)}, u32[]{:S(2)}) collective-permute-start(f32[16,128]{1,0:T(8,128)S(1)} %get-tuple-element.68), channel_id=1, source_target_pairs={{0,1},{1,0},{2,3},{3,2},{4,5},{5,4},{6,7},{7,6},{8,9},{9,8},{10,11... | collective-permute-start | bytes 24584 | tf_op jit(solution)/shard_map/ppermute | solution.py:489
  96.3 3.1 %collective-permute-start.7 = (f32[16,128]{1,0:T(8,128)S(1)}, f32[16,128]{1,0:T(8,128)S(1)}, u32[]{:S(2)}, u32[]{:S(2)}) collective-permute-start(f32[16,128]{1,0:T(8,128)S(1)} %get-tuple-element.68), channel_id=1, source_target_pairs={{1,2},{3,4},{5,6},{7,8},{9,10},{11,12},{13,14},{15,16},{17,18},{19... | collective-permute-start | bytes 24584 | tf_op jit(solution)/shard_map/ppermute | solution.py:495
  101.3 18.4 %all-to-all-start.3 = ((f32[128,1,128]{2,1,0:T(1,128)}), f32[128,1,128]{2,1,0:T(1,128)S(1)}, u32[]{:S(2)}, u32[]{:S(2)}) async-start(f32[128,1,128]{2,1,0:T(1,128)} %bitcast.14), calls=%async_computation.3 | async-start | bytes 131072 | tf_op jit(solution)/shard_map/all_to_all | solution.py:499

commit v7 on v6

--- a/solution.py
+++ b/solution.py
@@ -12,6 +12,8 @@
 CAP = 8
 LANES = 128
 STEPS = 4
+KNOWN = [(i, j) for j in range(STEPS) for i in range(j + 1)]
+HELD = 16
 F32 = jnp.float32
 BF16 = jnp.bfloat16
 NN = (((1,), (0,)), ((), ()))
@@ -332,7 +334,10 @@
     )(mapped, onehot, *near_core(precond, listed))
 
 
-def inside_kernel(blocks_ref, local_ref, outer_ref, old_ref, pre_ref, near_ref, part_ref, taken_ref):
+def inside_kernel(
+    blocks_ref, local_ref, outer_ref, old_ref, pre_ref, near_ref, *refs
+):
+    earlier, (part_ref, taken_ref, *more) = refs[:-3], refs[-3:]
     pre = pre_ref[...]
     size = pre.shape[0]
     count = near_ref.shape[0]
@@ -344,19 +349,26 @@
     for neighbor in range(2):
         taken = pick(pre, local_ref[neighbor], NN)
         taken_ref[neighbor] = taken + pick(near_ref[...], outer_ref[neighbor, :count, :], TN)[:size]
-
-
-def inside(blocks, local, outer, old, pre, near):
+    if not earlier:
+        more[0][...] = old_ref[...]
+    else:
+        vectors = [ref[...] for ref in earlier] + [old_ref[...]]
+        sums = [jnp.sum(vectors[i] * vectors[j], axis=0, keepdims=True) for i, j in KNOWN]
+        more[0][...] = pad_rows(jnp.concatenate(sums, axis=0), HELD)
+
+
+def inside(blocks, local, outer, old, pre, near, earlier):
     size = old.shape[0]
+    more = pltpu.VMEM((HELD, LANES), F32) if earlier else jax.ShapeDtypeStruct(old.shape, F32)
     return pl.pallas_call(
         inside_kernel,
-        out_shape=(pltpu.VMEM(old.shape, F32), pltpu.VMEM((2, size, LANES), F32)),
-        in_specs=[VMEM] * 6,
-        out_specs=[VMEM] * 2,
+        out_shape=(pltpu.VMEM(old.shape, F32), pltpu.VMEM((2, size, LANES), F32), more),
+        in_specs=[VMEM] * (6 + len(earlier)),
+        out_specs=[VMEM] * 3,
         compiler_params=limit(6),
         cost_estimate=pl.CostEstimate(flops=0, bytes_accessed=2 * MIB, transcendentals=0),
         name="inside",
-    )(*near_core(blocks, local, outer, old, pre, near))
+    )(*near_core(blocks, local, outer, old, pre, near, *earlier))
 
 
 def outside(blocks_ref, outer_ref, part_ref, taken_ref, far_ref, new_ref):
@@ -393,46 +405,47 @@
     )(*near_core(blocks, precond, outer, listed, part, taken, far))
 
 
-PAIRS = [(i, j) for i in range(STEPS + 1) for j in range(i, STEPS + 1)]
-
-
 def last_kernel(
-    blocks_ref, outer_ref, part_ref, taken_ref, far_ref, b0_ref, b1_ref, b2_ref, b3_ref,
+    blocks_ref, outer_ref, part_ref, taken_ref, far_ref, known_ref, b0_ref, b1_ref, b2_ref, b3_ref,
     new_ref, sums_ref,
 ):
     outside(blocks_ref, outer_ref, part_ref, taken_ref, far_ref, new_ref)
-    vectors = [ref[...] for ref in (b0_ref, b1_ref, b2_ref, b3_ref, new_ref)]
-    sums = [jnp.sum(vectors[i] * vectors[j], axis=0, keepdims=True) for i, j in PAIRS]
-    sums.append(jnp.zeros((LANES - len(sums), LANES), F32))
+    new = new_ref[...]
+    vectors = [ref[...] for ref in (b0_ref, b1_ref, b2_ref, b3_ref)] + [new]
+    sums = [known_ref[...]] + [jnp.sum(v * new, axis=0, keepdims=True) for v in vectors]
     ones = jnp.ones((sums_ref.shape[0], LANES), BF16)
-    sums_ref[...] = pick_from(ones, jnp.concatenate(sums, axis=0))
-
-
-def last(blocks, outer, part, taken, far, basis, parts):
+    sums_ref[...] = pick_from(ones, pad_rows(jnp.concatenate(sums, axis=0), LANES))
+
+
+def last(blocks, outer, part, taken, far, known, basis, parts):
     return pl.pallas_call(
         last_kernel,
         out_shape=(pltpu.VMEM(part.shape, F32), pltpu.VMEM((parts, LANES), F32)),
-        in_specs=[VMEM] * 9,
+        in_specs=[VMEM] * 10,
         out_specs=[VMEM] * 2,
         compiler_params=limit(6),
         name="last",
-    )(*near_core(blocks, outer, part, taken, far, *basis))
+    )(*near_core(blocks, outer, part, taken, far, known, *basis))
 
 
 def plus(x, y):
     return [a + b for a, b in zip(x, y)]
 
 
+def tree(terms):
+    while len(terms) > 1:
+        terms = [sum(terms[k : k + 2]) for k in range(0, len(terms), 2)]
+    return terms[0]
+
+
 def scaled(scale, x):
     return [scale * a for a in x]
 
 
 def recurrences(product):
     def inner(x, y):
-        return sum(
-            a * b * product[min(i, j), max(i, j)]
-            for i, a in enumerate(x)
-            for j, b in enumerate(y)
+        return tree(
+            [a * b * product[min(i, j), max(i, j)] for i, a in enumerate(x) for j, b in enumerate(y)]
         )
 
     def image_of(x):
@@ -467,7 +480,9 @@
 def finish_kernel(sums_ref, *refs):
     basis, pres, (solution_ref, residual_ref) = refs[:5], refs[5:9], refs[9:]
     totals = jnp.sum(sums_ref[...], axis=0, keepdims=True)
-    product = {pair: totals[:, k : k + 1] for k, pair in enumerate(PAIRS)}
+    lane = dict(zip(KNOWN, range(len(KNOWN))))
+    lane.update({(i, STEPS): HELD + i for i in range(STEPS + 1)})
+    product = {pair: totals[:, k : k + 1] for pair, k in lane.items()}
     answer, residual = recurrences(product)
     solution_ref[...] = sum(a * ref[...] for a, ref in zip(answer, pres))
     residual_ref[...] = sum(a * ref[...] for a, ref in zip(residual, basis))
@@ -520,15 +535,17 @@
     for j in range(STEPS):
         far = to_far(send, j > 0)
         near = to_near(send)
-        part, taken = inside(blocks, local, outer, basis[-1], pres[-1], near)
+        earlier = basis[:-1] if j == STEPS - 1 else []
+        part, taken, more = inside(blocks, local, outer, basis[-1], pres[-1], near, earlier)
+        load_field = more if j == 0 else load_field
         if j < STEPS - 1:
             new, pre, send = step(blocks, precond, outer, listed, part, taken, far)
             pres.append(pre)
         else:
-            new, sums = last(blocks, outer, part, taken, far, basis, parts)
+            new, sums = last(blocks, outer, part, taken, far, more, basis, parts)
         basis.append(new)
     solution, residual = finish(to_all(sums), basis, pres)
-    return load, solution, residual
+    return load_field, solution, residual
 
 
 def solution(mesh):

time: 121 us -> 120 us (level)
  blocking collectives: 33.4 us -> 51.2 us
  waiting for transfers between devices: 24.5 us -> 14.3 us
  starting transfers between devices: 35.3 us -> 26.4 us
    all_to_all x2 -> x3, blocking collectives: 33.4 us -> 51.2 us  [to_all(): return lax.all_to_all(x, DOM, split_axis=0, concat_axis=0, tiled=True)]
    all_to_all x2 -> x1, starting transfers between devices: 20.4 us -> 11.5 us  [to_all(): return lax.all_to_all(x, DOM, split_axis=0, concat_axis=0, tiled=True)]
    all_to_all x2 -> x1, waiting for transfers between devices: 15.6 us -> 6.68 us  [to_all(): return lax.all_to_all(x, DOM, split_axis=0, concat_axis=0, tiled=True)]
    pallas_call x4, Pallas kernels: 3.11 us -> 4.42 us  [inside(): pl.pallas_call(inside_kernel, out_shape=(pltpu.VMEM(old.shape, F32), pltp...]
    ppermute x4, waiting for transfers between devices: 6.35 us -> 5.06 us  [to_far(): return lax.ppermute(send, DOM, pairs + [(j, i) for i, j in pairs])]
  transfers between devices with their start and end apart: 10 -> 9, of which waited for: 9 -> 8; matrix products, arithmetic and copies ran while one was open for 1% -> 0% of each run, Pallas kernels for 5% -> 6%
where the time goes in v7:
time: 120 us; the launch traced here: 119 us
  blocking collectives  51.2 us (43%)
  Pallas kernels  26.7 us (22%)
  starting transfers between devices  26.4 us (22%)
  waiting for transfers between devices  14.3 us (12%)
    all_to_all x3, blocking collectives, to_all(): return lax.all_to_all(x, DOM, split_axis=0, concat_axis=0, tiled=True)  51.2 us
    ppermute x4, starting transfers between devices, to_near(): return lax.ppermute(send, DOM, [(i, i ^ 1) for i in range(devices)])  12.7 us
    all_to_all x1, starting transfers between devices, to_all(): return lax.all_to_all(x, DOM, split_axis=0, concat_axis=0, tiled=True)  11.5 us
    pallas_call x1, Pallas kernels, transfer(): pl.pallas_call(transfer_kernel, out_shape=(jax.ShapeDtypeStruct(coords.sh...  8.31 us
    all_to_all x1, waiting for transfers between devices, to_all(): return lax.all_to_all(x, DOM, split_axis=0, concat_axis=0, tiled=True)  6.68 us
    pallas_call x3, Pallas kernels, step(): pl.pallas_call(step_kernel, out_shape=(shape, shape, pltpu.VMEM(far.shape...  5.3 us
    ppermute x4, waiting for transfers between devices, to_far(): return lax.ppermute(send, DOM, pairs + [(j, i) for i, j in pairs])  5.06 us
    pallas_call x4, Pallas kernels, inside(): pl.pallas_call(inside_kernel, out_shape=(pltpu.VMEM(old.shape, F32), pltp...  4.42 us
  transfers between devices with their start and end apart: 9, of which 8 were waited for; matrix products, arithmetic and copies ran while one was open for 0% of the time, Pallas kernels for 6%

profile of v7, /device:TPU:1, one launch (start us, length us, event | category | flops | bytes accessed | tf_op | source)
XLA Modules:
  0.0 119.3 jit_solution(3169656292435611679)
XLA Ops:
  0.6 1.8 %slots.1 = (f32[128,128]{1,0:T(8,128)}, s32[1,512]{1,0:T(1,128)S(1)}) custom-call(s32[1,512]{1,0:T(1,128)} %bitcast.28, s32[1,512]{1,0:T(1,128)} %bitcast.29), custom_call_target="tpu_custom_call" | custom-call | tf_op jit(solution)/shard_map/slots/pallas_call | solution.py:121
  2.4 11.5 %all-to-all-start = ((f32[128,1,128]{2,1,0:T(1,128)}), f32[128,1,128]{2,1,0:T(1,128)S(1)}, u32[]{:S(2)}, u32[]{:S(2)}) async-start(f32[128,1,128]{2,1,0:T(1,128)} %bitcast.3), calls=%async_computation | async-start | bytes 131072 | tf_op jit(solution)/shard_map/all_to_all | solution.py:514
  13.9 2.7 %prepare.1 = (f32[4,7,128,128]{3,2,1,0:T(8,128)S(1)}, f32[128,128]{1,0:T(8,128)S(1)}, bf16[2,128,128]{2,1,0:T(8,128)(2,1)S(1)}, bf16[2,32,128]{2,1,0:T(8,128)(2,1)S(1)}, bf16[16,128]{1,0:T(8,128)(2,1)S(1)}) custom-call(s32[16]{0:T(128)} %halo_ref.1, s32[1]{0:T(128)} %bitcast.5.place_ref, s32[2,128]{1,0:T(2,128)} %columns_ref.1, f32[96,128]{1,0:T(8,128)} %bitcast.27, ...), custom_call_target="tpu_custom_call" | custom-call | bytes 3145728 | tf_op jit(solution)/shard_map/prepare/pallas_call | solution.py:175
  16.6 6.7 %all-to-all-done = f32[128,1,128]{2,1,0:T(1,128)S(1)} async-done(((f32[128,1,128]{2,1,0:T(1,128)}), f32[128,1,128]{2,1,0:T(1,128)S(1)}, u32[]{:S(2)}, u32[]{:S(2)}) %all-to-all-start) | async-done | bytes 65568 | tf_op jit(solution)/shard_map/all_to_all | solution.py:514
  23.3 0.8 answer.1
  24.1 16.7 %all_to_all.32 = f32[128,1,768]{2,1,0:T(1,128)S(1)} all-to-all(f32[128,1,768]{2,1,0:T(1,128)S(1)} %bitcast.21), channel_id=1, replica_groups=mesh['dom'=128] {'dom'}, dimensions={0} | all-to-all | bytes 786432 | tf_op jit(solution)/shard_map/all_to_all | solution.py:514
  40.8 8.3 %transfer.1 = (f32[768,128]{1,0:T(8,128)S(1)}, f32[3,96,96,128]{3,2,1,0:T(8,128)S(1)}, f32[96,96,128]{2,1,0:T(8,128)S(1)}) custom-call(s32[1,512]{1,0:T(1,128)S(1)} %get-tuple-element.41.slot_ref, f32[768,128]{1,0:T(8,128)S(1)} %bitcast.19, f32[4,7,128,128]{3,2,1,0:T(8,128)S(1)} %get-tuple-element.45.turned_ref, f32[3,96,96,128]{3,2,1,0:T(8,128)} %blocks_ref.1, ...), custom_call_target="tpu_custom_call" | custom-call | tf_op jit(solution)/shard_map/transfer/pallas_call | solution.py:271
  49.1 16.7 %all_to_all.33 = f32[128,1,768]{2,1,0:T(1,128)S(1)} all-to-all(f32[128,1,768]{2,1,0:T(1,128)S(1)} %bitcast.20), channel_id=1, replica_groups=mesh['dom'=128] {'dom'}, dimensions={0} | all-to-all | bytes 786432 | tf_op jit(solution)/shard_map/all_to_all | solution.py:514
  65.8 1.3 %start.1 = (f32[96,128]{1,0:T(8,128)S(1)}, f32[96,128]{1,0:T(8,128)S(1)}, f32[16,128]{1,0:T(8,128)S(1)}) custom-call(f32[768,128]{1,0:T(8,128)S(1)} %bitcast.18, bf16[1024,128]{1,0:T(8,128)(2,1)S(1)} %get-tuple-element.50.onehot_ref, f32[96,96,128]{2,1,0:T(8,128)S(1)} %get-tuple-element.51.precond_ref, bf16[16,128]{1,0:T(8,128)(2,1)S(1)} %get-tuple-element.52.listed_ref), custom_call_target="tpu_custom_call" | custom-call | tf_op jit(solution)/shard_map/start/pallas_call | solution.py:326
  67.0 1.3 %collective-permute-start = (f32[16,128]{1,0:T(8,128)S(1)}, f32[16,128]{1,0:T(8,128)S(1)}, u32[]{:S(2)}, u32[]{:S(2)}) collective-permute-start(f32[16,128]{1,0:T(8,128)S(1)} %get-tuple-element.55), channel_id=1, source_target_pairs={{0,1},{1,0},{2,3},{3,2},{4,5},{5,4},{6,7},{7,6},{8,9},{9,8},{10,11... | collective-permute-start | bytes 24584 | tf_op jit(solution)/shard_map/ppermute | solution.py:504
  68.4 1.9 %collective-permute-start.1 = (f32[16,128]{1,0:T(8,128)S(1)}, f32[16,128]{1,0:T(8,128)S(1)}, u32[]{:S(2)}, u32[]{:S(2)}) collective-permute-start(f32[16,128]{1,0:T(8,128)S(1)} %get-tuple-element.55), channel_id=1, source_target_pairs={{1,2},{3,4},{5,6},{7,8},{9,10},{11,12},{13,14},{15,16},{17,18},{19... | collective-permute-start | bytes 24584 | tf_op jit(solution)/shard_map/ppermute | solution.py:510
  70.3 0.0 collective-permute-done.near_ref
  70.3 1.2 %inside.4 = (f32[96,128]{1,0:T(8,128)S(1)}, f32[2,96,128]{2,1,0:T(8,128)S(1)}, f32[96,128]{1,0:T(8,128)}) custom-call(f32[3,96,96,128]{3,2,1,0:T(8,128)S(1)} %get-tuple-element.46.blocks_ref, bf16[2,128,128]{2,1,0:T(8,128)(2,1)S(1)} %get-tuple-element.47.local_ref, bf16[2,32,128]{2,1,0:T(8,128)(2,1)S(1)} %get-tuple-element.48.outer_ref, ...), custom_call_target="tpu_custom_call" | custom-call | bytes 2097152 | tf_op jit(solution)/shard_map/inside/pallas_call | solution.py:363
  71.5 1.8 %collective-permute-done.1.far_ref = f32[16,128]{1,0:T(8,128)S(1)} collective-permute-done((f32[16,128]{1,0:T(8,128)S(1)}, f32[16,128]{1,0:T(8,128)S(1)}, u32[]{:S(2)}, u32[]{:S(2)}) %collective-permute-start.1) | collective-permute-done | bytes 8224 | tf_op jit(solution)/shard_map/ppermute | solution.py:510
  73.3 1.8 %step.3 = (f32[96,128]{1,0:T(8,128)S(1)}, f32[96,128]{1,0:T(8,128)S(1)}, f32[16,128]{1,0:T(8,128)S(1)}) custom-call(f32[3,96,96,128]{3,2,1,0:T(8,128)S(1)} %get-tuple-element.46.blocks_ref, f32[96,96,128]{2,1,0:T(8,128)S(1)} %get-tuple-element.51.precond_ref, bf16[2,32,128]{2,1,0:T(8,128)(2,1)S(1)} %get-tuple-element.48.outer_ref, ...), custom_call_target="tpu_custom_call" | custom-call | tf_op jit(solution)/shard_map/step/pallas_call | solution.py:398
  75.1 0.0 collective-permute-start.2
  75.1 0.3 collective-permute-start.3
  75.4 0.9 collective-permute-done.2.near_ref
  76.3 1.2 %inside.5 = (f32[96,128]{1,0:T(8,128)S(1)}, f32[2,96,128]{2,1,0:T(8,128)S(1)}, f32[96,128]{1,0:T(8,128)}) custom-call(f32[3,96,96,128]{3,2,1,0:T(8,128)S(1)} %get-tuple-element.46.blocks_ref, bf16[2,128,128]{2,1,0:T(8,128)(2,1)S(1)} %get-tuple-element.47.local_ref, bf16[2,32,128]{2,1,0:T(8,128)(2,1)S(1)} %get-tuple-element.48.outer_ref, ...), custom_call_target="tpu_custom_call" | custom-call | bytes 2097152 | tf_op jit(solution)/shard_map/inside/pallas_call | solution.py:363
  77.5 0.8 collective-permute-done.3.far_ref
  78.2 1.8 %step.4 = (f32[96,128]{1,0:T(8,128)S(1)}, f32[96,128]{1,0:T(8,128)S(1)}, f32[16,128]{1,0:T(8,128)S(1)}) custom-call(f32[3,96,96,128]{3,2,1,0:T(8,128)S(1)} %get-tuple-element.46.blocks_ref, f32[96,96,128]{2,1,0:T(8,128)S(1)} %get-tuple-element.51.precond_ref, bf16[2,32,128]{2,1,0:T(8,128)(2,1)S(1)} %get-tuple-element.48.outer_ref, ...), custom_call_target="tpu_custom_call" | custom-call | tf_op jit(solution)/shard_map/step/pallas_call | solution.py:398
  80.0 5.9 %collective-permute-start.4 = (f32[16,128]{1,0:T(8,128)S(1)}, f32[16,128]{1,0:T(8,128)S(1)}, u32[]{:S(2)}, u32[]{:S(2)}) collective-permute-start(f32[16,128]{1,0:T(8,128)S(1)} %get-tuple-element.66), channel_id=1, source_target_pairs={{0,1},{1,0},{2,3},{3,2},{4,5},{5,4},{6,7},{7,6},{8,9},{9,8},{10,11... | collective-permute-start | bytes 24584 | tf_op jit(solution)/shard_map/ppermute | solution.py:504
  85.9 0.0 collective-permute-start.5
  85.9 0.8 collective-permute-done.4.near_ref
  86.7 1.2 %inside.6 = (f32[96,128]{1,0:T(8,128)S(1)}, f32[2,96,128]{2,1,0:T(8,128)S(1)}, f32[96,128]{1,0:T(8,128)}) custom-call(f32[3,96,96,128]{3,2,1,0:T(8,128)S(1)} %get-tuple-element.46.blocks_ref, bf16[2,128,128]{2,1,0:T(8,128)(2,1)S(1)} %get-tuple-element.47.local_ref, bf16[2,32,128]{2,1,0:T(8,128)(2,1)S(1)} %get-tuple-element.48.outer_ref, ...), custom_call_target="tpu_custom_call" | custom-call | bytes 2097152 | tf_op jit(solution)/shard_map/inside/pallas_call | solution.py:363
  87.9 1.0 collective-permute-done.5.far_ref
  89.0 1.8 %step.5 = (f32[96,128]{1,0:T(8,128)S(1)}, f32[96,128]{1,0:T(8,128)S(1)}, f32[16,128]{1,0:T(8,128)S(1)}) custom-call(f32[3,96,96,128]{3,2,1,0:T(8,128)S(1)} %get-tuple-element.46.blocks_ref, f32[96,96,128]{2,1,0:T(8,128)S(1)} %get-tuple-element.51.precond_ref, bf16[2,32,128]{2,1,0:T(8,128)(2,1)S(1)} %get-tuple-element.48.outer_ref, ...), custom_call_target="tpu_custom_call" | custom-call | tf_op jit(solution)/shard_map/step/pallas_call | solution.py:398
  90.7 5.5 %collective-permute-start.6 = (f32[16,128]{1,0:T(8,128)S(1)}, f32[16,128]{1,0:T(8,128)S(1)}, u32[]{:S(2)}, u32[]{:S(2)}) collective-permute-start(f32[16,128]{1,0:T(8,128)S(1)} %get-tuple-element.71), channel_id=1, source_target_pairs={{0,1},{1,0},{2,3},{3,2},{4,5},{5,4},{6,7},{7,6},{8,9},{9,8},{10,11... | collective-permute-start | bytes 24584 | tf_op jit(solution)/shard_map/ppermute | solution.py:504
  96.2 0.0 collective-permute-start.7
  96.2 0.8 collective-permute-done.6.near_ref
  97.1 0.8 inside.7
  97.9 1.5 %collective-permute-done.7.far_ref = f32[16,128]{1,0:T(8,128)S(1)} collective-permute-done((f32[16,128]{1,0:T(8,128)S(1)}, f32[16,128]{1,0:T(8,128)S(1)}, u32[]{:S(2)}, u32[]{:S(2)}) %collective-permute-start.7) | collective-permute-done | bytes 8224 | tf_op jit(solution)/shard_map/ppermute | solution.py:510
  99.3 1.3 %last.1 = (f32[96,128]{1,0:T(8,128)S(1)}, f32[128,128]{1,0:T(8,128)S(1)}) custom-call(f32[3,96,96,128]{3,2,1,0:T(8,128)S(1)} %get-tuple-element.46.blocks_ref, bf16[2,32,128]{2,1,0:T(8,128)(2,1)S(1)} %get-tuple-element.48.outer_ref, f32[96,128]{1,0:T(8,128)S(1)} %get-tuple-element.72.part_ref, f32[2,96,128]{2,1,0:T(8,128)S(1)} %get-tuple-element.73.taken_ref, ...), custom_call_target="tpu_custom_call" | custom-call | tf_op jit(solution)/shard_map/last/pallas_call | solution.py:421
  100.7 17.8 %all_to_all.34 = f32[128,1,128]{2,1,0:T(1,128)S(1)} all-to-all(f32[128,1,128]{2,1,0:T(1,128)S(1)} %bitcast.24), channel_id=1, replica_groups=mesh['dom'=128] {'dom'}, dimensions={0} | all-to-all | bytes 131072 | tf_op jit(solution)/shard_map/all_to_all | solution.py:514
  118.4 0.9 finish.1
Async XLA Ops:
  2.4 20.9 %all-to-all-start = ((f32[128,1,128]{2,1,0:T(1,128)}), f32[128,1,128]{2,1,0:T(1,128)S(1)}, u32[]{:S(2)}, u32[]{:S(2)}) async-start(f32[128,1,128]{2,1,0:T(1,128)} %bitcast.3), calls=%async_computation | async-start | bytes 131072 | tf_op jit(solution)/shard_map/all_to_all | solution.py:514
  67.0 3.2 %collective-permute-start = (f32[16,128]{1,0:T(8,128)S(1)}, f32[16,128]{1,0:T(8,128)S(1)}, u32[]{:S(2)}, u32[]{:S(2)}) collective-permute-start(f32[16,128]{1,0:T(8,128)S(1)} %get-tuple-element.55), channel_id=1, source_target_pairs={{0,1},{1,0},{2,3},{3,2},{4,5},{5,4},{6,7},{7,6},{8,9},{9,8},{10,11... | collective-permute-start | bytes 24584 | tf_op jit(solution)/shard_map/ppermute | solution.py:504
  68.4 5.0 %collective-permute-start.1 = (f32[16,128]{1,0:T(8,128)S(1)}, f32[16,128]{1,0:T(8,128)S(1)}, u32[]{:S(2)}, u32[]{:S(2)}) collective-permute-start(f32[16,128]{1,0:T(8,128)S(1)} %get-tuple-element.55), channel_id=1, source_target_pairs={{1,2},{3,4},{5,6},{7,8},{9,10},{11,12},{13,14},{15,16},{17,18},{19... | collective-permute-start | bytes 24584 | tf_op jit(solution)/shard_map/ppermute | solution.py:510
  75.1 1.2 collective-permute-start.2
  75.1 3.2 %collective-permute-start.3 = (f32[16,128]{1,0:T(8,128)S(1)}, f32[16,128]{1,0:T(8,128)S(1)}, u32[]{:S(2)}, u32[]{:S(2)}) collective-permute-start(f32[16,128]{1,0:T(8,128)S(1)} %get-tuple-element.61), channel_id=1, source_target_pairs={{1,2},{3,4},{5,6},{7,8},{9,10},{11,12},{13,14},{15,16},{17,18},{19... | collective-permute-start | bytes 24584 | tf_op jit(solution)/shard_map/ppermute | solution.py:510
  80.0 6.7 %collective-permute-start.4 = (f32[16,128]{1,0:T(8,128)S(1)}, f32[16,128]{1,0:T(8,128)S(1)}, u32[]{:S(2)}, u32[]{:S(2)}) collective-permute-start(f32[16,128]{1,0:T(8,128)S(1)} %get-tuple-element.66), channel_id=1, source_target_pairs={{0,1},{1,0},{2,3},{3,2},{4,5},{5,4},{6,7},{7,6},{8,9},{9,8},{10,11... | collective-permute-start | bytes 24584 | tf_op jit(solution)/shard_map/ppermute | solution.py:504
  85.9 3.1 %collective-permute-start.5 = (f32[16,128]{1,0:T(8,128)S(1)}, f32[16,128]{1,0:T(8,128)S(1)}, u32[]{:S(2)}, u32[]{:S(2)}) collective-permute-start(f32[16,128]{1,0:T(8,128)S(1)} %get-tuple-element.66), channel_id=1, source_target_pairs={{1,2},{3,4},{5,6},{7,8},{9,10},{11,12},{13,14},{15,16},{17,18},{19... | collective-permute-start | bytes 24584 | tf_op jit(solution)/shard_map/ppermute | solution.py:510
  90.7 6.3 %collective-permute-start.6 = (f32[16,128]{1,0:T(8,128)S(1)}, f32[16,128]{1,0:T(8,128)S(1)}, u32[]{:S(2)}, u32[]{:S(2)}) collective-permute-start(f32[16,128]{1,0:T(8,128)S(1)} %get-tuple-element.71), channel_id=1, source_target_pairs={{0,1},{1,0},{2,3},{3,2},{4,5},{5,4},{6,7},{7,6},{8,9},{9,8},{10,11... | collective-permute-start | bytes 24584 | tf_op jit(solution)/shard_map/ppermute | solution.py:504
  96.2 3.1 %collective-permute-start.7 = (f32[16,128]{1,0:T(8,128)S(1)}, f32[16,128]{1,0:T(8,128)S(1)}, u32[]{:S(2)}, u32[]{:S(2)}) collective-permute-start(f32[16,128]{1,0:T(8,128)S(1)} %get-tuple-element.71), channel_id=1, source_target_pairs={{1,2},{3,4},{5,6},{7,8},{9,10},{11,12},{13,14},{15,16},{17,18},{19... | collective-permute-start | bytes 24584 | tf_op jit(solution)/shard_map/ppermute | solution.py:510

commit v8 on v7

--- a/solution.py
+++ b/solution.py
@@ -130,8 +130,8 @@
 
 
 def prepare_kernel(
-    parts, halo_ref, place_ref, columns_ref, coords_ref, after_ref, fluid_ref, force_ref,
-    turned_ref, coords_out, local_ref, outer_ref, listed_ref,
+    parts, halo_ref, place_ref, columns_ref, coords_ref, slot_ref, after_ref, fluid_ref, force_ref,
+    turned_ref, chosen_ref, coords_out, local_ref, outer_ref, listed_ref,
     points, sems,
 ):
     copies = [
@@ -140,6 +140,7 @@
     ]
     for copy in copies:
         copy.start()
+    chosen_ref[...] = flag(iota(chosen_ref.shape, 0) == slot_ref[...])
     coords_out[...] = pad_rows(coords_ref[...], LANES)
     halo = listed_ref.shape[0]
     core = place_ref[0] % 2
@@ -147,10 +148,11 @@
     held = jnp.where(at_end, halo, 2 * halo)
     for neighbor in range(2):
         column = columns_ref[pl.ds(neighbor, 1), :]
-        local_ref[neighbor] = flag(iota((LANES, LANES), 0) == column)
+        lanes = pl.ds(neighbor * LANES, LANES)
+        local_ref[:, lanes] = flag(iota((LANES, LANES), 0) == column)
         outer = (column - LANES) ^ ((1 - core) * halo)
         outer = jnp.where(outer < held, outer, -1)
-        outer_ref[neighbor] = flag(iota(outer_ref.shape[1:], 0) == outer)
+        outer_ref[:, lanes] = flag(iota((2 * halo, LANES), 0) == outer)
     rows = iota(listed_ref.shape, 0)
     column = jnp.zeros(listed_ref.shape, jnp.int32)
     for h in range(listed_ref.shape[0]):
@@ -169,25 +171,26 @@
         turned_ref[group, 6] = length
 
 
-def prepare(halo_list, place, columns, coords, after, fluid, force):
+def prepare(halo_list, place, columns, coords, slot, after, fluid, force):
     count, nodes = fluid.shape[1:]
     halo = halo_list.shape[0]
     return pl.pallas_call(
         functools.partial(prepare_kernel, after.shape[0]),
         out_shape=(
             pltpu.VMEM((count // LANES, 7, nodes, LANES), F32),
+            pltpu.VMEM((after.shape[0] * CAP, count), BF16),
             pltpu.VMEM((LANES, LANES), F32),
-            pltpu.VMEM((2, LANES, LANES), BF16),
-            pltpu.VMEM((2, 2 * halo, LANES), BF16),
+            pltpu.VMEM((LANES, 2 * LANES), BF16),
+            pltpu.VMEM((2 * halo, 2 * LANES), BF16),
             pltpu.VMEM((halo, LANES), BF16),
         ),
-        in_specs=[SMEM, SMEM, VMEM, VMEM] + [ANY] * 3,
-        out_specs=[VMEM] * 5,
+        in_specs=[SMEM, SMEM, VMEM, VMEM, VMEM] + [ANY] * 3,
+        out_specs=[VMEM] * 6,
         scratch_shapes=[pltpu.VMEM((2, 3, count, nodes), F32), pltpu.SemaphoreType.DMA((2,))],
         compiler_params=limit(4),
         cost_estimate=pl.CostEstimate(flops=0, bytes_accessed=3 * MIB, transcendentals=0),
         name="prepare",
-    )(*in_hbm(halo_list, place, columns, coords, after, fluid, force))
+    )(*in_hbm(halo_list, place, columns, coords), slot, *in_hbm(after, fluid, force))
 
 
 def answer_kernel(labels_ref, coords_ref, onehot_ref, out_ref, wide):
@@ -220,7 +223,7 @@
 
 
 def transfer_kernel(
-    slot_ref, coords_ref, turned_ref, blocks_ref, precond_ref, out_ref, blocks_out, precond_out,
+    chosen_ref, coords_ref, turned_ref, blocks_ref, precond_ref, out_ref, blocks_out, precond_out,
     wide, struct, mapped, sems,
 ):
     tables = [
@@ -229,11 +232,9 @@
     ]
     for copy in tables:
         copy.start()
-    rows = wide.shape[0]
-    count = slot_ref.shape[1]
+    count = chosen_ref.shape[1]
     unpack(coords_ref, wide)
-    chosen = flag(iota((rows, count), 0) == slot_ref[...])
-    struct[...] = pick(wide[...], chosen, TN) * (1.0 / SUPPORT)
+    struct[...] = pick(wide[...], chosen_ref[...], TN) * (1.0 / SUPPORT)
     nodes = turned_ref.shape[2]
     for group in range(count // LANES):
         lanes = pl.ds(group * LANES, LANES)
@@ -260,14 +261,14 @@
         for c in range(3):
             mapped[pl.ds(c * 32, 32), lanes] = sums[c]
     mapped[pl.ds(96, 32), :] = jnp.zeros((32, count), F32)
-    wide[...] = pick_from(chosen, mapped[...])
+    wide[...] = pick_from(chosen_ref[...], mapped[...])
     pack(wide, out_ref)
     for copy in tables:
         copy.wait()
 
 
-def transfer(slot, coords, turned, blocks, precond):
-    count = slot.shape[1]
+def transfer(chosen, coords, turned, blocks, precond):
+    count = chosen.shape[1]
     return pl.pallas_call(
         transfer_kernel,
         out_shape=(
@@ -285,7 +286,7 @@
         ],
         compiler_params=limit(10),
         name="transfer",
-    )(slot, coords, *near_core(turned), *in_hbm(blocks, precond))
+    )(*near_core(chosen), coords, *near_core(turned), *in_hbm(blocks, precond))
 
 
 def times(matrices, vectors, put):
@@ -346,9 +347,8 @@
         part_ref[pl.ds(row, 1), :] = value - old_ref[pl.ds(row, 1), :]
 
     times([blocks_ref.at[0]], [pre], put)
-    for neighbor in range(2):
-        taken = pick(pre, local_ref[neighbor], NN)
-        taken_ref[neighbor] = taken + pick(near_ref[...], outer_ref[neighbor, :count, :], TN)[:size]
+    taken = pick(near_ref[...], outer_ref[:count, :], TN)[:size]
+    taken_ref[...] = taken + pick(pre, local_ref[...], NN)
     if not earlier:
         more[0][...] = old_ref[...]
     else:
@@ -362,7 +362,7 @@
     more = pltpu.VMEM((HELD, LANES), F32) if earlier else jax.ShapeDtypeStruct(old.shape, F32)
     return pl.pallas_call(
         inside_kernel,
-        out_shape=(pltpu.VMEM(old.shape, F32), pltpu.VMEM((2, size, LANES), F32), more),
+        out_shape=(pltpu.VMEM(old.shape, F32), pltpu.VMEM((size, 2 * LANES), F32), more),
         in_specs=[VMEM] * (6 + len(earlier)),
         out_specs=[VMEM] * 3,
         compiler_params=limit(6),
@@ -374,10 +374,8 @@
 def outside(blocks_ref, outer_ref, part_ref, taken_ref, far_ref, new_ref):
     size = part_ref.shape[0]
     count = far_ref.shape[0]
-    vectors = [
-        taken_ref[neighbor] + pick(far_ref[...], outer_ref[neighbor, count:, :], TN)[:size]
-        for neighbor in range(2)
-    ]
+    taken = taken_ref[...] + pick(far_ref[...], outer_ref[count:, :], TN)[:size]
+    vectors = [taken[:, :LANES], taken[:, LANES:]]
 
     def put(row, value):
         new_ref[pl.ds(row, 1), :] = value + part_ref[pl.ds(row, 1), :]
@@ -523,12 +521,12 @@
     fluid = jnp.transpose(fluid_coords, (1, 0, 2))
     coords = struct_coords.reshape(-1, struct_coords.shape[2])
     wanted, slot = slots(dest.reshape(1, -1), target.reshape(1, -1), parts)
-    turned, coords, local, outer, listed = prepare(
-        halo_list, place, columns, coords, wanted, fluid, force
+    turned, chosen, coords, local, outer, listed = prepare(
+        halo_list, place, columns, coords, slot, wanted, fluid, force
     )
     onehot, answered = answer(to_all(wanted), coords)
     answered = to_all(answered.reshape(parts, 1, -1)).reshape(answered.shape)
-    mapped, blocks, precond = transfer(slot, answered, turned, blocks, precond)
+    mapped, blocks, precond = transfer(chosen, answered, turned, blocks, precond)
     mapped = to_all(mapped.reshape(parts, 1, -1)).reshape(mapped.shape)
     load, pre, send = start(mapped, onehot, precond, listed)
     basis, pres = [load], [pre]

time: 120 us -> 120 us (level)
  no operation moved by 1% of the time
where the time goes in v8:
time: 120 us; the launch traced here: 119 us
  blocking collectives  51.2 us (43%)
  Pallas kernels  27 us (22%)
  starting transfers between devices  26.6 us (22%)
  waiting for transfers between devices  14 us (12%)
    all_to_all x3, blocking collectives, to_all(): return lax.all_to_all(x, DOM, split_axis=0, concat_axis=0, tiled=True)  51.2 us
    ppermute x4, starting transfers between devices, to_near(): return lax.ppermute(send, DOM, [(i, i ^ 1) for i in range(devices)])  12.9 us
    all_to_all x1, starting transfers between devices, to_all(): return lax.all_to_all(x, DOM, split_axis=0, concat_axis=0, tiled=True)  11.5 us
    pallas_call x1, Pallas kernels, transfer(): pl.pallas_call(transfer_kernel, out_shape=(jax.ShapeDtypeStruct(coords.sh...  8.28 us
    all_to_all x1, waiting for transfers between devices, to_all(): return lax.all_to_all(x, DOM, split_axis=0, concat_axis=0, tiled=True)  6.68 us
    pallas_call x3, Pallas kernels, step(): pl.pallas_call(step_kernel, out_shape=(shape, shape, pltpu.VMEM(far.shape...  5.34 us
    ppermute x4, waiting for transfers between devices, to_far(): return lax.ppermute(send, DOM, pairs + [(j, i) for i, j in pairs])  4.77 us
    pallas_call x4, Pallas kernels, inside(): pl.pallas_call(inside_kernel, out_shape=(pltpu.VMEM(old.shape, F32), pltp...  4.7 us
  transfers between devices with their start and end apart: 9, of which 8 were waited for; matrix products, arithmetic and copies ran while one was open for 0% of the time, Pallas kernels for 6%

profile of v8, /device:TPU:1, one launch (start us, length us, event | category | flops | bytes accessed | tf_op | source)
XLA Modules:
  0.0 119.5 jit_solution(10042595038397014209)
XLA Ops:
  0.6 1.8 %slots.1 = (f32[128,128]{1,0:T(8,128)}, s32[1,512]{1,0:T(1,128)S(1)}) custom-call(s32[1,512]{1,0:T(1,128)} %bitcast.28, s32[1,512]{1,0:T(1,128)} %bitcast.29), custom_call_target="tpu_custom_call" | custom-call | tf_op jit(solution)/shard_map/slots/pallas_call | solution.py:121
  2.4 11.5 %all-to-all-start = ((f32[128,1,128]{2,1,0:T(1,128)}), f32[128,1,128]{2,1,0:T(1,128)S(1)}, u32[]{:S(2)}, u32[]{:S(2)}) async-start(f32[128,1,128]{2,1,0:T(1,128)} %bitcast.7), calls=%async_computation | async-start | bytes 131072 | tf_op jit(solution)/shard_map/all_to_all | solution.py:512
  13.9 2.7 %prepare.1 = (f32[4,7,128,128]{3,2,1,0:T(8,128)S(1)}, bf16[1024,512]{1,0:T(8,128)(2,1)S(1)}, f32[128,128]{1,0:T(8,128)S(1)}, bf16[128,256]{1,0:T(8,128)(2,1)S(1)...) custom-call(s32[16]{0:T(128)} %halo_ref.1, s32[1]{0:T(128)} %bitcast.place_ref, s32[2,128]{1,0:T(2,128)} %columns_ref.1, ...), custom_call_target="tpu_custom_call" | custom-call | bytes 3145728 | tf_op jit(solution)/shard_map/prepare/pallas_call | solution.py:177
  16.6 6.7 %all-to-all-done = f32[128,1,128]{2,1,0:T(1,128)S(1)} async-done(((f32[128,1,128]{2,1,0:T(1,128)}), f32[128,1,128]{2,1,0:T(1,128)S(1)}, u32[]{:S(2)}, u32[]{:S(2)}) %all-to-all-start) | async-done | bytes 65568 | tf_op jit(solution)/shard_map/all_to_all | solution.py:512
  23.3 0.8 answer.1
  24.1 16.7 %all_to_all.32 = f32[128,1,768]{2,1,0:T(1,128)S(1)} all-to-all(f32[128,1,768]{2,1,0:T(1,128)S(1)} %bitcast.21), channel_id=1, replica_groups=mesh['dom'=128] {'dom'}, dimensions={0} | all-to-all | bytes 786432 | tf_op jit(solution)/shard_map/all_to_all | solution.py:512
  40.8 8.3 %transfer.1 = (f32[768,128]{1,0:T(8,128)S(1)}, f32[3,96,96,128]{3,2,1,0:T(8,128)S(1)}, f32[96,96,128]{2,1,0:T(8,128)S(1)}) custom-call(bf16[1024,512]{1,0:T(8,128)(2,1)S(1)} %get-tuple-element.44.chosen_ref, f32[768,128]{1,0:T(8,128)S(1)} %bitcast.19, f32[4,7,128,128]{3,2,1,0:T(8,128)S(1)} %get-tuple-element.47.turned_ref, f32[3,96,96,128]{3,2,1,0:T(8,128)} %blocks_ref.1, ...), custom_call_target="tpu_custom_call" | custom-call | tf_op jit(solution)/shard_map/transfer/pallas_call | solution.py:272
  49.0 16.7 %all_to_all.33 = f32[128,1,768]{2,1,0:T(1,128)S(1)} all-to-all(f32[128,1,768]{2,1,0:T(1,128)S(1)} %bitcast.20), channel_id=1, replica_groups=mesh['dom'=128] {'dom'}, dimensions={0} | all-to-all | bytes 786432 | tf_op jit(solution)/shard_map/all_to_all | solution.py:512
  65.7 1.3 %start.1 = (f32[96,128]{1,0:T(8,128)S(1)}, f32[96,128]{1,0:T(8,128)S(1)}, f32[16,128]{1,0:T(8,128)S(1)}) custom-call(f32[768,128]{1,0:T(8,128)S(1)} %bitcast.18, bf16[1024,128]{1,0:T(8,128)(2,1)S(1)} %get-tuple-element.52.onehot_ref, f32[96,96,128]{2,1,0:T(8,128)S(1)} %get-tuple-element.53.precond_ref, bf16[16,128]{1,0:T(8,128)(2,1)S(1)} %get-tuple-element.54.listed_ref), custom_call_target="tpu_custom_call" | custom-call | tf_op jit(solution)/shard_map/start/pallas_call | solution.py:327
  67.0 1.3 %collective-permute-start = (f32[16,128]{1,0:T(8,128)S(1)}, f32[16,128]{1,0:T(8,128)S(1)}, u32[]{:S(2)}, u32[]{:S(2)}) collective-permute-start(f32[16,128]{1,0:T(8,128)S(1)} %get-tuple-element.57), channel_id=1, source_target_pairs={{0,1},{1,0},{2,3},{3,2},{4,5},{5,4},{6,7},{7,6},{8,9},{9,8},{10,11... | collective-permute-start | bytes 24584 | tf_op jit(solution)/shard_map/ppermute | solution.py:502
  68.3 1.9 %collective-permute-start.1 = (f32[16,128]{1,0:T(8,128)S(1)}, f32[16,128]{1,0:T(8,128)S(1)}, u32[]{:S(2)}, u32[]{:S(2)}) collective-permute-start(f32[16,128]{1,0:T(8,128)S(1)} %get-tuple-element.57), channel_id=1, source_target_pairs={{1,2},{3,4},{5,6},{7,8},{9,10},{11,12},{13,14},{15,16},{17,18},{19... | collective-permute-start | bytes 24584 | tf_op jit(solution)/shard_map/ppermute | solution.py:508
  70.2 0.0 collective-permute-done.near_ref
  70.2 1.3 %inside.4 = (f32[96,128]{1,0:T(8,128)S(1)}, f32[96,256]{1,0:T(8,128)S(1)}, f32[96,128]{1,0:T(8,128)}) custom-call(f32[3,96,96,128]{3,2,1,0:T(8,128)S(1)} %get-tuple-element.48.blocks_ref, bf16[128,256]{1,0:T(8,128)(2,1)S(1)} %get-tuple-element.49.local_ref, bf16[32,256]{1,0:T(8,128)(2,1)S(1)} %get-tuple-element.50.outer_ref, ...), custom_call_target="tpu_custom_call" | custom-call | bytes 2097152 | tf_op jit(solution)/shard_map/inside/pallas_call | solution.py:363
  71.5 1.7 %collective-permute-done.1.far_ref = f32[16,128]{1,0:T(8,128)S(1)} collective-permute-done((f32[16,128]{1,0:T(8,128)S(1)}, f32[16,128]{1,0:T(8,128)S(1)}, u32[]{:S(2)}, u32[]{:S(2)}) %collective-permute-start.1) | collective-permute-done | bytes 8224 | tf_op jit(solution)/shard_map/ppermute | solution.py:508
  73.3 1.8 %step.3 = (f32[96,128]{1,0:T(8,128)S(1)}, f32[96,128]{1,0:T(8,128)S(1)}, f32[16,128]{1,0:T(8,128)S(1)}) custom-call(f32[3,96,96,128]{3,2,1,0:T(8,128)S(1)} %get-tuple-element.48.blocks_ref, f32[96,96,128]{2,1,0:T(8,128)S(1)} %get-tuple-element.53.precond_ref, bf16[32,256]{1,0:T(8,128)(2,1)S(1)} %get-tuple-element.50.outer_ref, ...), custom_call_target="tpu_custom_call" | custom-call | tf_op jit(solution)/shard_map/step/pallas_call | solution.py:396
  75.1 0.0 collective-permute-start.2
  75.1 0.3 collective-permute-start.3
  75.4 0.9 collective-permute-done.2.near_ref
  76.3 1.3 %inside.5 = (f32[96,128]{1,0:T(8,128)S(1)}, f32[96,256]{1,0:T(8,128)S(1)}, f32[96,128]{1,0:T(8,128)}) custom-call(f32[3,96,96,128]{3,2,1,0:T(8,128)S(1)} %get-tuple-element.48.blocks_ref, bf16[128,256]{1,0:T(8,128)(2,1)S(1)} %get-tuple-element.49.local_ref, bf16[32,256]{1,0:T(8,128)(2,1)S(1)} %get-tuple-element.50.outer_ref, ...), custom_call_target="tpu_custom_call" | custom-call | bytes 2097152 | tf_op jit(solution)/shard_map/inside/pallas_call | solution.py:363
  77.6 0.7 collective-permute-done.3.far_ref
  78.3 1.8 %step.4 = (f32[96,128]{1,0:T(8,128)S(1)}, f32[96,128]{1,0:T(8,128)S(1)}, f32[16,128]{1,0:T(8,128)S(1)}) custom-call(f32[3,96,96,128]{3,2,1,0:T(8,128)S(1)} %get-tuple-element.48.blocks_ref, f32[96,96,128]{2,1,0:T(8,128)S(1)} %get-tuple-element.53.precond_ref, bf16[32,256]{1,0:T(8,128)(2,1)S(1)} %get-tuple-element.50.outer_ref, ...), custom_call_target="tpu_custom_call" | custom-call | tf_op jit(solution)/shard_map/step/pallas_call | solution.py:396
  80.0 6.0 %collective-permute-start.4 = (f32[16,128]{1,0:T(8,128)S(1)}, f32[16,128]{1,0:T(8,128)S(1)}, u32[]{:S(2)}, u32[]{:S(2)}) collective-permute-start(f32[16,128]{1,0:T(8,128)S(1)} %get-tuple-element.68), channel_id=1, source_target_pairs={{0,1},{1,0},{2,3},{3,2},{4,5},{5,4},{6,7},{7,6},{8,9},{9,8},{10,11... | collective-permute-start | bytes 24584 | tf_op jit(solution)/shard_map/ppermute | solution.py:502
  86.0 0.0 collective-permute-start.5
  86.0 0.8 collective-permute-done.4.near_ref
  86.8 1.3 %inside.6 = (f32[96,128]{1,0:T(8,128)S(1)}, f32[96,256]{1,0:T(8,128)S(1)}, f32[96,128]{1,0:T(8,128)}) custom-call(f32[3,96,96,128]{3,2,1,0:T(8,128)S(1)} %get-tuple-element.48.blocks_ref, bf16[128,256]{1,0:T(8,128)(2,1)S(1)} %get-tuple-element.49.local_ref, bf16[32,256]{1,0:T(8,128)(2,1)S(1)} %get-tuple-element.50.outer_ref, ...), custom_call_target="tpu_custom_call" | custom-call | bytes 2097152 | tf_op jit(solution)/shard_map/inside/pallas_call | solution.py:363
  88.1 1.0 collective-permute-done.5.far_ref
  89.1 1.8 %step.5 = (f32[96,128]{1,0:T(8,128)S(1)}, f32[96,128]{1,0:T(8,128)S(1)}, f32[16,128]{1,0:T(8,128)S(1)}) custom-call(f32[3,96,96,128]{3,2,1,0:T(8,128)S(1)} %get-tuple-element.48.blocks_ref, f32[96,96,128]{2,1,0:T(8,128)S(1)} %get-tuple-element.53.precond_ref, bf16[32,256]{1,0:T(8,128)(2,1)S(1)} %get-tuple-element.50.outer_ref, ...), custom_call_target="tpu_custom_call" | custom-call | tf_op jit(solution)/shard_map/step/pallas_call | solution.py:396
  90.9 5.5 %collective-permute-start.6 = (f32[16,128]{1,0:T(8,128)S(1)}, f32[16,128]{1,0:T(8,128)S(1)}, u32[]{:S(2)}, u32[]{:S(2)}) collective-permute-start(f32[16,128]{1,0:T(8,128)S(1)} %get-tuple-element.73), channel_id=1, source_target_pairs={{0,1},{1,0},{2,3},{3,2},{4,5},{5,4},{6,7},{7,6},{8,9},{9,8},{10,11... | collective-permute-start | bytes 24584 | tf_op jit(solution)/shard_map/ppermute | solution.py:502
  96.4 0.0 collective-permute-start.7
  96.4 0.8 collective-permute-done.6.near_ref
  97.2 0.8 inside.7
  98.0 1.4 %collective-permute-done.7.far_ref = f32[16,128]{1,0:T(8,128)S(1)} collective-permute-done((f32[16,128]{1,0:T(8,128)S(1)}, f32[16,128]{1,0:T(8,128)S(1)}, u32[]{:S(2)}, u32[]{:S(2)}) %collective-permute-start.7) | collective-permute-done | bytes 8224 | tf_op jit(solution)/shard_map/ppermute | solution.py:508
  99.5 1.4 %last.1 = (f32[96,128]{1,0:T(8,128)S(1)}, f32[128,128]{1,0:T(8,128)S(1)}) custom-call(f32[3,96,96,128]{3,2,1,0:T(8,128)S(1)} %get-tuple-element.48.blocks_ref, bf16[32,256]{1,0:T(8,128)(2,1)S(1)} %get-tuple-element.50.outer_ref, f32[96,128]{1,0:T(8,128)S(1)} %get-tuple-element.74.part_ref, f32[96,256]{1,0:T(8,128)S(1)} %get-tuple-element.75.taken_ref, ...), custom_call_target="tpu_custom_call" | custom-call | tf_op jit(solution)/shard_map/last/pallas_call | solution.py:419
  100.8 17.8 %all_to_all.34 = f32[128,1,128]{2,1,0:T(1,128)S(1)} all-to-all(f32[128,1,128]{2,1,0:T(1,128)S(1)} %bitcast.24), channel_id=1, replica_groups=mesh['dom'=128] {'dom'}, dimensions={0} | all-to-all | bytes 131072 | tf_op jit(solution)/shard_map/all_to_all | solution.py:512
  118.6 0.9 finish.1
Async XLA Ops:
  2.4 20.9 %all-to-all-start = ((f32[128,1,128]{2,1,0:T(1,128)}), f32[128,1,128]{2,1,0:T(1,128)S(1)}, u32[]{:S(2)}, u32[]{:S(2)}) async-start(f32[128,1,128]{2,1,0:T(1,128)} %bitcast.7), calls=%async_computation | async-start | bytes 131072 | tf_op jit(solution)/shard_map/all_to_all | solution.py:512
  67.0 3.2 %collective-permute-start = (f32[16,128]{1,0:T(8,128)S(1)}, f32[16,128]{1,0:T(8,128)S(1)}, u32[]{:S(2)}, u32[]{:S(2)}) collective-permute-start(f32[16,128]{1,0:T(8,128)S(1)} %get-tuple-element.57), channel_id=1, source_target_pairs={{0,1},{1,0},{2,3},{3,2},{4,5},{5,4},{6,7},{7,6},{8,9},{9,8},{10,11... | collective-permute-start | bytes 24584 | tf_op jit(solution)/shard_map/ppermute | solution.py:502
  68.3 5.0 %collective-permute-start.1 = (f32[16,128]{1,0:T(8,128)S(1)}, f32[16,128]{1,0:T(8,128)S(1)}, u32[]{:S(2)}, u32[]{:S(2)}) collective-permute-start(f32[16,128]{1,0:T(8,128)S(1)} %get-tuple-element.57), channel_id=1, source_target_pairs={{1,2},{3,4},{5,6},{7,8},{9,10},{11,12},{13,14},{15,16},{17,18},{19... | collective-permute-start | bytes 24584 | tf_op jit(solution)/shard_map/ppermute | solution.py:508
  75.1 1.2 %collective-permute-start.2 = (f32[16,128]{1,0:T(8,128)S(1)}, f32[16,128]{1,0:T(8,128)S(1)}, u32[]{:S(2)}, u32[]{:S(2)}) collective-permute-start(f32[16,128]{1,0:T(8,128)S(1)} %get-tuple-element.63), channel_id=1, source_target_pairs={{0,1},{1,0},{2,3},{3,2},{4,5},{5,4},{6,7},{7,6},{8,9},{9,8},{10,11... | collective-permute-start | bytes 24584 | tf_op jit(solution)/shard_map/ppermute | solution.py:502
  75.1 3.2 %collective-permute-start.3 = (f32[16,128]{1,0:T(8,128)S(1)}, f32[16,128]{1,0:T(8,128)S(1)}, u32[]{:S(2)}, u32[]{:S(2)}) collective-permute-start(f32[16,128]{1,0:T(8,128)S(1)} %get-tuple-element.63), channel_id=1, source_target_pairs={{1,2},{3,4},{5,6},{7,8},{9,10},{11,12},{13,14},{15,16},{17,18},{19... | collective-permute-start | bytes 24584 | tf_op jit(solution)/shard_map/ppermute | solution.py:508
  80.0 6.8 %collective-permute-start.4 = (f32[16,128]{1,0:T(8,128)S(1)}, f32[16,128]{1,0:T(8,128)S(1)}, u32[]{:S(2)}, u32[]{:S(2)}) collective-permute-start(f32[16,128]{1,0:T(8,128)S(1)} %get-tuple-element.68), channel_id=1, source_target_pairs={{0,1},{1,0},{2,3},{3,2},{4,5},{5,4},{6,7},{7,6},{8,9},{9,8},{10,11... | collective-permute-start | bytes 24584 | tf_op jit(solution)/shard_map/ppermute | solution.py:502
  86.0 3.1 %collective-permute-start.5 = (f32[16,128]{1,0:T(8,128)S(1)}, f32[16,128]{1,0:T(8,128)S(1)}, u32[]{:S(2)}, u32[]{:S(2)}) collective-permute-start(f32[16,128]{1,0:T(8,128)S(1)} %get-tuple-element.68), channel_id=1, source_target_pairs={{1,2},{3,4},{5,6},{7,8},{9,10},{11,12},{13,14},{15,16},{17,18},{19... | collective-permute-start | bytes 24584 | tf_op jit(solution)/shard_map/ppermute | solution.py:508
  90.9 6.4 %collective-permute-start.6 = (f32[16,128]{1,0:T(8,128)S(1)}, f32[16,128]{1,0:T(8,128)S(1)}, u32[]{:S(2)}, u32[]{:S(2)}) collective-permute-start(f32[16,128]{1,0:T(8,128)S(1)} %get-tuple-element.73), channel_id=1, source_target_pairs={{0,1},{1,0},{2,3},{3,2},{4,5},{5,4},{6,7},{7,6},{8,9},{9,8},{10,11... | collective-permute-start | bytes 24584 | tf_op jit(solution)/shard_map/ppermute | solution.py:502
  96.4 3.1 %collective-permute-start.7 = (f32[16,128]{1,0:T(8,128)S(1)}, f32[16,128]{1,0:T(8,128)S(1)}, u32[]{:S(2)}, u32[]{:S(2)}) collective-permute-start(f32[16,128]{1,0:T(8,128)S(1)} %get-tuple-element.73), channel_id=1, source_target_pairs={{1,2},{3,4},{5,6},{7,8},{9,10},{11,12},{13,14},{15,16},{17,18},{19... | collective-permute-start | bytes 24584 | tf_op jit(solution)/shard_map/ppermute | solution.py:508

commit v9 on v7

--- a/solution.py
+++ b/solution.py
@@ -14,6 +14,7 @@
 STEPS = 4
 KNOWN = [(i, j) for j in range(STEPS) for i in range(j + 1)]
 HELD = 16
+UNROLL = 24
 F32 = jnp.float32
 BF16 = jnp.bfloat16
 NN = (((1,), (0,)), ((), ()))
@@ -107,9 +108,15 @@
     count = dest.shape[1]
     parts = labels_ref.shape[0]
     hits = flag(iota((parts, count), 0) == dest)
-    earlier = flag(iota((count, count), 0) < iota((count, count), 1))
-    running = dot(hits, earlier, NN)
-    before = jnp.sum(running * hits.astype(F32), axis=0, keepdims=True)
+    earlier = flag(iota((LANES, LANES), 0) < iota((LANES, LANES), 1))
+    passed = jnp.zeros((parts, LANES), F32)
+    before = []
+    for chunk in range(count // LANES):
+        own = hits[:, chunk * LANES : (chunk + 1) * LANES]
+        running = dot(own, earlier, NN) + passed
+        before.append(jnp.sum(running * own.astype(F32), axis=0, keepdims=True))
+        passed = passed + dot(own, jnp.ones((LANES, LANES), BF16), NN)
+    before = jnp.concatenate(before, axis=1)
     slot_ref[...] = dest * CAP + before.astype(jnp.int32)
     place = iota((LANES, count), 0).astype(F32)
     wanted = jnp.where(place == before, (target_ref[...] + 1).astype(F32), 0.0)
@@ -292,8 +299,8 @@
     rows = vectors[0].shape[0]
 
     def body(step, carry):
-        for k in range(8):
-            row = step * 8 + k
+        for k in range(UNROLL):
+            row = step * UNROLL + k
             total = None
             for matrix, vector in zip(matrices, vectors):
                 term = matrix[row] * vector
@@ -301,7 +308,7 @@
             put(row, jnp.sum(total, axis=0, keepdims=True))
         return carry
 
-    lax.fori_loop(0, rows // 8, body, 0)
+    lax.fori_loop(0, rows // UNROLL, body, 0)
 
 
 def precondition(precond_ref, listed_ref, vector, out_ref, send_ref):

time: 120 us -> 119 us (level)
  Pallas kernels: 26.7 us -> 25.4 us
where the time goes in v9:
time: 119 us; the launch traced here: 118 us
  blocking collectives  51.2 us (43%)
  starting transfers between devices  26.4 us (22%)
  Pallas kernels  25.4 us (21%)
  waiting for transfers between devices  14.7 us (12%)
    all_to_all x3, blocking collectives, to_all(): return lax.all_to_all(x, DOM, split_axis=0, concat_axis=0, tiled=True)  51.2 us
    ppermute x4, starting transfers between devices, to_near(): return lax.ppermute(send, DOM, [(i, i ^ 1) for i in range(devices)])  12.7 us
    all_to_all x1, starting transfers between devices, to_all(): return lax.all_to_all(x, DOM, split_axis=0, concat_axis=0, tiled=True)  11.5 us
    pallas_call x1, Pallas kernels, transfer(): pl.pallas_call(transfer_kernel, out_shape=(jax.ShapeDtypeStruct(coords.sh...  8.3 us
    all_to_all x1, waiting for transfers between devices, to_all(): return lax.all_to_all(x, DOM, split_axis=0, concat_axis=0, tiled=True)  6.68 us
    ppermute x4, waiting for transfers between devices, to_far(): return lax.ppermute(send, DOM, pairs + [(j, i) for i, j in pairs])  5.49 us
    pallas_call x3, Pallas kernels, step(): pl.pallas_call(step_kernel, out_shape=(shape, shape, pltpu.VMEM(far.shape...  4.65 us
    pallas_call x4, Pallas kernels, inside(): pl.pallas_call(inside_kernel, out_shape=(pltpu.VMEM(old.shape, F32), pltp...  4 us
  transfers between devices with their start and end apart: 9, of which 8 were waited for; matrix products, arithmetic and copies ran while one was open for 0% of the time, Pallas kernels for 6%

profile of v9, /device:TPU:1, one launch (start us, length us, event | category | flops | bytes accessed | tf_op | source)
XLA Modules:
  0.0 118.4 jit_solution(13057076447438044390)
XLA Ops:
  0.6 1.7 %slots.1 = (f32[128,128]{1,0:T(8,128)}, s32[1,512]{1,0:T(1,128)S(1)}) custom-call(s32[1,512]{1,0:T(1,128)} %bitcast.28, s32[1,512]{1,0:T(1,128)} %bitcast.29), custom_call_target="tpu_custom_call" | custom-call | tf_op jit(solution)/shard_map/slots/pallas_call | solution.py:128
  2.4 11.5 %all-to-all-start = ((f32[128,1,128]{2,1,0:T(1,128)}), f32[128,1,128]{2,1,0:T(1,128)S(1)}, u32[]{:S(2)}, u32[]{:S(2)}) async-start(f32[128,1,128]{2,1,0:T(1,128)} %bitcast.3), calls=%async_computation | async-start | bytes 131072 | tf_op jit(solution)/shard_map/all_to_all | solution.py:521
  13.8 2.7 %prepare.1 = (f32[4,7,128,128]{3,2,1,0:T(8,128)S(1)}, f32[128,128]{1,0:T(8,128)S(1)}, bf16[2,128,128]{2,1,0:T(8,128)(2,1)S(1)}, bf16[2,32,128]{2,1,0:T(8,128)(2,1)S(1)}, bf16[16,128]{1,0:T(8,128)(2,1)S(1)}) custom-call(s32[16]{0:T(128)} %halo_ref.1, s32[1]{0:T(128)} %bitcast.5.place_ref, s32[2,128]{1,0:T(2,128)} %columns_ref.1, f32[96,128]{1,0:T(8,128)} %bitcast.27, ...), custom_call_target="tpu_custom_call" | custom-call | bytes 3145728 | tf_op jit(solution)/shard_map/prepare/pallas_call | solution.py:182
  16.5 6.7 %all-to-all-done = f32[128,1,128]{2,1,0:T(1,128)S(1)} async-done(((f32[128,1,128]{2,1,0:T(1,128)}), f32[128,1,128]{2,1,0:T(1,128)S(1)}, u32[]{:S(2)}, u32[]{:S(2)}) %all-to-all-start) | async-done | bytes 65568 | tf_op jit(solution)/shard_map/all_to_all | solution.py:521
  23.2 0.8 answer.1
  24.0 16.7 %all_to_all.32 = f32[128,1,768]{2,1,0:T(1,128)S(1)} all-to-all(f32[128,1,768]{2,1,0:T(1,128)S(1)} %bitcast.21), channel_id=1, replica_groups=mesh['dom'=128] {'dom'}, dimensions={0} | all-to-all | bytes 786432 | tf_op jit(solution)/shard_map/all_to_all | solution.py:521
  40.7 8.3 %transfer.1 = (f32[768,128]{1,0:T(8,128)S(1)}, f32[3,96,96,128]{3,2,1,0:T(8,128)S(1)}, f32[96,96,128]{2,1,0:T(8,128)S(1)}) custom-call(s32[1,512]{1,0:T(1,128)S(1)} %get-tuple-element.41.slot_ref, f32[768,128]{1,0:T(8,128)S(1)} %bitcast.19, f32[4,7,128,128]{3,2,1,0:T(8,128)S(1)} %get-tuple-element.45.turned_ref, f32[3,96,96,128]{3,2,1,0:T(8,128)} %blocks_ref.1, ...), custom_call_target="tpu_custom_call" | custom-call | tf_op jit(solution)/shard_map/transfer/pallas_call | solution.py:278
  49.0 16.7 %all_to_all.33 = f32[128,1,768]{2,1,0:T(1,128)S(1)} all-to-all(f32[128,1,768]{2,1,0:T(1,128)S(1)} %bitcast.20), channel_id=1, replica_groups=mesh['dom'=128] {'dom'}, dimensions={0} | all-to-all | bytes 786432 | tf_op jit(solution)/shard_map/all_to_all | solution.py:521
  65.7 1.2 start.1
  66.9 1.3 %collective-permute-start = (f32[16,128]{1,0:T(8,128)S(1)}, f32[16,128]{1,0:T(8,128)S(1)}, u32[]{:S(2)}, u32[]{:S(2)}) collective-permute-start(f32[16,128]{1,0:T(8,128)S(1)} %get-tuple-element.55), channel_id=1, source_target_pairs={{0,1},{1,0},{2,3},{3,2},{4,5},{5,4},{6,7},{7,6},{8,9},{9,8},{10,11... | collective-permute-start | bytes 24584 | tf_op jit(solution)/shard_map/ppermute | solution.py:511
  68.2 1.9 %collective-permute-start.1 = (f32[16,128]{1,0:T(8,128)S(1)}, f32[16,128]{1,0:T(8,128)S(1)}, u32[]{:S(2)}, u32[]{:S(2)}) collective-permute-start(f32[16,128]{1,0:T(8,128)S(1)} %get-tuple-element.55), channel_id=1, source_target_pairs={{1,2},{3,4},{5,6},{7,8},{9,10},{11,12},{13,14},{15,16},{17,18},{19... | collective-permute-start | bytes 24584 | tf_op jit(solution)/shard_map/ppermute | solution.py:517
  70.1 0.0 collective-permute-done.near_ref
  70.1 1.1 inside.4
  71.2 1.9 %collective-permute-done.1.far_ref = f32[16,128]{1,0:T(8,128)S(1)} collective-permute-done((f32[16,128]{1,0:T(8,128)S(1)}, f32[16,128]{1,0:T(8,128)S(1)}, u32[]{:S(2)}, u32[]{:S(2)}) %collective-permute-start.1) | collective-permute-done | bytes 8224 | tf_op jit(solution)/shard_map/ppermute | solution.py:517
  73.2 1.5 %step.3 = (f32[96,128]{1,0:T(8,128)S(1)}, f32[96,128]{1,0:T(8,128)S(1)}, f32[16,128]{1,0:T(8,128)S(1)}) custom-call(f32[3,96,96,128]{3,2,1,0:T(8,128)S(1)} %get-tuple-element.46.blocks_ref, f32[96,96,128]{2,1,0:T(8,128)S(1)} %get-tuple-element.51.precond_ref, bf16[2,32,128]{2,1,0:T(8,128)(2,1)S(1)} %get-tuple-element.48.outer_ref, ...), custom_call_target="tpu_custom_call" | custom-call | tf_op jit(solution)/shard_map/step/pallas_call | solution.py:405
  74.7 0.0 collective-permute-start.2
  74.7 0.3 collective-permute-start.3
  75.0 0.9 collective-permute-done.2.near_ref
  75.9 1.1 inside.5
  77.0 0.9 collective-permute-done.3.far_ref
  77.9 1.5 %step.4 = (f32[96,128]{1,0:T(8,128)S(1)}, f32[96,128]{1,0:T(8,128)S(1)}, f32[16,128]{1,0:T(8,128)S(1)}) custom-call(f32[3,96,96,128]{3,2,1,0:T(8,128)S(1)} %get-tuple-element.46.blocks_ref, f32[96,96,128]{2,1,0:T(8,128)S(1)} %get-tuple-element.51.precond_ref, bf16[2,32,128]{2,1,0:T(8,128)(2,1)S(1)} %get-tuple-element.48.outer_ref, ...), custom_call_target="tpu_custom_call" | custom-call | tf_op jit(solution)/shard_map/step/pallas_call | solution.py:405
  79.4 5.9 %collective-permute-start.4 = (f32[16,128]{1,0:T(8,128)S(1)}, f32[16,128]{1,0:T(8,128)S(1)}, u32[]{:S(2)}, u32[]{:S(2)}) collective-permute-start(f32[16,128]{1,0:T(8,128)S(1)} %get-tuple-element.66), channel_id=1, source_target_pairs={{0,1},{1,0},{2,3},{3,2},{4,5},{5,4},{6,7},{7,6},{8,9},{9,8},{10,11... | collective-permute-start | bytes 24584 | tf_op jit(solution)/shard_map/ppermute | solution.py:511
  85.3 0.0 collective-permute-start.5
  85.3 0.8 collective-permute-done.4.near_ref
  86.1 1.1 inside.6
  87.3 1.1 collective-permute-done.5.far_ref
  88.4 1.6 %step.5 = (f32[96,128]{1,0:T(8,128)S(1)}, f32[96,128]{1,0:T(8,128)S(1)}, f32[16,128]{1,0:T(8,128)S(1)}) custom-call(f32[3,96,96,128]{3,2,1,0:T(8,128)S(1)} %get-tuple-element.46.blocks_ref, f32[96,96,128]{2,1,0:T(8,128)S(1)} %get-tuple-element.51.precond_ref, bf16[2,32,128]{2,1,0:T(8,128)(2,1)S(1)} %get-tuple-element.48.outer_ref, ...), custom_call_target="tpu_custom_call" | custom-call | tf_op jit(solution)/shard_map/step/pallas_call | solution.py:405
  89.9 5.5 %collective-permute-start.6 = (f32[16,128]{1,0:T(8,128)S(1)}, f32[16,128]{1,0:T(8,128)S(1)}, u32[]{:S(2)}, u32[]{:S(2)}) collective-permute-start(f32[16,128]{1,0:T(8,128)S(1)} %get-tuple-element.71), channel_id=1, source_target_pairs={{0,1},{1,0},{2,3},{3,2},{4,5},{5,4},{6,7},{7,6},{8,9},{9,8},{10,11... | collective-permute-start | bytes 24584 | tf_op jit(solution)/shard_map/ppermute | solution.py:511
  95.5 0.0 collective-permute-start.7
  95.5 0.8 collective-permute-done.6.near_ref
  96.3 0.7 inside.7
  97.0 1.6 %collective-permute-done.7.far_ref = f32[16,128]{1,0:T(8,128)S(1)} collective-permute-done((f32[16,128]{1,0:T(8,128)S(1)}, f32[16,128]{1,0:T(8,128)S(1)}, u32[]{:S(2)}, u32[]{:S(2)}) %collective-permute-start.7) | collective-permute-done | bytes 8224 | tf_op jit(solution)/shard_map/ppermute | solution.py:517
  98.5 1.2 %last.1 = (f32[96,128]{1,0:T(8,128)S(1)}, f32[128,128]{1,0:T(8,128)S(1)}) custom-call(f32[3,96,96,128]{3,2,1,0:T(8,128)S(1)} %get-tuple-element.46.blocks_ref, bf16[2,32,128]{2,1,0:T(8,128)(2,1)S(1)} %get-tuple-element.48.outer_ref, f32[96,128]{1,0:T(8,128)S(1)} %get-tuple-element.72.part_ref, f32[2,96,128]{2,1,0:T(8,128)S(1)} %get-tuple-element.73.taken_ref, ...), custom_call_target="tpu_custom_call" | custom-call | tf_op jit(solution)/shard_map/last/pallas_call | solution.py:428
  99.8 17.8 %all_to_all.34 = f32[128,1,128]{2,1,0:T(1,128)S(1)} all-to-all(f32[128,1,128]{2,1,0:T(1,128)S(1)} %bitcast.24), channel_id=1, replica_groups=mesh['dom'=128] {'dom'}, dimensions={0} | all-to-all | bytes 131072 | tf_op jit(solution)/shard_map/all_to_all | solution.py:521
  117.5 0.9 finish.1
Async XLA Ops:
  2.4 20.9 %all-to-all-start = ((f32[128,1,128]{2,1,0:T(1,128)}), f32[128,1,128]{2,1,0:T(1,128)S(1)}, u32[]{:S(2)}, u32[]{:S(2)}) async-start(f32[128,1,128]{2,1,0:T(1,128)} %bitcast.3), calls=%async_computation | async-start | bytes 131072 | tf_op jit(solution)/shard_map/all_to_all | solution.py:521
  66.9 3.2 %collective-permute-start = (f32[16,128]{1,0:T(8,128)S(1)}, f32[16,128]{1,0:T(8,128)S(1)}, u32[]{:S(2)}, u32[]{:S(2)}) collective-permute-start(f32[16,128]{1,0:T(8,128)S(1)} %get-tuple-element.55), channel_id=1, source_target_pairs={{0,1},{1,0},{2,3},{3,2},{4,5},{5,4},{6,7},{7,6},{8,9},{9,8},{10,11... | collective-permute-start | bytes 24584 | tf_op jit(solution)/shard_map/ppermute | solution.py:511
  68.2 5.0 %collective-permute-start.1 = (f32[16,128]{1,0:T(8,128)S(1)}, f32[16,128]{1,0:T(8,128)S(1)}, u32[]{:S(2)}, u32[]{:S(2)}) collective-permute-start(f32[16,128]{1,0:T(8,128)S(1)} %get-tuple-element.55), channel_id=1, source_target_pairs={{1,2},{3,4},{5,6},{7,8},{9,10},{11,12},{13,14},{15,16},{17,18},{19... | collective-permute-start | bytes 24584 | tf_op jit(solution)/shard_map/ppermute | solution.py:517
  74.7 1.2 %collective-permute-start.2 = (f32[16,128]{1,0:T(8,128)S(1)}, f32[16,128]{1,0:T(8,128)S(1)}, u32[]{:S(2)}, u32[]{:S(2)}) collective-permute-start(f32[16,128]{1,0:T(8,128)S(1)} %get-tuple-element.61), channel_id=1, source_target_pairs={{0,1},{1,0},{2,3},{3,2},{4,5},{5,4},{6,7},{7,6},{8,9},{9,8},{10,11... | collective-permute-start | bytes 24584 | tf_op jit(solution)/shard_map/ppermute | solution.py:511
  74.7 3.2 %collective-permute-start.3 = (f32[16,128]{1,0:T(8,128)S(1)}, f32[16,128]{1,0:T(8,128)S(1)}, u32[]{:S(2)}, u32[]{:S(2)}) collective-permute-start(f32[16,128]{1,0:T(8,128)S(1)} %get-tuple-element.61), channel_id=1, source_target_pairs={{1,2},{3,4},{5,6},{7,8},{9,10},{11,12},{13,14},{15,16},{17,18},{19... | collective-permute-start | bytes 24584 | tf_op jit(solution)/shard_map/ppermute | solution.py:517
  79.4 6.7 %collective-permute-start.4 = (f32[16,128]{1,0:T(8,128)S(1)}, f32[16,128]{1,0:T(8,128)S(1)}, u32[]{:S(2)}, u32[]{:S(2)}) collective-permute-start(f32[16,128]{1,0:T(8,128)S(1)} %get-tuple-element.66), channel_id=1, source_target_pairs={{0,1},{1,0},{2,3},{3,2},{4,5},{5,4},{6,7},{7,6},{8,9},{9,8},{10,11... | collective-permute-start | bytes 24584 | tf_op jit(solution)/shard_map/ppermute | solution.py:511
  85.3 3.1 %collective-permute-start.5 = (f32[16,128]{1,0:T(8,128)S(1)}, f32[16,128]{1,0:T(8,128)S(1)}, u32[]{:S(2)}, u32[]{:S(2)}) collective-permute-start(f32[16,128]{1,0:T(8,128)S(1)} %get-tuple-element.66), channel_id=1, source_target_pairs={{1,2},{3,4},{5,6},{7,8},{9,10},{11,12},{13,14},{15,16},{17,18},{19... | collective-permute-start | bytes 24584 | tf_op jit(solution)/shard_map/ppermute | solution.py:517
  89.9 6.3 %collective-permute-start.6 = (f32[16,128]{1,0:T(8,128)S(1)}, f32[16,128]{1,0:T(8,128)S(1)}, u32[]{:S(2)}, u32[]{:S(2)}) collective-permute-start(f32[16,128]{1,0:T(8,128)S(1)} %get-tuple-element.71), channel_id=1, source_target_pairs={{0,1},{1,0},{2,3},{3,2},{4,5},{5,4},{6,7},{7,6},{8,9},{9,8},{10,11... | collective-permute-start | bytes 24584 | tf_op jit(solution)/shard_map/ppermute | solution.py:511
  95.5 3.1 %collective-permute-start.7 = (f32[16,128]{1,0:T(8,128)S(1)}, f32[16,128]{1,0:T(8,128)S(1)}, u32[]{:S(2)}, u32[]{:S(2)}) collective-permute-start(f32[16,128]{1,0:T(8,128)S(1)} %get-tuple-element.71), channel_id=1, source_target_pairs={{1,2},{3,4},{5,6},{7,8},{9,10},{11,12},{13,14},{15,16},{17,18},{19... | collective-permute-start | bytes 24584 | tf_op jit(solution)/shard_map/ppermute | solution.py:517

commit v10 on v9

--- a/solution.py
+++ b/solution.py
@@ -14,7 +14,7 @@
 STEPS = 4
 KNOWN = [(i, j) for j in range(STEPS) for i in range(j + 1)]
 HELD = 16
-UNROLL = 24
+UNROLL = 48
 F32 = jnp.float32
 BF16 = jnp.bfloat16
 NN = (((1,), (0,)), ((), ()))
@@ -540,7 +540,7 @@
     load, pre, send = start(mapped, onehot, precond, listed)
     basis, pres = [load], [pre]
     for j in range(STEPS):
-        far = to_far(send, j > 0)
+        far = to_far(send, j < STEPS - 1)
         near = to_near(send)
         earlier = basis[:-1] if j == STEPS - 1 else []
         part, taken, more = inside(blocks, local, outer, basis[-1], pres[-1], near, earlier)

time: 119 us -> 118 us (level)
  blocking collectives: 51.2 us -> 45.8 us
  starting transfers between devices: 26.4 us -> 31.2 us
    all_to_all x3, blocking collectives: 51.2 us -> 45.8 us  [to_all(): return lax.all_to_all(x, DOM, split_axis=0, concat_axis=0, tiled=True)]
    ppermute x4, starting transfers between devices: 12.7 us -> 17.8 us  [to_near(): return lax.ppermute(send, DOM, [(i, i ^ 1) for i in range(devices)])]
where the time goes in v10:
time: 118 us
  blocking collectives  45.8 us (39%)
  starting transfers between devices  31.2 us (26%)
  Pallas kernels  25.1 us (21%)
  waiting for transfers between devices  15 us (13%)
    all_to_all x3, blocking collectives, to_all(): return lax.all_to_all(x, DOM, split_axis=0, concat_axis=0, tiled=True)  45.8 us
    ppermute x4, starting transfers between devices, to_near(): return lax.ppermute(send, DOM, [(i, i ^ 1) for i in range(devices)])  17.8 us
    all_to_all x1, starting transfers between devices, to_all(): return lax.all_to_all(x, DOM, split_axis=0, concat_axis=0, tiled=True)  11.5 us
    pallas_call x1, Pallas kernels, transfer(): pl.pallas_call(transfer_kernel, out_shape=(jax.ShapeDtypeStruct(coords.sh...  8.3 us
    all_to_all x1, waiting for transfers between devices, to_all(): return lax.all_to_all(x, DOM, split_axis=0, concat_axis=0, tiled=True)  6.68 us
    ppermute x4, waiting for transfers between devices, to_far(): return lax.ppermute(send, DOM, pairs + [(j, i) for i, j in pairs])  5.86 us
    pallas_call x3, Pallas kernels, step(): pl.pallas_call(step_kernel, out_shape=(shape, shape, pltpu.VMEM(far.shape...  4.52 us
    pallas_call x4, Pallas kernels, inside(): pl.pallas_call(inside_kernel, out_shape=(pltpu.VMEM(old.shape, F32), pltp...  3.9 us
  transfers between devices with their start and end apart: 9, of which 8 were waited for; matrix products, arithmetic and copies ran while one was open for 0% of the time, Pallas kernels for 6%

profile of v10, /device:TPU:1, one launch (start us, length us, event | category | flops | bytes accessed | tf_op | source)
XLA Modules:
  0.0 117.9 jit_solution(10489777080047874315)
XLA Ops:
  0.6 1.7 %slots.1 = (f32[128,128]{1,0:T(8,128)}, s32[1,512]{1,0:T(1,128)S(1)}) custom-call(s32[1,512]{1,0:T(1,128)} %bitcast.28, s32[1,512]{1,0:T(1,128)} %bitcast.29), custom_call_target="tpu_custom_call" | custom-call | tf_op jit(solution)/shard_map/slots/pallas_call | solution.py:128
  2.4 11.5 %all-to-all-start = ((f32[128,1,128]{2,1,0:T(1,128)}), f32[128,1,128]{2,1,0:T(1,128)S(1)}, u32[]{:S(2)}, u32[]{:S(2)}) async-start(f32[128,1,128]{2,1,0:T(1,128)} %bitcast.3), calls=%async_computation | async-start | bytes 131072 | tf_op jit(solution)/shard_map/all_to_all | solution.py:521
  13.8 2.7 %prepare.1 = (f32[4,7,128,128]{3,2,1,0:T(8,128)S(1)}, f32[128,128]{1,0:T(8,128)S(1)}, bf16[2,128,128]{2,1,0:T(8,128)(2,1)S(1)}, bf16[2,32,128]{2,1,0:T(8,128)(2,1)S(1)}, bf16[16,128]{1,0:T(8,128)(2,1)S(1)}) custom-call(s32[16]{0:T(128)} %halo_ref.1, s32[1]{0:T(128)} %bitcast.5.place_ref, s32[2,128]{1,0:T(2,128)} %columns_ref.1, f32[96,128]{1,0:T(8,128)} %bitcast.27, ...), custom_call_target="tpu_custom_call" | custom-call | bytes 3145728 | tf_op jit(solution)/shard_map/prepare/pallas_call | solution.py:182
  16.5 6.7 %all-to-all-done = f32[128,1,128]{2,1,0:T(1,128)S(1)} async-done(((f32[128,1,128]{2,1,0:T(1,128)}), f32[128,1,128]{2,1,0:T(1,128)S(1)}, u32[]{:S(2)}, u32[]{:S(2)}) %all-to-all-start) | async-done | bytes 65568 | tf_op jit(solution)/shard_map/all_to_all | solution.py:521
  23.2 0.8 answer.1
  24.0 16.7 %all_to_all.32 = f32[128,1,768]{2,1,0:T(1,128)S(1)} all-to-all(f32[128,1,768]{2,1,0:T(1,128)S(1)} %bitcast.21), channel_id=1, replica_groups=mesh['dom'=128] {'dom'}, dimensions={0} | all-to-all | bytes 786432 | tf_op jit(solution)/shard_map/all_to_all | solution.py:521
  40.7 8.3 %transfer.1 = (f32[768,128]{1,0:T(8,128)S(1)}, f32[3,96,96,128]{3,2,1,0:T(8,128)S(1)}, f32[96,96,128]{2,1,0:T(8,128)S(1)}) custom-call(s32[1,512]{1,0:T(1,128)S(1)} %get-tuple-element.41.slot_ref, f32[768,128]{1,0:T(8,128)S(1)} %bitcast.19, f32[4,7,128,128]{3,2,1,0:T(8,128)S(1)} %get-tuple-element.45.turned_ref, f32[3,96,96,128]{3,2,1,0:T(8,128)} %blocks_ref.1, ...), custom_call_target="tpu_custom_call" | custom-call | tf_op jit(solution)/shard_map/transfer/pallas_call | solution.py:278
  49.0 16.7 %all_to_all.33 = f32[128,1,768]{2,1,0:T(1,128)S(1)} all-to-all(f32[128,1,768]{2,1,0:T(1,128)S(1)} %bitcast.20), channel_id=1, replica_groups=mesh['dom'=128] {'dom'}, dimensions={0} | all-to-all | bytes 786432 | tf_op jit(solution)/shard_map/all_to_all | solution.py:521
  65.7 1.1 start.1
  66.9 1.3 %collective-permute-start = (f32[16,128]{1,0:T(8,128)S(1)}, f32[16,128]{1,0:T(8,128)S(1)}, u32[]{:S(2)}, u32[]{:S(2)}) collective-permute-start(f32[16,128]{1,0:T(8,128)S(1)} %get-tuple-element.55), channel_id=1, source_target_pairs={{0,1},{1,0},{2,3},{3,2},{4,5},{5,4},{6,7},{7,6},{8,9},{9,8},{10,11... | collective-permute-start | bytes 24584 | tf_op jit(solution)/shard_map/ppermute | solution.py:511
  68.2 0.0 collective-permute-start.1
  68.2 0.8 collective-permute-done.near_ref
  69.0 1.1 inside.4
  70.1 1.2 collective-permute-done.1.far_ref
  71.3 1.5 %step.3 = (f32[96,128]{1,0:T(8,128)S(1)}, f32[96,128]{1,0:T(8,128)S(1)}, f32[16,128]{1,0:T(8,128)S(1)}) custom-call(f32[3,96,96,128]{3,2,1,0:T(8,128)S(1)} %get-tuple-element.46.blocks_ref, f32[96,96,128]{2,1,0:T(8,128)S(1)} %get-tuple-element.51.precond_ref, bf16[2,32,128]{2,1,0:T(8,128)(2,1)S(1)} %get-tuple-element.48.outer_ref, ...), custom_call_target="tpu_custom_call" | custom-call | tf_op jit(solution)/shard_map/step/pallas_call | solution.py:405
  72.8 5.5 %collective-permute-start.2 = (f32[16,128]{1,0:T(8,128)S(1)}, f32[16,128]{1,0:T(8,128)S(1)}, u32[]{:S(2)}, u32[]{:S(2)}) collective-permute-start(f32[16,128]{1,0:T(8,128)S(1)} %get-tuple-element.61), channel_id=1, source_target_pairs={{0,1},{1,0},{2,3},{3,2},{4,5},{5,4},{6,7},{7,6},{8,9},{9,8},{10,11... | collective-permute-start | bytes 24584 | tf_op jit(solution)/shard_map/ppermute | solution.py:511
  78.3 0.0 collective-permute-start.3
  78.3 0.8 collective-permute-done.2.near_ref
  79.1 1.1 inside.5
  80.2 1.2 collective-permute-done.3.far_ref
  81.3 1.5 %step.4 = (f32[96,128]{1,0:T(8,128)S(1)}, f32[96,128]{1,0:T(8,128)S(1)}, f32[16,128]{1,0:T(8,128)S(1)}) custom-call(f32[3,96,96,128]{3,2,1,0:T(8,128)S(1)} %get-tuple-element.46.blocks_ref, f32[96,96,128]{2,1,0:T(8,128)S(1)} %get-tuple-element.51.precond_ref, bf16[2,32,128]{2,1,0:T(8,128)(2,1)S(1)} %get-tuple-element.48.outer_ref, ...), custom_call_target="tpu_custom_call" | custom-call | tf_op jit(solution)/shard_map/step/pallas_call | solution.py:405
  82.9 5.5 %collective-permute-start.4 = (f32[16,128]{1,0:T(8,128)S(1)}, f32[16,128]{1,0:T(8,128)S(1)}, u32[]{:S(2)}, u32[]{:S(2)}) collective-permute-start(f32[16,128]{1,0:T(8,128)S(1)} %get-tuple-element.66), channel_id=1, source_target_pairs={{0,1},{1,0},{2,3},{3,2},{4,5},{5,4},{6,7},{7,6},{8,9},{9,8},{10,11... | collective-permute-start | bytes 24584 | tf_op jit(solution)/shard_map/ppermute | solution.py:511
  88.4 0.0 collective-permute-start.5
  88.4 0.8 collective-permute-done.4.near_ref
  89.2 1.1 inside.6
  90.3 1.2 collective-permute-done.5.far_ref
  91.4 1.5 %step.5 = (f32[96,128]{1,0:T(8,128)S(1)}, f32[96,128]{1,0:T(8,128)S(1)}, f32[16,128]{1,0:T(8,128)S(1)}) custom-call(f32[3,96,96,128]{3,2,1,0:T(8,128)S(1)} %get-tuple-element.46.blocks_ref, f32[96,96,128]{2,1,0:T(8,128)S(1)} %get-tuple-element.51.precond_ref, bf16[2,32,128]{2,1,0:T(8,128)(2,1)S(1)} %get-tuple-element.48.outer_ref, ...), custom_call_target="tpu_custom_call" | custom-call | tf_op jit(solution)/shard_map/step/pallas_call | solution.py:405
  93.0 5.5 %collective-permute-start.6 = (f32[16,128]{1,0:T(8,128)S(1)}, f32[16,128]{1,0:T(8,128)S(1)}, u32[]{:S(2)}, u32[]{:S(2)}) collective-permute-start(f32[16,128]{1,0:T(8,128)S(1)} %get-tuple-element.71), channel_id=1, source_target_pairs={{0,1},{1,0},{2,3},{3,2},{4,5},{5,4},{6,7},{7,6},{8,9},{9,8},{10,11... | collective-permute-start | bytes 24584 | tf_op jit(solution)/shard_map/ppermute | solution.py:511
  98.5 1.9 %collective-permute-start.7 = (f32[16,128]{1,0:T(8,128)S(1)}, f32[16,128]{1,0:T(8,128)S(1)}, u32[]{:S(2)}, u32[]{:S(2)}) collective-permute-start(f32[16,128]{1,0:T(8,128)S(1)} %get-tuple-element.71), channel_id=1, source_target_pairs={{1,2},{3,4},{5,6},{7,8},{9,10},{11,12},{13,14},{15,16},{17,18},{19... | collective-permute-start | bytes 24584 | tf_op jit(solution)/shard_map/ppermute | solution.py:517
  100.4 0.0 collective-permute-done.6.near_ref
  100.4 0.7 inside.7
  101.1 2.4 %collective-permute-done.7.far_ref = f32[16,128]{1,0:T(8,128)S(1)} collective-permute-done((f32[16,128]{1,0:T(8,128)S(1)}, f32[16,128]{1,0:T(8,128)S(1)}, u32[]{:S(2)}, u32[]{:S(2)}) %collective-permute-start.7) | collective-permute-done | bytes 8224 | tf_op jit(solution)/shard_map/ppermute | solution.py:517
  103.4 1.2 %last.1 = (f32[96,128]{1,0:T(8,128)S(1)}, f32[128,128]{1,0:T(8,128)S(1)}) custom-call(f32[3,96,96,128]{3,2,1,0:T(8,128)S(1)} %get-tuple-element.46.blocks_ref, bf16[2,32,128]{2,1,0:T(8,128)(2,1)S(1)} %get-tuple-element.48.outer_ref, f32[96,128]{1,0:T(8,128)S(1)} %get-tuple-element.72.part_ref, f32[2,96,128]{2,1,0:T(8,128)S(1)} %get-tuple-element.73.taken_ref, ...), custom_call_target="tpu_custom_call" | custom-call | tf_op jit(solution)/shard_map/last/pallas_call | solution.py:428
  104.6 12.4 %all_to_all.34 = f32[128,1,128]{2,1,0:T(1,128)S(1)} all-to-all(f32[128,1,128]{2,1,0:T(1,128)S(1)} %bitcast.24), channel_id=1, replica_groups=mesh['dom'=128] {'dom'}, dimensions={0} | all-to-all | bytes 131072 | tf_op jit(solution)/shard_map/all_to_all | solution.py:521
  117.1 0.9 finish.1
Async XLA Ops:
  2.4 20.9 %all-to-all-start = ((f32[128,1,128]{2,1,0:T(1,128)}), f32[128,1,128]{2,1,0:T(1,128)S(1)}, u32[]{:S(2)}, u32[]{:S(2)}) async-start(f32[128,1,128]{2,1,0:T(1,128)} %bitcast.3), calls=%async_computation | async-start | bytes 131072 | tf_op jit(solution)/shard_map/all_to_all | solution.py:521
  66.9 2.1 %collective-permute-start = (f32[16,128]{1,0:T(8,128)S(1)}, f32[16,128]{1,0:T(8,128)S(1)}, u32[]{:S(2)}, u32[]{:S(2)}) collective-permute-start(f32[16,128]{1,0:T(8,128)S(1)} %get-tuple-element.55), channel_id=1, source_target_pairs={{0,1},{1,0},{2,3},{3,2},{4,5},{5,4},{6,7},{7,6},{8,9},{9,8},{10,11... | collective-permute-start | bytes 24584 | tf_op jit(solution)/shard_map/ppermute | solution.py:511
  68.2 3.1 %collective-permute-start.1 = (f32[16,128]{1,0:T(8,128)S(1)}, f32[16,128]{1,0:T(8,128)S(1)}, u32[]{:S(2)}, u32[]{:S(2)}) collective-permute-start(f32[16,128]{1,0:T(8,128)S(1)} %get-tuple-element.55), channel_id=1, source_target_pairs={{1,2},{3,4},{5,6},{7,8},{9,10},{11,12},{13,14},{15,16},{17,18},{19... | collective-permute-start | bytes 24584 | tf_op jit(solution)/shard_map/ppermute | solution.py:517
  72.8 6.3 %collective-permute-start.2 = (f32[16,128]{1,0:T(8,128)S(1)}, f32[16,128]{1,0:T(8,128)S(1)}, u32[]{:S(2)}, u32[]{:S(2)}) collective-permute-start(f32[16,128]{1,0:T(8,128)S(1)} %get-tuple-element.61), channel_id=1, source_target_pairs={{0,1},{1,0},{2,3},{3,2},{4,5},{5,4},{6,7},{7,6},{8,9},{9,8},{10,11... | collective-permute-start | bytes 24584 | tf_op jit(solution)/shard_map/ppermute | solution.py:511
  78.3 3.1 %collective-permute-start.3 = (f32[16,128]{1,0:T(8,128)S(1)}, f32[16,128]{1,0:T(8,128)S(1)}, u32[]{:S(2)}, u32[]{:S(2)}) collective-permute-start(f32[16,128]{1,0:T(8,128)S(1)} %get-tuple-element.61), channel_id=1, source_target_pairs={{1,2},{3,4},{5,6},{7,8},{9,10},{11,12},{13,14},{15,16},{17,18},{19... | collective-permute-start | bytes 24584 | tf_op jit(solution)/shard_map/ppermute | solution.py:517
  82.9 6.3 %collective-permute-start.4 = (f32[16,128]{1,0:T(8,128)S(1)}, f32[16,128]{1,0:T(8,128)S(1)}, u32[]{:S(2)}, u32[]{:S(2)}) collective-permute-start(f32[16,128]{1,0:T(8,128)S(1)} %get-tuple-element.66), channel_id=1, source_target_pairs={{0,1},{1,0},{2,3},{3,2},{4,5},{5,4},{6,7},{7,6},{8,9},{9,8},{10,11... | collective-permute-start | bytes 24584 | tf_op jit(solution)/shard_map/ppermute | solution.py:511
  88.4 3.1 %collective-permute-start.5 = (f32[16,128]{1,0:T(8,128)S(1)}, f32[16,128]{1,0:T(8,128)S(1)}, u32[]{:S(2)}, u32[]{:S(2)}) collective-permute-start(f32[16,128]{1,0:T(8,128)S(1)} %get-tuple-element.66), channel_id=1, source_target_pairs={{1,2},{3,4},{5,6},{7,8},{9,10},{11,12},{13,14},{15,16},{17,18},{19... | collective-permute-start | bytes 24584 | tf_op jit(solution)/shard_map/ppermute | solution.py:517
  93.0 7.4 %collective-permute-start.6 = (f32[16,128]{1,0:T(8,128)S(1)}, f32[16,128]{1,0:T(8,128)S(1)}, u32[]{:S(2)}, u32[]{:S(2)}) collective-permute-start(f32[16,128]{1,0:T(8,128)S(1)} %get-tuple-element.71), channel_id=1, source_target_pairs={{0,1},{1,0},{2,3},{3,2},{4,5},{5,4},{6,7},{7,6},{8,9},{9,8},{10,11... | collective-permute-start | bytes 24584 | tf_op jit(solution)/shard_map/ppermute | solution.py:511
  98.5 5.0 %collective-permute-start.7 = (f32[16,128]{1,0:T(8,128)S(1)}, f32[16,128]{1,0:T(8,128)S(1)}, u32[]{:S(2)}, u32[]{:S(2)}) collective-permute-start(f32[16,128]{1,0:T(8,128)S(1)} %get-tuple-element.71), channel_id=1, source_target_pairs={{1,2},{3,4},{5,6},{7,8},{9,10},{11,12},{13,14},{15,16},{17,18},{19... | collective-permute-start | bytes 24584 | tf_op jit(solution)/shard_map/ppermute | solution.py:517
